TPU v7x, 32 devices: a whole 2x2x4 slice. The times are simulated.
32 devices in a mesh: ctx: 8 (over y, x, core), exp: 4 (over z).
Axes of the slice: x: 2, y: 2, z: 4, core: 2. Of those that a mesh axis runs over, the one named last changes fastest.
Arguments:
- query: bfloat16 [1024, 4096], P('ctx', 'exp'), may hold values from -8 to 8
- keys_values: bfloat16 [2, 1024, 1024], P(None, 'ctx', 'exp'), may hold values from -8 to 8
- cache: bfloat16 [2, 2048, 1024], P(None, 'ctx', 'exp'), may hold values from -8 to 8
- residual: bfloat16 [1024, 4096], P(('ctx', 'exp')), may hold values from -6 to 6
- out_proj: bfloat16 [4096, 4096], P('exp'), may hold values from -0.09375 to 0.09375
- norm_gain: float32 [4096], replicated, may hold values from 0.1 to 1.9
- router: bfloat16 [4096, 4], replicated, may hold values from -0.09375 to 0.09375
- expert_ids: int32 [1024, 2], P(('ctx', 'exp')), may hold values from 0 to 3, all different within a row; in each aligned block of 32 rows (0 to 31, 32 to 63, ...) at most 32 rows name the same one
- w_gate: bfloat16 [4, 4096, 8192], P('exp', None, 'ctx'), may hold values from -0.09375 to 0.09375
- w_up: bfloat16 [4, 4096, 8192], P('exp', None, 'ctx'), may hold values from -0.09375 to 0.09375
- w_down: bfloat16 [4, 8192, 4096], P('exp', 'ctx'), may hold values from -0.0625 to 0.0625
- cotangent: bfloat16 [1024, 4096], P(('ctx', 'exp')), may hold values from -6 to 6
Outputs:
- layer_out: bfloat16 [1024, 4096], P(('ctx', 'exp'))
- grad_down: float32 [4, 8192, 4096], P('exp', 'ctx')
Inputs may be any that keep to these rules, and one draw needn't show every extreme that they name: `expert_ids`: each row names two different experts. Within each aligned block of 32 rows no expert is named by more than 32 rows.
All inputs are finite; a program needn't handle non-finite values.
Results may differ from a plain program's by a relative error of at most 0.012.
Values may be sent and summed in bfloat16 or wider, within the bound.
No kernel may reach another device: no remote copies, remote signals or barrier semaphores. Data moves between devices by JAX's collectives and lax.ppermute only.
A program may use at most 128 MiB of HBM per device.

v0:
```python
import functools
import math

import jax
import jax.numpy as jnp
from jax import lax
from jax.experimental import pallas as pl
from jax.experimental.pallas import tpu as pltpu
from jax.sharding import PartitionSpec as P


HEAD_SIZE = 128
WINDOW = 4096
HIDDEN = -1e30
EPSILON = 1e-05


def swap(value, bit):
    return lax.ppermute(value, "ctx", [(i, i ^ bit) for i in range(lax.axis_size("ctx"))])


def swap_plane(value, bits):
    return lax.ppermute(value, "exp", [(i, i ^ bits) for i in range(lax.axis_size("exp"))])


def link_bits():
    devices = lax.axis_size("ctx")
    return [1 << b for b in range(1, devices.bit_length() - 1)]


def cross(value, turn):
    near, far = link_bits()
    even, odd = (near, far) if turn == 0 else (far, near)
    pairs = [(i, i ^ (odd if i % 2 else even)) for i in range(lax.axis_size("ctx"))]
    return lax.ppermute(value, "ctx", pairs)


def gather(block):
    bits = link_bits()
    if len(bits) != 2:
        held = block
        for bit in bits + [1]:
            held = jnp.concatenate([held, swap(held, bit)], axis=0)
        return [held]
    rows = block.shape[0]
    pair = jnp.concatenate([block, swap(block, 1)], axis=0)
    beside = cross(pair, 0)
    opposite = cross(beside[:rows], 1)
    sent = jnp.concatenate([beside, opposite], axis=0)
    return [pair, sent, swap(sent, 1)]


def plus(a, b):
    return (a.astype(jnp.float32) + b.astype(jnp.float32)).astype(jnp.bfloat16)


def scatter(parts):
    bits = link_bits()
    if len(bits) != 2:
        held = parts[0]
        for bit in [1] + bits[::-1]:
            middle = held.shape[0] // 2
            held = plus(held[:middle], swap(held[middle:], bit))
        return held
    pair, sent, theirs = parts
    rows = pair.shape[0] // 2
    got = swap(theirs, 1)
    returned = cross(plus(sent[2 * rows :], got[2 * rows :]), 1)
    beside = plus(sent[: 2 * rows], got[: 2 * rows])
    beside = jnp.concatenate([plus(beside[:rows], returned), beside[rows:]], axis=0)
    pair = plus(pair, cross(beside, 0))
    return plus(pair[:rows], swap(pair[rows:], 1))


def expert_kernel(parts, steps, place, tags_ref, router_ref, *refs):
    rows_refs = refs[:parts]
    gate_ref, up_ref, down_ref = refs[parts : parts + 3]
    part_refs = refs[parts + 3 : 2 * parts + 3]
    turned_ref, rows_all, weight_ref, hidden_ref = refs[2 * parts + 3 :]
    step = pl.program_id(0)
    wide = gate_ref.shape[1]

    @pl.when(step == 0)
    def _():
        at = 0
        for ref in rows_refs:
            rows_all[at : at + ref.shape[0]] = ref[...]
            at += ref.shape[0]
        logits = jnp.dot(rows_all[...], router_ref[...], preferred_element_type=jnp.float32)
        lane = lax.broadcasted_iota(jnp.int32, logits.shape, 1).astype(jnp.float32)
        tags = tags_ref[...].astype(jnp.float32)
        one, two = tags[:, :1], tags[:, 1:2]
        first = jnp.sum(jnp.where(lane == one, logits, 0.0), axis=1, keepdims=True)
        second = jnp.sum(jnp.where(lane == two, logits, 0.0), axis=1, keepdims=True)
        gate = 1.0 / (1.0 + jnp.exp(second - first))
        mine = place[0].astype(jnp.float32)
        weight = jnp.where(one == mine, gate, 0.0) + jnp.where(two == mine, 1.0 - gate, 0.0)
        weight_ref[...] = jnp.broadcast_to(weight, weight_ref.shape)

    @pl.when(step < steps)
    def _():
        rows = rows_all[...]
        gate = jnp.dot(rows, gate_ref[...], preferred_element_type=jnp.float32)
        up = jnp.dot(rows, up_ref[...], preferred_element_type=jnp.float32)
        hidden = gate / (1.0 + jnp.exp(-gate)) * up * weight_ref[:, :1]
        hidden = hidden.astype(jnp.bfloat16)
        hidden_ref[:, pl.ds(pl.multiple_of(step * wide, wide), wide)] = hidden
        turned_ref[...] = hidden.T

    @pl.when(step >= steps)
    def _():
        part = jnp.dot(hidden_ref[...], down_ref[...], preferred_element_type=jnp.float32)
        part = part.astype(jnp.bfloat16)
        at = 0
        for ref in part_refs:
            ref[...] = part[at : at + ref.shape[0]]
            at += ref.shape[0]


def expert(place, tags, router, rows, gate_mat, up_mat, down_mat):
    width, units = gate_mat.shape
    experts = router.shape[1]
    router = jnp.pad(router, ((0, 0), (0, HEAD_SIZE - experts)))
    count = sum(r.shape[0] for r in rows)
    wide, broad = min(256, units), min(1024, width)
    steps, turns = units // wide, width // broad
    whole = lambda shape: pl.BlockSpec(
        shape, lambda i, place: (0, 0), pipeline_mode=pl.Buffered(1)
    )
    late = lambda i, place: (0, jnp.maximum(i - steps, 0))
    early = lambda i, place: (0, jnp.minimum(i, steps - 1))
    return pl.pallas_call(
        functools.partial(expert_kernel, len(rows), steps),
        out_shape=[jax.ShapeDtypeStruct(r.shape, jnp.bfloat16) for r in rows]
        + [jax.ShapeDtypeStruct((units, count), jnp.bfloat16)],
        grid_spec=pltpu.PrefetchScalarGridSpec(
            num_scalar_prefetch=1,
            grid=(steps + turns,),
            in_specs=[whole(tags.shape), whole(router.shape)]
            + [whole(r.shape) for r in rows]
            + [pl.BlockSpec((width, wide), early)] * 2
            + [pl.BlockSpec((units, broad), late)],
            out_specs=[pl.BlockSpec((r.shape[0], broad), late) for r in rows]
            + [pl.BlockSpec((wide, count), lambda i, place: (jnp.minimum(i, steps - 1), 0))],
            scratch_shapes=[
                pltpu.VMEM((count, width), jnp.bfloat16),
                pltpu.VMEM((count, HEAD_SIZE), jnp.float32),
                pltpu.VMEM((count, units), jnp.bfloat16),
            ],
        ),
        compiler_params=pltpu.CompilerParams(vmem_limit_bytes=36 << 20),
        cost_estimate=pl.CostEstimate(
            flops=6 * count * width * units,
            transcendentals=count * units,
            bytes_accessed=2 * (3 * width * units + 2 * count * width),
        ),
        name="expert",
    )(place, tags, router, *rows, gate_mat, up_mat, down_mat)


def outer_kernel(parts, pieces, blocks, *refs):
    grad_refs = refs[:parts]
    turned_refs = refs[parts : parts + pieces]
    out_ref, grads_ref = refs[parts + pieces :]
    length = grads_ref.shape[1] // blocks
    block = 0
    for ref in grad_refs:
        for at in range(0, ref.shape[0], pieces * length):
            for piece in range(pieces):
                start = at + piece * length
                grads_ref[piece, block * length : (block + 1) * length] = ref[
                    start : start + length
                ]
            block += 1
    total = jnp.dot(turned_refs[0][...], grads_ref[0], preferred_element_type=jnp.float32)
    for piece in range(1, pieces):
        total += jnp.dot(
            turned_refs[piece][...], grads_ref[piece], preferred_element_type=jnp.float32
        )
    out_ref[...] = total


def outer(grads, turned, blocks, width):
    units, count = turned[0].shape
    broad = min(512, width)
    pieces = len(turned)
    return pl.pallas_call(
        functools.partial(outer_kernel, len(grads), pieces, blocks),
        out_shape=jax.ShapeDtypeStruct((units, width), jnp.float32),
        grid=(width // broad,),
        in_specs=[pl.BlockSpec((g.shape[0], broad), lambda i: (0, i)) for g in grads]
        + [
            pl.BlockSpec((units, count), lambda i: (0, 0), pipeline_mode=pl.Buffered(1))
            for _ in turned
        ],
        out_specs=pl.BlockSpec((units, broad), lambda i: (0, i)),
        scratch_shapes=[pltpu.VMEM((pieces, count, broad), jnp.bfloat16)],
        compiler_params=pltpu.CompilerParams(vmem_limit_bytes=24 << 20),
        cost_estimate=pl.CostEstimate(
            flops=2 * units * count * pieces * width,
            transcendentals=0,
            bytes_accessed=4 * units * width + 4 * count * pieces * width,
        ),
        name="outer",
    )(*grads, *turned)


def attend_kernel(slots, cached, window_free, start, final, *refs):
    place = refs[0]
    q_ref = refs[1]
    keys = refs[2 : 2 + slots]
    values = refs[2 + slots : 2 + 2 * slots]
    at = 2 + 2 * slots
    if not start:
        max_in, sum_in, acc_in = refs[at : at + 3]
        at += 3
    if final:
        out_ref = refs[at]
        at += 1
    else:
        max_out, sum_out, acc_out = refs[at : at + 3]
        at += 3
    scores_ref = refs[at]
    tokens = q_ref.shape[0]
    heads = q_ref.shape[1] // HEAD_SIZE
    count = keys[0].shape[1]
    lanes = 128
    power = math.log2(math.e) / math.sqrt(HEAD_SIZE)
    queries = jnp.concatenate(
        [q_ref[:, j * HEAD_SIZE : (j + 1) * HEAD_SIZE] for j in range(heads)], axis=0
    )
    rows = heads * tokens
    new = count - cached
    gap = lax.broadcasted_iota(jnp.int32, (tokens, new), 1) - lax.broadcasted_iota(
        jnp.int32, (tokens, new), 0
    )
    gap = jnp.concatenate([gap] * heads, axis=0)
    if not window_free:
        gap_cached = lax.broadcasted_iota(jnp.int32, (tokens, cached), 1) - (
            lax.broadcasted_iota(jnp.int32, (tokens, cached), 0)
        )
        gap_cached = jnp.concatenate([gap_cached] * heads, axis=0)
    largest = jnp.full((rows, lanes), HIDDEN, jnp.float32)
    for s in range(slots):
        old = lax.dot_general(
            queries,
            keys[s][0, :cached, :],
            (((1,), (1,)), ((), ())),
            preferred_element_type=jnp.float32,
        )
        if not window_free:
            old = jnp.where(gap_cached > place[slots + s], old, HIDDEN)
        fresh = lax.dot_general(
            queries,
            keys[s][0, cached:, :],
            (((1,), (1,)), ((), ())),
            preferred_element_type=jnp.float32,
        )
        seen = gap <= place[s]
        if not window_free:
            seen = seen & (gap > place[s] - WINDOW)
        fresh = jnp.where(seen, fresh, HIDDEN)
        base = s * count
        scores_ref[:, base : base + cached] = old
        scores_ref[:, base + cached : base + count] = fresh
        for j in range(cached // lanes):
            largest = jnp.maximum(largest, old[:, j * lanes : (j + 1) * lanes])
        for j in range(new // lanes):
            largest = jnp.maximum(largest, fresh[:, j * lanes : (j + 1) * lanes])
    top = jnp.max(largest, axis=1, keepdims=True)
    if not start:
        before = max_in[0][:, :1]
        top = jnp.maximum(top, before)
        rescale = jnp.exp2((before - top) * power)
        total = sum_in[0] * rescale
        acc = acc_in[0] * rescale
    else:
        total = jnp.zeros((rows, lanes), jnp.float32)
        acc = jnp.zeros((rows, HEAD_SIZE), jnp.float32)
    for s in range(slots):
        weights = jnp.exp2((scores_ref[:, s * count : (s + 1) * count] - top) * power)
        for j in range(count // lanes):
            total = total + weights[:, j * lanes : (j + 1) * lanes]
        acc = acc + jnp.dot(
            weights.astype(jnp.bfloat16), values[s][0], preferred_element_type=jnp.float32
        )
    if final:
        result = acc / jnp.sum(total, axis=1, keepdims=True)
        for j in range(heads):
            out_ref[:, j * HEAD_SIZE : (j + 1) * HEAD_SIZE] = result[
                j * tokens : (j + 1) * tokens
            ].astype(jnp.bfloat16)
    else:
        max_out[0] = jnp.broadcast_to(top, (rows, lanes))
        sum_out[0] = total
        acc_out[0] = acc


def attend(queries, blocks, places, cached, window_free, state, final):
    slots = len(blocks)
    tokens = queries.shape[0]
    key_arrays = [b[0] for b in blocks]
    value_arrays = [b[1] for b in blocks]
    heads_kv = key_arrays[0][0].shape[2] // HEAD_SIZE
    group = queries.shape[1] // heads_kv
    count = key_arrays[0][0].shape[1]
    rows = tokens * group // HEAD_SIZE

    def plane_spec(plane):
        return pl.BlockSpec((1, count, HEAD_SIZE), lambda h, place, plane=plane: (plane, 0, h))

    carried = pl.BlockSpec((1, rows, HEAD_SIZE), lambda h, place: (h, 0, 0))
    wide = pl.BlockSpec((tokens, group), lambda h, place: (0, h))
    in_specs = [wide]
    in_specs += [plane_spec(p) for _, p in key_arrays]
    in_specs += [plane_spec(p) for _, p in value_arrays]
    operands = [queries] + [a for a, _ in key_arrays] + [a for a, _ in value_arrays]
    if state is not None:
        in_specs += [carried] * 3
        operands += list(state)
    shape = jax.ShapeDtypeStruct((heads_kv, rows, HEAD_SIZE), jnp.float32)
    if final:
        out_specs, out_shape = wide, jax.ShapeDtypeStruct(queries.shape, jnp.bfloat16)
    else:
        out_specs, out_shape = (carried,) * 3, (shape,) * 3
    work = queries.shape[0] * queries.shape[1] * slots * count
    return pl.pallas_call(
        functools.partial(attend_kernel, slots, cached, window_free, state is None, final),
        out_shape=out_shape,
        grid_spec=pltpu.PrefetchScalarGridSpec(
            num_scalar_prefetch=1,
            grid=(heads_kv,),
            in_specs=in_specs,
            out_specs=out_specs,
            scratch_shapes=[pltpu.VMEM((rows, slots * count), jnp.float32)],
        ),
        cost_estimate=pl.CostEstimate(
            flops=4 * work, transcendentals=work // HEAD_SIZE, bytes_accessed=work // 64
        ),
        name="attend",
    )(places, *operands)


def attention(query, keys_values, cache):
    ctx_size = lax.axis_size("ctx")
    here = lax.axis_index("ctx")
    tokens = query.shape[0]
    cached = cache.shape[1]
    window_free = (cached + tokens) * ctx_size <= WINDOW

    def places(offsets):
        new, old = [], []
        for s in offsets:
            owner = here ^ s
            new.append((here - owner) * tokens)
            old.append(cached * ctx_size + here * tokens - owner * cached - WINDOW)
        return jnp.stack(new + old).astype(jnp.int32)

    stage = functools.partial(attend, query, cached=cached, window_free=window_free)
    own = jnp.concatenate([cache, keys_values], axis=1)
    bits = link_bits()
    if len(bits) != 2:
        held = [(own, 0)]
        for bit in [1] + bits:
            held = held + [(swap(a, bit), s ^ bit) for a, s in held]
        state = None
        for index, (a, s) in enumerate(held):
            last = index == len(held) - 1
            state = stage([((a, 0), (a, 1))], places([s]), state=state, final=last)
        return state
    parity = here % 2
    near = jnp.where(parity == 0, bits[0], bits[1])
    far = jnp.where(parity == 0, bits[1], bits[0])
    mate = swap(own, 1)
    pair = jnp.concatenate([own, mate], axis=0)
    beside = cross(pair, 0)
    opposite = cross(beside[:2], 1)
    mate_beside = swap(beside, 1)
    mate_opposite = swap(opposite, 1)
    slot = lambda a, i: ((a, 2 * i), (a, 2 * i + 1))
    state = stage([slot(pair, 0), slot(pair, 1)], places([0, 1]), state=None, final=False)
    state = stage(
        [slot(beside, 0), slot(beside, 1), slot(mate_beside, 0), slot(mate_beside, 1)],
        places([near, near ^ 1, far ^ 1, far]),
        state=state,
        final=False,
    )
    return stage(
        [slot(opposite, 0), slot(mate_opposite, 0)],
        places([near ^ far, near ^ far ^ 1]),
        state=state,
        final=True,
    )


def planes_of(value):
    blocks = [value]
    for k in range(1, lax.axis_size("exp")):
        source, bits = (value, k) if k == 1 or k % 2 == 0 else (blocks[k - 1], 1)
        blocks.append(swap_plane(source, bits))
    return blocks


def on_device(
    query,
    keys_values,
    cache,
    residual,
    out_proj,
    norm_gain,
    router,
    expert_ids,
    w_gate,
    w_up,
    w_down,
    cotangent,
):
    ctx_size = lax.axis_size("ctx")
    planes = lax.axis_size("exp")
    plane = lax.axis_index("exp")
    row_count, width = residual.shape

    tags = jnp.pad(expert_ids.astype(jnp.bfloat16), ((0, 0), (0, HEAD_SIZE - 2)))
    tagged = planes_of(jnp.concatenate([cotangent, tags], axis=1))
    grads = gather(jnp.concatenate(tagged, axis=0))
    ids = jnp.concatenate([g[:, width:] for g in grads], axis=0)
    ids = ids.reshape(ctx_size, planes, row_count, HEAD_SIZE)

    attn = attention(query, keys_values, cache)

    partial = jnp.dot(attn, out_proj, preferred_element_type=jnp.float32)
    partial = partial.reshape(planes, row_count, width)

    def share(k):
        return lax.dynamic_index_in_dim(partial, plane ^ k, 0, keepdims=False)

    hidden_one = residual.astype(jnp.float32) + share(0)
    for k in range(0, planes, 2):
        both = swap_plane(share(k + 1).astype(jnp.bfloat16), 1)
        if k:
            both = swap_plane((share(k) + both.astype(jnp.float32)).astype(jnp.bfloat16), k)
        hidden_one = hidden_one + both.astype(jnp.float32)
    mean_square = jnp.mean(hidden_one * hidden_one, axis=-1, keepdims=True)
    normed = (hidden_one * lax.rsqrt(mean_square + EPSILON) * norm_gain).astype(jnp.bfloat16)

    gate_mat = w_gate[0]
    up_mat = w_up[0]
    down_mat = w_down[0]
    place = jnp.full((1,), plane, jnp.int32)
    blocks = planes_of(normed)
    turned = []
    layer = hidden_one
    for k in range(0, planes, 2):
        rows = gather(jnp.concatenate(blocks[k : k + 2], axis=0))
        tags = ids[:, k : k + 2].reshape(-1, HEAD_SIZE)
        *parts, turned_piece = expert(
            place, tags, router, rows, gate_mat, up_mat, down_mat
        )
        turned.append(turned_piece)
        summed = scatter(parts)
        both = plus(summed[:row_count], swap_plane(summed[row_count:], 1))
        if k:
            both = swap_plane(both, k)
        layer = layer + both.astype(jnp.float32)
    layer_out = layer.astype(jnp.bfloat16)

    gradient = outer(grads, turned, ctx_size, width)
    return (layer_out, gradient[None])


def solution(mesh):
    placed = (
        P("ctx", "exp"),
        P(None, "ctx", "exp"),
        P(None, "ctx", "exp"),
        P(("ctx", "exp"), None),
        P("exp", None),
        P(),
        P(),
        P(("ctx", "exp"), None),
        P("exp", None, "ctx"),
        P("exp", None, "ctx"),
        P("exp", "ctx", None),
        P(("ctx", "exp"), None),
    )

    return jax.shard_map(
        on_device,
        mesh=mesh,
        in_specs=placed,
        out_specs=(P(("ctx", "exp"), None), P("exp", "ctx", None)),
        check_vma=False,
    )
```

profile of v0, /device:TPU:0, one launch (start us, length us, event | category | flops | bytes accessed | tf_op | source)
XLA Modules:
  0.0 265.6 jit_solution(11590361667938592594)
XLA Ops:
  0.6 1.0 constant_dynamic-update-slice_fusion.1
  1.6 0.9 constant_dynamic-update-slice_fusion
  3.9 1.7 pad_maximum_fusion.7
  5.6 2.6 collective-permute-start.8
  8.2 2.6 collective-permute-start.9
  11.4 1.1 pad_maximum_fusion.4.refs_2_.refs_3_.refs_4_.refs_5_
  12.4 1.6 collective-permute-start.1
  15.2 8.6 %collective-permute-done.9 = bf16[32,4224]{1,0:T(8,128)(2,1)} collective-permute-done((bf16[32,4224]{1,0:T(8,128)(2,1)}, bf16[32,4224]{1,0:T(8,128)(2,1)}, u32[]{:S(2)}, u32[]{:S(2)}) %collective-permute-start.9) | collective-permute-done | bytes 270368 | tf_op jit(solution)/shard_map/ppermute | solution.py:23
  24.3 1.0 constant_dynamic-update-slice_fusion.5
  25.3 1.8 slice.116
  27.0 1.5 collective-permute-start.2
  28.6 1.0 constant_dynamic-update-slice_fusion.4
  29.5 4.2 %attend.3 = (f32[2,512,128]{2,1,0:T(8,128)}, f32[2,512,128]{2,1,0:T(8,128)}, f32[2,512,128]{2,1,0:T(8,128)}) custom-call(s32[4]{0:T(128)} %pad_add_fusion.1.refs_0_, bf16[128,1024]{1,0:T(8,128)(2,1)} %refs_1_.5, bf16[4,384,256]{2,1,0:T(8,128)(2,1)} %copy-done.6, bf16[4,384,256]{2,1,0:T(8,128)(2,1)} %copy-done.6, bf16[4,384,256]{2,1,0:T(8,128)(2,1)} %copy-done.6, ...), custom_call_target="tpu_custom_call" | custom-call | flops 402653184 | bytes 1572864 | tf_op jit(solution)/shard_map/attend/pallas_call | solution.py:327
  33.8 1.3 collective-permute-done.2.refs_2_.refs_4_
  35.0 2.4 pad_maximum_fusion
  37.8 5.9 %attend.4 = (f32[2,512,128]{2,1,0:T(8,128)}, f32[2,512,128]{2,1,0:T(8,128)}, f32[2,512,128]{2,1,0:T(8,128)}) custom-call(s32[8]{0:T(128)} %stack.67.refs_0_, bf16[128,1024]{1,0:T(8,128)(2,1)} %refs_1_.5, bf16[4,384,256]{2,1,0:T(8,128)(2,1)} %collective-permute-done.1.refs_2_.refs_3_.refs_6_.refs_7_, ...), custom_call_target="tpu_custom_call" | custom-call | flops 805306368 | bytes 3145728 | tf_op jit(solution)/shard_map/attend/pallas_call | solution.py:327
  44.5 4.6 %attend.5 = bf16[128,1024]{1,0:T(8,128)(2,1)} custom-call(s32[4]{0:T(128)} %pad_add_fusion.refs_0_, bf16[128,1024]{1,0:T(8,128)(2,1)} %refs_1_.5, bf16[2,384,256]{2,1,0:T(8,128)(2,1)} %copy-done.11, bf16[2,384,256]{2,1,0:T(8,128)(2,1)} %copy-done.12, bf16[2,384,256]{2,1,0:T(8,128)(2,1)} %copy-done.11, bf16[2,384,256]{2,1,0:T(8,128)(2,1)} %copy-done.12, ...), custom_call_target="tpu_custom_call" | custom-call | flops 402653184 | bytes 1572864 | tf_op jit(solution)/shard_map/attend/pallas_call | solution.py:327
  49.1 4.7 %fusion.7 = f32[128,4096]{1,0:T(8,128)S(1)} fusion(bf16[128,1024]{1,0:T(8,128)(2,1)} %attend.5, bf16[1024,4096]{1,0:T(8,128)(2,1)} %param.16), kind=kOutput, calls=%fused_computation.53 | convolution fusion | flops 1073741824 | bytes 10747904 | tf_op jit(solution)/shard_map/dot_general | solution.py:431
  53.9 1.7 collective-permute-start.6
  55.6 1.0 constant_dynamic-update-slice_fusion.3
  57.1 6.1 %collective-permute-done.6 = bf16[32,4096]{1,0:T(8,128)(2,1)S(1)} collective-permute-done((bf16[32,4096]{1,0:T(8,128)(2,1)S(1)}, bf16[32,4096]{1,0:T(8,128)(2,1)S(1)}, u32[]{:S(2)}, u32[]{:S(2)}) %collective-permute-start.6) | collective-permute-done | bytes 262176 | tf_op jit(solution)/shard_map/ppermute | solution.py:23
  63.2 2.6 collective-permute-start.7
  65.9 1.4 constant_dynamic-update-slice_fusion.2.refs_0_
  67.3 1.6 collective-permute-start.12
  68.8 3.9 %collective-permute-done.5 = bf16[32,4096]{1,0:T(8,128)(2,1)S(1)} collective-permute-done((bf16[32,4096]{1,0:T(8,128)(2,1)S(1)}, bf16[32,4096]{1,0:T(8,128)(2,1)S(1)}, u32[]{:S(2)}, u32[]{:S(2)}) %collective-permute-start.5) | collective-permute-done | bytes 262176 | tf_op jit(solution)/shard_map/ppermute | solution.py:23
  72.8 3.8 %collective-permute-done.7 = bf16[32,4096]{1,0:T(8,128)(2,1)S(1)} collective-permute-done((bf16[32,4096]{1,0:T(8,128)(2,1)S(1)}, bf16[32,4096]{1,0:T(8,128)(2,1)S(1)}, u32[]{:S(2)}, u32[]{:S(2)}) %collective-permute-start.7) | collective-permute-done | bytes 262176 | tf_op jit(solution)/shard_map/ppermute | solution.py:23
  77.0 10.9 %collective-permute-done.25 = bf16[32,4096]{1,0:T(8,128)(2,1)S(1)} collective-permute-done((bf16[32,4096]{1,0:T(8,128)(2,1)S(1)}, bf16[32,4096]{1,0:T(8,128)(2,1)S(1)}, u32[]{:S(2)}, u32[]{:S(2)}) %collective-permute-start.25) | collective-permute-done | bytes 262176 | tf_op jit(solution)/shard_map/ppermute | solution.py:23
  88.7 1.3 collective-permute-start.15
  90.0 7.1 %collective-permute-done.26 = bf16[32,4096]{1,0:T(8,128)(2,1)S(1)} collective-permute-done((bf16[32,4096]{1,0:T(8,128)(2,1)S(1)}, bf16[32,4096]{1,0:T(8,128)(2,1)S(1)}, u32[]{:S(2)}, u32[]{:S(2)}) %collective-permute-start.26) | collective-permute-done | bytes 262176 | tf_op jit(solution)/shard_map/ppermute | solution.py:23
  97.4 1.6 collective-permute-start.13
  99.2 1.5 collective-permute-start.28
  100.9 22.4 %collective-permute-done.13 = bf16[128,4224]{1,0:T(8,128)(2,1)S(1)} collective-permute-done((bf16[128,4224]{1,0:T(8,128)(2,1)S(1)}, bf16[128,4224]{1,0:T(8,128)(2,1)S(1)}, u32[]{:S(2)}, u32[]{:S(2)}) %collective-permute-start.13) | collective-permute-done | bytes 1081376 | tf_op jit(solution)/shard_map/ppermute | solution.py:35
  124.2 1.6 collective-permute-start.29
  125.8 4.3 %collective-permute-done.16 = bf16[64,4096]{1,0:T(8,128)(2,1)S(1)} collective-permute-done((bf16[64,4096]{1,0:T(8,128)(2,1)S(1)}, bf16[64,4096]{1,0:T(8,128)(2,1)S(1)}, u32[]{:S(2)}, u32[]{:S(2)}) %collective-permute-start.16) | collective-permute-done | bytes 524320 | tf_op jit(solution)/shard_map/ppermute | solution.py:19
  130.2 1.5 collective-permute-start.17
  131.7 1.1 constant_dynamic-update-slice_fusion.15
  132.8 1.1 collective-permute-done.29
  133.9 0.9 constant_dynamic-update-slice_fusion.14.refs_1_
  134.7 10.3 %collective-permute-done.17 = bf16[128,4096]{1,0:T(8,128)(2,1)S(1)} collective-permute-done((bf16[128,4096]{1,0:T(8,128)(2,1)S(1)}, bf16[128,4096]{1,0:T(8,128)(2,1)S(1)}, u32[]{:S(2)}, u32[]{:S(2)}) %collective-permute-start.17) | collective-permute-done | bytes 1048608 | tf_op jit(solution)/shard_map/ppermute | solution.py:35
  145.0 1.0 copy-done.9
  146.0 0.8 slice.122
  146.8 1.5 collective-permute-start.18
  148.4 1.4 copy.17
  149.8 1.5 pad.10.router_ref
  151.3 0.8 slice.117
  152.3 4.1 %collective-permute-done.18 = bf16[64,4096]{1,0:T(8,128)(2,1)} collective-permute-done((bf16[64,4096]{1,0:T(8,128)(2,1)}, bf16[64,4096]{1,0:T(8,128)(2,1)}, u32[]{:S(2)}, u32[]{:S(2)}) %collective-permute-start.18) | collective-permute-done | bytes 524320 | tf_op jit(solution)/shard_map/ppermute | solution.py:35
  156.3 1.1 constant_dynamic-update-slice_fusion.9.refs_1_
  157.5 0.9 slice.120
  158.5 22.3 %expert.3 = (bf16[128,4096]{1,0:T(8,128)(2,1)S(1)}, bf16[192,4096]{1,0:T(8,128)(2,1)S(1)}, bf16[192,4096]{1,0:T(8,128)(2,1)S(1)}, bf16[1024,512]{1,0:T(8,128)(2,1)S(1)}) custom-call(s32[1]{0:T(128)} %bitcast.20.place, bf16[512,128]{1,0:T(8,128)(2,1)S(1)} %bitcast.42, bf16[4096,128]{1,0:T(8,128)(2,1)S(1)} %pad.10.router_ref, bf16[128,4096]{1,0:T(8,128)(2,1)S(1)} %copy-done.3, ...), custom_call_target="tpu_custom_call" | custom-call | flops 12884901888 | bytes 33554432 | tf_op jit(solution)/shard_map/expert/pallas_call | solution.py:132
  181.4 20.5 %expert.2 = (bf16[128,4096]{1,0:T(8,128)(2,1)S(1)}, bf16[192,4096]{1,0:T(8,128)(2,1)S(1)}, bf16[192,4096]{1,0:T(8,128)(2,1)S(1)}, bf16[1024,512]{1,0:T(8,128)(2,1)S(1)}) custom-call(s32[1]{0:T(128)} %bitcast.20.place, bf16[512,128]{1,0:T(8,128)(2,1)S(1)} %bitcast.41, bf16[4096,128]{1,0:T(8,128)(2,1)S(1)} %pad.10.router_ref, bf16[128,4096]{1,0:T(8,128)(2,1)S(1)} %copy-done.1, ...), custom_call_target="tpu_custom_call" | custom-call | flops 12884901888 | bytes 33554432 | tf_op jit(solution)/shard_map/expert/pallas_call | solution.py:132
  202.5 1.6 collective-permute-start.32
  204.1 1.3 collective-permute-done.20
  205.8 1.6 collective-permute-start.21
  207.4 4.3 %collective-permute-done.32 = bf16[64,4096]{1,0:T(8,128)(2,1)S(1)} collective-permute-done((bf16[64,4096]{1,0:T(8,128)(2,1)S(1)}, bf16[64,4096]{1,0:T(8,128)(2,1)S(1)}, u32[]{:S(2)}, u32[]{:S(2)}) %collective-permute-start.32) | collective-permute-done | bytes 524320 | tf_op jit(solution)/shard_map/ppermute | solution.py:35
  211.9 1.5 collective-permute-start.33
  213.5 7.0 %collective-permute-done.21 = bf16[64,4096]{1,0:T(8,128)(2,1)S(1)} collective-permute-done((bf16[64,4096]{1,0:T(8,128)(2,1)S(1)}, bf16[64,4096]{1,0:T(8,128)(2,1)S(1)}, u32[]{:S(2)}, u32[]{:S(2)}) %collective-permute-start.21) | collective-permute-done | bytes 524320 | tf_op jit(solution)/shard_map/ppermute | solution.py:35
  220.7 1.5 collective-permute-start.22
  222.2 5.9 %collective-permute-done.33 = bf16[128,4096]{1,0:T(8,128)(2,1)S(1)} collective-permute-done((bf16[128,4096]{1,0:T(8,128)(2,1)S(1)}, bf16[128,4096]{1,0:T(8,128)(2,1)S(1)}, u32[]{:S(2)}, u32[]{:S(2)}) %collective-permute-start.33) | collective-permute-done | bytes 1048608 | tf_op jit(solution)/shard_map/ppermute | solution.py:35
  229.0 10.3 %collective-permute-done.22 = bf16[128,4096]{1,0:T(8,128)(2,1)S(1)} collective-permute-done((bf16[128,4096]{1,0:T(8,128)(2,1)S(1)}, bf16[128,4096]{1,0:T(8,128)(2,1)S(1)}, u32[]{:S(2)}, u32[]{:S(2)}) %collective-permute-start.22) | collective-permute-done | bytes 1048608 | tf_op jit(solution)/shard_map/ppermute | solution.py:35
  241.7 0.8 collective-permute-start.24
  242.5 6.9 %collective-permute-done.35 = bf16[32,4096]{1,0:T(8,128)(2,1)S(1)} collective-permute-done((bf16[32,4096]{1,0:T(8,128)(2,1)S(1)}, bf16[32,4096]{1,0:T(8,128)(2,1)S(1)}, u32[]{:S(2)}, u32[]{:S(2)}) %collective-permute-start.35) | collective-permute-done | bytes 262176 | tf_op jit(solution)/shard_map/ppermute | solution.py:23
  249.5 2.1 collective-permute-start.36
  251.6 13.2 %outer.1 = f32[1024,4096]{1,0:T(8,128)} custom-call(bf16[256,4224]{1,0:T(8,128)(2,1)S(1)} %copy-done.5, bf16[384,4224]{1,0:T(8,128)(2,1)S(1)} %constant_dynamic-update-slice_fusion.7.refs_1_, bf16[384,4224]{1,0:T(8,128)(2,1)} %collective-permute-done.14.refs_2_, bf16[1024,512]{1,0:T(8,128)(2,1)S(1)} %get-tuple-element.28.refs_3_, ...), custom_call_target="tpu_custom_call" | custom-call | flops 8589934592 | bytes 33554432 | tf_op jit(solution)/shard_map/outer/pallas_call | solution.py:187
  264.8 0.8 add_convert_fusion.10
  (112 shorter events, 13.6 us)
Async XLA Ops:
  2.5 8.8 %collective-permute-start = (bf16[2,384,256]{2,1,0:T(8,128)(2,1)S(1)}, bf16[2,384,256]{2,1,0:T(8,128)(2,1)}, u32[]{:S(2)}, u32[]{:S(2)}) collective-permute-start(bf16[2,384,256]{2,1,0:T(8,128)(2,1)S(1)} %constant_dynamic-update-slice_fusion), channel_id=1, source_target_pairs={{0,4},{4,0},{8,12},{12,8},{16,20},{20,16},{24,28},{28,24},{1,5},{5... | collective-permute-start | bytes 1179656 | tf_op jit(solution)/shard_map/ppermute | solution.py:19
  5.6 18.7 %collective-permute-start.8 = (bf16[32,4224]{1,0:T(8,128)(2,1)}, bf16[32,4224]{1,0:T(8,128)(2,1)}, u32[]{:S(2)}, u32[]{:S(2)}) collective-permute-start(bf16[32,4224]{1,0:T(8,128)(2,1)} %get-tuple-element.34), channel_id=1, source_target_pairs={{0,1},{1,0},{2,3},{3,2},{4,5},{5,4},{6,7},{7,6},{8,9},{9,8},{10,11... | collective-permute-start | bytes 811016 | tf_op jit(solution)/shard_map/ppermute | solution.py:23
  8.2 15.7 %collective-permute-start.9 = (bf16[32,4224]{1,0:T(8,128)(2,1)}, bf16[32,4224]{1,0:T(8,128)(2,1)}, u32[]{:S(2)}, u32[]{:S(2)}) collective-permute-start(bf16[32,4224]{1,0:T(8,128)(2,1)} %get-tuple-element.34), channel_id=1, source_target_pairs={{0,2},{1,3},{2,0},{3,1},{4,6},{5,7},{6,4},{7,5},{8,10},{9,11},{10,... | collective-permute-start | bytes 811016 | tf_op jit(solution)/shard_map/ppermute | solution.py:23
  12.4 17.1 %copy-start.6 = (bf16[4,384,256]{2,1,0:T(8,128)(2,1)}, bf16[4,384,256]{2,1,0:T(8,128)(2,1)S(1)}, u32[]{:S(2)}) copy-start(bf16[4,384,256]{2,1,0:T(8,128)(2,1)S(1)} %pad_maximum_fusion.4.refs_2_.refs_3_.refs_4_.refs_5_) | copy-start | bytes 2359300
  12.4 12.8 %collective-permute-start.1 = (bf16[4,384,256]{2,1,0:T(8,128)(2,1)S(1)}, bf16[4,384,256]{2,1,0:T(8,128)(2,1)}, u32[]{:S(2)}, u32[]{:S(2)}) collective-permute-start(bf16[4,384,256]{2,1,0:T(8,128)(2,1)S(1)} %pad_maximum_fusion.4.refs_2_.refs_3_.refs_4_.refs_5_), channel_id=1, source_target_pairs={{0,8},{4,20},{8,0},{12,28},{16,24},{20,4},{24,16},{28,12},{1,9},{5... | collective-permute-start | bytes 2359304 | tf_op jit(solution)/shard_map/ppermute | solution.py:35
  23.8 11.2 %collective-permute-start.10 = (bf16[32,4224]{1,0:T(8,128)(2,1)}, bf16[32,4224]{1,0:T(8,128)(2,1)}, u32[]{:S(2)}, u32[]{:S(2)}) collective-permute-start(bf16[32,4224]{1,0:T(8,128)(2,1)} %collective-permute-done.9), channel_id=1, source_target_pairs={{0,1},{1,0},{2,3},{3,2},{4,5},{5,4},{6,7},{7,6},{8,9},{9,8},{10,11... | collective-permute-start | bytes 811016 | tf_op jit(solution)/shard_map/ppermute | solution.py:23
  27.0 8.0 %collective-permute-start.2 = (bf16[2,384,256]{2,1,0:T(8,128)(2,1)}, bf16[2,384,256]{2,1,0:T(8,128)(2,1)S(1)}, u32[]{:S(2)}, u32[]{:S(2)}) collective-permute-start(bf16[2,384,256]{2,1,0:T(8,128)(2,1)} %slice.116), channel_id=1, source_target_pairs={{0,16},{4,12},{8,24},{12,4},{16,0},{20,28},{24,8},{28,20},{1,17},{... | collective-permute-start | bytes 1179656 | tf_op jit(solution)/shard_map/ppermute | solution.py:35
  28.6 9.2 %collective-permute-start.4 = (bf16[4,384,256]{2,1,0:T(8,128)(2,1)}, bf16[4,384,256]{2,1,0:T(8,128)(2,1)}, u32[]{:S(2)}, u32[]{:S(2)}) collective-permute-start(bf16[4,384,256]{2,1,0:T(8,128)(2,1)} %collective-permute-done.1.refs_2_.refs_3_.refs_6_.refs_7_), channel_id=1, source_target_pairs={{0,4},{4,0},{8,12},{12,8},{16,20},{20,16},{24,28},{28,24},{1,5},{5... | collective-permute-start | bytes 2359304 | tf_op jit(solution)/shard_map/ppermute | solution.py:19
  35.0 8.6 %copy-start.11 = (bf16[2,384,256]{2,1,0:T(8,128)(2,1)}, bf16[2,384,256]{2,1,0:T(8,128)(2,1)S(1)}, u32[]{:S(2)}) copy-start(bf16[2,384,256]{2,1,0:T(8,128)(2,1)S(1)} %collective-permute-done.2.refs_2_.refs_4_) | copy-start | bytes 1179652
  35.0 8.6 %collective-permute-start.3 = (bf16[2,384,256]{2,1,0:T(8,128)(2,1)S(1)}, bf16[2,384,256]{2,1,0:T(8,128)(2,1)S(1)}, u32[]{:S(2)}, u32[]{:S(2)}) collective-permute-start(bf16[2,384,256]{2,1,0:T(8,128)(2,1)S(1)} %collective-permute-done.2.refs_2_.refs_4_), channel_id=1, source_target_pairs={{0,4},{4,0},{8,12},{12,8},{16,20},{20,16},{24,28},{28,24},{1,5},{5... | collective-permute-start | bytes 1179656 | tf_op jit(solution)/shard_map/ppermute | solution.py:19
  37.4 28.5 %collective-permute-start.11 = (bf16[128,4224]{1,0:T(8,128)(2,1)}, bf16[128,4224]{1,0:T(8,128)(2,1)}, u32[]{:S(2)}, u32[]{:S(2)}) collective-permute-start(bf16[128,4224]{1,0:T(8,128)(2,1)} %pad_maximum_fusion), channel_id=1, source_target_pairs={{0,4},{4,0},{8,12},{12,8},{16,20},{20,16},{24,28},{28,24},{1,5},{5... | collective-permute-start | bytes 3244040 | tf_op jit(solution)/shard_map/ppermute | solution.py:19
  43.7 0.8 copy-start.12
  53.9 22.6 %copy-start.13 = (bf16[32,4096]{1,0:T(8,128)(2,1)S(1)}, bf16[32,4096]{1,0:T(8,128)(2,1)}, u32[]{:S(2)}) copy-start(bf16[32,4096]{1,0:T(8,128)(2,1)} %param.15) | copy-start | bytes 786436
  53.9 9.2 %collective-permute-start.6 = (bf16[32,4096]{1,0:T(8,128)(2,1)S(1)}, bf16[32,4096]{1,0:T(8,128)(2,1)S(1)}, u32[]{:S(2)}, u32[]{:S(2)}) collective-permute-start(bf16[32,4096]{1,0:T(8,128)(2,1)S(1)} %get-tuple-element.33), channel_id=1, source_target_pairs={{0,1},{1,0},{2,3},{3,2},{4,5},{5,4},{6,7},{7,6},{8,9},{9,8},{10,11... | collective-permute-start | bytes 786440 | tf_op jit(solution)/shard_map/ppermute | solution.py:23
  56.6 16.2 %collective-permute-start.5 = (bf16[32,4096]{1,0:T(8,128)(2,1)S(1)}, bf16[32,4096]{1,0:T(8,128)(2,1)S(1)}, u32[]{:S(2)}, u32[]{:S(2)}) collective-permute-start(bf16[32,4096]{1,0:T(8,128)(2,1)S(1)} %get-tuple-element.32), channel_id=1, source_target_pairs={{0,1},{1,0},{2,3},{3,2},{4,5},{5,4},{6,7},{7,6},{8,9},{9,8},{10,11... | collective-permute-start | bytes 786440 | tf_op jit(solution)/shard_map/ppermute | solution.py:23
  63.2 13.6 %copy-start.15 = (f32[4096]{0:T(1024)S(1)}, f32[4096]{0:T(1024)}, u32[]{:S(2)}) copy-start(f32[4096]{0:T(1024)} %param.17) | copy-start | bytes 49156
  63.2 13.3 %collective-permute-start.7 = (bf16[32,4096]{1,0:T(8,128)(2,1)S(1)}, bf16[32,4096]{1,0:T(8,128)(2,1)S(1)}, u32[]{:S(2)}, u32[]{:S(2)}) collective-permute-start(bf16[32,4096]{1,0:T(8,128)(2,1)S(1)} %fusion), channel_id=1, source_target_pairs={{0,2},{1,3},{2,0},{3,1},{4,6},{5,7},{6,4},{7,5},{8,10},{9,11},{10,... | collective-permute-start | bytes 786440 | tf_op jit(solution)/shard_map/ppermute | solution.py:23
  67.3 30.0 %copy-start.4 = (bf16[256,4224]{1,0:T(8,128)(2,1)}, bf16[256,4224]{1,0:T(8,128)(2,1)S(1)}, u32[]{:S(2)}) copy-start(bf16[256,4224]{1,0:T(8,128)(2,1)S(1)} %constant_dynamic-update-slice_fusion.2.refs_0_) | copy-start | bytes 6488068
  67.3 30.1 %collective-permute-start.12 = (bf16[256,4224]{1,0:T(8,128)(2,1)S(1)}, bf16[256,4224]{1,0:T(8,128)(2,1)S(1)}, u32[]{:S(2)}, u32[]{:S(2)}) collective-permute-start(bf16[256,4224]{1,0:T(8,128)(2,1)S(1)} %constant_dynamic-update-slice_fusion.2.refs_0_), channel_id=1, source_target_pairs={{0,8},{4,20},{8,0},{12,28},{16,24},{20,4},{24,16},{28,12},{1,9},{5... | collective-permute-start | bytes 6488072 | tf_op jit(solution)/shard_map/ppermute | solution.py:35
  76.8 20.5 %copy-start.7 = (f32[32,4096]{1,0:T(8,128)}, f32[32,4096]{1,0:T(8,128)S(1)}, u32[]{:S(2)}) copy-start(f32[32,4096]{1,0:T(8,128)S(1)} %get-tuple-element.31) | copy-start | bytes 1572868
  77.0 11.0 %collective-permute-start.25 = (bf16[32,4096]{1,0:T(8,128)(2,1)S(1)}, bf16[32,4096]{1,0:T(8,128)(2,1)S(1)}, u32[]{:S(2)}, u32[]{:S(2)}) collective-permute-start(bf16[32,4096]{1,0:T(8,128)(2,1)S(1)} %multiply_convert_fusion), channel_id=1, source_target_pairs={{0,2},{1,3},{2,0},{3,1},{4,6},{5,7},{6,4},{7,5},{8,10},{9,11},{10,... | collective-permute-start | bytes 786440 | tf_op jit(solution)/shard_map/ppermute | solution.py:23
  88.0 9.2 %collective-permute-start.26 = (bf16[32,4096]{1,0:T(8,128)(2,1)S(1)}, bf16[32,4096]{1,0:T(8,128)(2,1)S(1)}, u32[]{:S(2)}, u32[]{:S(2)}) collective-permute-start(bf16[32,4096]{1,0:T(8,128)(2,1)S(1)} %collective-permute-done.25), channel_id=1, source_target_pairs={{0,1},{1,0},{2,3},{3,2},{4,5},{5,4},{6,7},{7,6},{8,9},{9,8},{10,11... | collective-permute-start | bytes 786440 | tf_op jit(solution)/shard_map/ppermute | solution.py:23
  88.7 34.8 %collective-permute-start.15 = (bf16[32,4096]{1,0:T(8,128)(2,1)S(1)}, bf16[32,4096]{1,0:T(8,128)(2,1)S(1)}, u32[]{:S(2)}, u32[]{:S(2)}) collective-permute-start(bf16[32,4096]{1,0:T(8,128)(2,1)S(1)} %multiply_convert_fusion), channel_id=1, source_target_pairs={{0,1},{1,0},{2,3},{3,2},{4,5},{5,4},{6,7},{7,6},{8,9},{9,8},{10,11... | collective-permute-start | bytes 786440 | tf_op jit(solution)/shard_map/ppermute | solution.py:23
  97.2 2.0 collective-permute-start.27
  97.4 25.9 %collective-permute-start.13 = (bf16[128,4224]{1,0:T(8,128)(2,1)S(1)}, bf16[128,4224]{1,0:T(8,128)(2,1)S(1)}, u32[]{:S(2)}, u32[]{:S(2)}) collective-permute-start(bf16[128,4224]{1,0:T(8,128)(2,1)S(1)} %slice.118), channel_id=1, source_target_pairs={{0,16},{4,12},{8,24},{12,4},{16,0},{20,28},{24,8},{28,20},{1,17},{... | collective-permute-start | bytes 3244040 | tf_op jit(solution)/shard_map/ppermute | solution.py:35
  99.2 1.7 copy-start.2
  99.2 24.9 %collective-permute-start.28 = (bf16[128,4096]{1,0:T(8,128)(2,1)S(1)}, bf16[128,4096]{1,0:T(8,128)(2,1)S(1)}, u32[]{:S(2)}, u32[]{:S(2)}) collective-permute-start(bf16[128,4096]{1,0:T(8,128)(2,1)S(1)} %constant_dynamic-update-slice_fusion.11.refs_0_), channel_id=1, source_target_pairs={{0,8},{4,20},{8,0},{12,28},{16,24},{20,4},{24,16},{28,12},{1,9},{5... | collective-permute-start | bytes 3145736 | tf_op jit(solution)/shard_map/ppermute | solution.py:35
  123.4 34.1 %collective-permute-start.14 = (bf16[384,4224]{1,0:T(8,128)(2,1)S(1)}, bf16[384,4224]{1,0:T(8,128)(2,1)}, u32[]{:S(2)}, u32[]{:S(2)}) collective-permute-start(bf16[384,4224]{1,0:T(8,128)(2,1)S(1)} %constant_dynamic-update-slice_fusion.7.refs_1_), channel_id=1, source_target_pairs={{0,4},{4,0},{8,12},{12,8},{16,20},{20,16},{24,28},{28,24},{1,5},{5... | collective-permute-start | bytes 9732104 | tf_op jit(solution)/shard_map/ppermute | solution.py:19
  123.6 6.5 %collective-permute-start.16 = (bf16[64,4096]{1,0:T(8,128)(2,1)S(1)}, bf16[64,4096]{1,0:T(8,128)(2,1)S(1)}, u32[]{:S(2)}, u32[]{:S(2)}) collective-permute-start(bf16[64,4096]{1,0:T(8,128)(2,1)S(1)} %pad_maximum_fusion.5), channel_id=1, source_target_pairs={{0,4},{4,0},{8,12},{12,8},{16,20},{20,16},{24,28},{28,24},{1,5},{5... | collective-permute-start | bytes 1572872 | tf_op jit(solution)/shard_map/ppermute | solution.py:19
  124.2 9.7 %collective-permute-start.29 = (bf16[64,4096]{1,0:T(8,128)(2,1)S(1)}, bf16[64,4096]{1,0:T(8,128)(2,1)S(1)}, u32[]{:S(2)}, u32[]{:S(2)}) collective-permute-start(bf16[64,4096]{1,0:T(8,128)(2,1)S(1)} %slice.132), channel_id=1, source_target_pairs={{0,16},{4,12},{8,24},{12,4},{16,0},{20,28},{24,8},{28,20},{1,17},{... | collective-permute-start | bytes 1572872 | tf_op jit(solution)/shard_map/ppermute | solution.py:35
  130.1 16.7 %copy-start = (bf16[128,4096]{1,0:T(8,128)(2,1)}, bf16[128,4096]{1,0:T(8,128)(2,1)S(1)}, u32[]{:S(2)}) copy-start(bf16[128,4096]{1,0:T(8,128)(2,1)S(1)} %pad_maximum_fusion.1.refs_0_) | copy-start | bytes 3145732
  130.1 18.2 %copy-start.14 = (bf16[4096,4]{0,1:T(4,128)(2,1)S(1)}, bf16[4096,4]{0,1:T(4,128)(2,1)}, u32[]{:S(2)}) copy-start(bf16[4096,4]{0,1:T(4,128)(2,1)} %param.18) | copy-start | bytes 98308
  130.2 14.9 %collective-permute-start.17 = (bf16[128,4096]{1,0:T(8,128)(2,1)S(1)}, bf16[128,4096]{1,0:T(8,128)(2,1)S(1)}, u32[]{:S(2)}, u32[]{:S(2)}) collective-permute-start(bf16[128,4096]{1,0:T(8,128)(2,1)S(1)} %pad_maximum_fusion.1.refs_0_), channel_id=1, source_target_pairs={{0,8},{4,20},{8,0},{12,28},{16,24},{20,4},{24,16},{28,12},{1,9},{5... | collective-permute-start | bytes 3145736 | tf_op jit(solution)/shard_map/ppermute | solution.py:35
  134.7 23.7 %collective-permute-start.30 = (bf16[192,4096]{1,0:T(8,128)(2,1)}, bf16[192,4096]{1,0:T(8,128)(2,1)}, u32[]{:S(2)}, u32[]{:S(2)}) collective-permute-start(bf16[192,4096]{1,0:T(8,128)(2,1)} %constant_dynamic-update-slice_fusion.14.refs_1_), channel_id=1, source_target_pairs={{0,4},{4,0},{8,12},{12,8},{16,20},{20,16},{24,28},{28,24},{1,5},{5... | collective-permute-start | bytes 4718600 | tf_op jit(solution)/shard_map/ppermute | solution.py:19
  145.0 1.0 copy-start.9
  146.8 9.5 %collective-permute-start.18 = (bf16[64,4096]{1,0:T(8,128)(2,1)}, bf16[64,4096]{1,0:T(8,128)(2,1)}, u32[]{:S(2)}, u32[]{:S(2)}) collective-permute-start(bf16[64,4096]{1,0:T(8,128)(2,1)} %slice.122), channel_id=1, source_target_pairs={{0,16},{4,12},{8,24},{12,4},{16,0},{20,28},{24,8},{28,20},{1,17},{... | collective-permute-start | bytes 1572872 | tf_op jit(solution)/shard_map/ppermute | solution.py:35
  149.8 2.4 copy-start.10
  152.1 6.3 %copy-start.3 = (bf16[128,4096]{1,0:T(8,128)(2,1)S(1)}, bf16[128,4096]{1,0:T(8,128)(2,1)}, u32[]{:S(2)}) copy-start(bf16[128,4096]{1,0:T(8,128)(2,1)} %copy-done.2) | copy-start | bytes 3145732
  157.4 24.0 %collective-permute-start.19 = (bf16[192,4096]{1,0:T(8,128)(2,1)S(1)}, bf16[192,4096]{1,0:T(8,128)(2,1)S(1)}, u32[]{:S(2)}, u32[]{:S(2)}) collective-permute-start(bf16[192,4096]{1,0:T(8,128)(2,1)S(1)} %constant_dynamic-update-slice_fusion.9.refs_1_), channel_id=1, source_target_pairs={{0,4},{4,0},{8,12},{12,8},{16,20},{20,16},{24,28},{28,24},{1,5},{5... | collective-permute-start | bytes 4718600 | tf_op jit(solution)/shard_map/ppermute | solution.py:19
  158.5 22.9 %copy-start.1 = (bf16[128,4096]{1,0:T(8,128)(2,1)S(1)}, bf16[128,4096]{1,0:T(8,128)(2,1)}, u32[]{:S(2)}) copy-start(bf16[128,4096]{1,0:T(8,128)(2,1)} %copy-done) | copy-start | bytes 3145732
  180.8 21.2 %collective-permute-start.31 = (bf16[192,4096]{1,0:T(8,128)(2,1)S(1)}, bf16[192,4096]{1,0:T(8,128)(2,1)S(1)}, u32[]{:S(2)}, u32[]{:S(2)}) collective-permute-start(bf16[192,4096]{1,0:T(8,128)(2,1)S(1)} %get-tuple-element.27), channel_id=1, source_target_pairs={{0,4},{4,0},{8,12},{12,8},{16,20},{20,16},{24,28},{28,24},{1,5},{5... | collective-permute-start | bytes 4718600 | tf_op jit(solution)/shard_map/ppermute | solution.py:19
  201.9 3.5 %collective-permute-start.20 = (bf16[192,4096]{1,0:T(8,128)(2,1)S(1)}, bf16[192,4096]{1,0:T(8,128)(2,1)S(1)}, u32[]{:S(2)}, u32[]{:S(2)}) collective-permute-start(bf16[192,4096]{1,0:T(8,128)(2,1)S(1)} %get-tuple-element.24), channel_id=1, source_target_pairs={{0,4},{4,0},{8,12},{12,8},{16,20},{20,16},{24,28},{28,24},{1,5},{5... | collective-permute-start | bytes 4718600 | tf_op jit(solution)/shard_map/ppermute | solution.py:19
  202.5 9.2 %collective-permute-start.32 = (bf16[64,4096]{1,0:T(8,128)(2,1)S(1)}, bf16[64,4096]{1,0:T(8,128)(2,1)S(1)}, u32[]{:S(2)}, u32[]{:S(2)}) collective-permute-start(bf16[64,4096]{1,0:T(8,128)(2,1)S(1)} %add_convert_fusion.6), channel_id=1, source_target_pairs={{0,16},{4,12},{8,24},{12,4},{16,0},{20,28},{24,8},{28,20},{1,17},{... | collective-permute-start | bytes 1572872 | tf_op jit(solution)/shard_map/ppermute | solution.py:35
  205.8 14.6 %collective-permute-start.21 = (bf16[64,4096]{1,0:T(8,128)(2,1)S(1)}, bf16[64,4096]{1,0:T(8,128)(2,1)S(1)}, u32[]{:S(2)}, u32[]{:S(2)}) collective-permute-start(bf16[64,4096]{1,0:T(8,128)(2,1)S(1)} %add_convert_fusion.9), channel_id=1, source_target_pairs={{0,16},{4,12},{8,24},{12,4},{16,0},{20,28},{24,8},{28,20},{1,17},{... | collective-permute-start | bytes 1572872 | tf_op jit(solution)/shard_map/ppermute | solution.py:35
  211.9 16.1 %collective-permute-start.33 = (bf16[128,4096]{1,0:T(8,128)(2,1)S(1)}, bf16[128,4096]{1,0:T(8,128)(2,1)S(1)}, u32[]{:S(2)}, u32[]{:S(2)}) collective-permute-start(bf16[128,4096]{1,0:T(8,128)(2,1)S(1)} %pad_maximum_fusion.3), channel_id=1, source_target_pairs={{0,8},{4,20},{8,0},{12,28},{16,24},{20,4},{24,16},{28,12},{1,9},{5... | collective-permute-start | bytes 3145736 | tf_op jit(solution)/shard_map/ppermute | solution.py:35
  220.7 18.6 %collective-permute-start.22 = (bf16[128,4096]{1,0:T(8,128)(2,1)S(1)}, bf16[128,4096]{1,0:T(8,128)(2,1)S(1)}, u32[]{:S(2)}, u32[]{:S(2)}) collective-permute-start(bf16[128,4096]{1,0:T(8,128)(2,1)S(1)} %pad_maximum_fusion.2), channel_id=1, source_target_pairs={{0,8},{4,20},{8,0},{12,28},{16,24},{20,4},{24,16},{28,12},{1,9},{5... | collective-permute-start | bytes 3145736 | tf_op jit(solution)/shard_map/ppermute | solution.py:35
  228.4 11.6 %collective-permute-start.34 = (bf16[64,4096]{1,0:T(8,128)(2,1)S(1)}, bf16[64,4096]{1,0:T(8,128)(2,1)S(1)}, u32[]{:S(2)}, u32[]{:S(2)}) collective-permute-start(bf16[64,4096]{1,0:T(8,128)(2,1)S(1)} %slice.138), channel_id=1, source_target_pairs={{0,4},{4,0},{8,12},{12,8},{16,20},{20,16},{24,28},{28,24},{1,5},{5... | collective-permute-start | bytes 1572872 | tf_op jit(solution)/shard_map/ppermute | solution.py:19
  239.6 2.0 collective-permute-start.23
  240.1 11.5 %copy-start.5 = (bf16[256,4224]{1,0:T(8,128)(2,1)S(1)}, bf16[256,4224]{1,0:T(8,128)(2,1)}, u32[]{:S(2)}) copy-start(bf16[256,4224]{1,0:T(8,128)(2,1)} %copy-done.4) | copy-start | bytes 6488068
  240.2 9.2 %collective-permute-start.35 = (bf16[32,4096]{1,0:T(8,128)(2,1)S(1)}, bf16[32,4096]{1,0:T(8,128)(2,1)S(1)}, u32[]{:S(2)}, u32[]{:S(2)}) collective-permute-start(bf16[32,4096]{1,0:T(8,128)(2,1)S(1)} %slice.140), channel_id=1, source_target_pairs={{0,1},{1,0},{2,3},{3,2},{4,5},{5,4},{6,7},{7,6},{8,9},{9,8},{10,11... | collective-permute-start | bytes 786440 | tf_op jit(solution)/shard_map/ppermute | solution.py:23
  241.7 23.1 %collective-permute-start.24 = (bf16[32,4096]{1,0:T(8,128)(2,1)S(1)}, bf16[32,4096]{1,0:T(8,128)(2,1)S(1)}, u32[]{:S(2)}, u32[]{:S(2)}) collective-permute-start(bf16[32,4096]{1,0:T(8,128)(2,1)S(1)} %slice.130), channel_id=1, source_target_pairs={{0,1},{1,0},{2,3},{3,2},{4,5},{5,4},{6,7},{7,6},{8,9},{9,8},{10,11... | collective-permute-start | bytes 786440 | tf_op jit(solution)/shard_map/ppermute | solution.py:23
  249.5 15.3 %collective-permute-start.36 = (bf16[32,4096]{1,0:T(8,128)(2,1)S(1)}, bf16[32,4096]{1,0:T(8,128)(2,1)S(1)}, u32[]{:S(2)}, u32[]{:S(2)}) collective-permute-start(bf16[32,4096]{1,0:T(8,128)(2,1)S(1)} %add_convert_fusion.11), channel_id=1, source_target_pairs={{0,2},{1,3},{2,0},{3,1},{4,6},{5,7},{6,4},{7,5},{8,10},{9,11},{10,... | collective-permute-start | bytes 786440 | tf_op jit(solution)/shard_map/ppermute | solution.py:23
  251.6 13.2 %copy-start.8 = (f32[32,4096]{1,0:T(8,128)S(1)}, f32[32,4096]{1,0:T(8,128)}, u32[]{:S(2)}) copy-start(f32[32,4096]{1,0:T(8,128)} %copy-done.7) | copy-start | bytes 1572868
where the time goes:
time: 267 us; the launch traced here: 266 us
  waiting for transfers between devices  120 us (45%)
  Pallas kernels  70.7 us (26%)
  starting transfers between devices  38.4 us (14%)
  local copies, waits for them, and re-layouts  19.8 us (7%)
  other arithmetic  10.5 us (4%)
  matrix products  4.74 us (2%)
    ppermute x12, waiting for transfers between devices, cross(): return lax.ppermute(value, 'ctx', pairs)  66.5 us
    ppermute x12, waiting for transfers between devices, swap_plane(): lax.ppermute(value, 'exp', [(i, i ^ bits) for i in range(lax.axis_size('e...  47.4 us
    pallas_call x2, Pallas kernels, expert(): pl.pallas_call(functools.partial(expert_kernel, len(rows), steps), out_sh...  42.9 us
    ppermute x12, starting transfers between devices, cross(): return lax.ppermute(value, 'ctx', pairs)  18.8 us
    ppermute x12, starting transfers between devices, swap_plane(): lax.ppermute(value, 'exp', [(i, i ^ bits) for i in range(lax.axis_size('e...  16.2 us
    pallas_call x3, Pallas kernels, attend(): pl.pallas_call(functools.partial(attend_kernel, slots, cached, window_fre...  14.7 us
    pallas_call x1, Pallas kernels, outer(): pl.pallas_call(functools.partial(outer_kernel, len(grads), pieces, blocks...  13.2 us
    unnamed x42, local copies, waits for them, and re-layouts  8.45 us
  transfers between devices with their start and end apart: 37, of which 20 were waited for; matrix products, arithmetic and copies ran while one was open for 11% of the time, Pallas kernels for 27%

commit v1 on v0

--- a/solution.py
+++ b/solution.py
@@ -42,12 +42,20 @@
         for bit in bits + [1]:
             held = jnp.concatenate([held, swap(held, bit)], axis=0)
         return [held]
-    rows = block.shape[0]
-    pair = jnp.concatenate([block, swap(block, 1)], axis=0)
-    beside = cross(pair, 0)
-    opposite = cross(beside[:rows], 1)
-    sent = jnp.concatenate([beside, opposite], axis=0)
-    return [pair, sent, swap(sent, 1)]
+    beside = cross(block, 0)
+    mate = swap(block, 1)
+    beside_mate = cross(mate, 0)
+    opposite = cross(beside, 1)
+    return [
+        block,
+        mate,
+        beside,
+        beside_mate,
+        opposite,
+        swap(beside, 1),
+        swap(beside_mate, 1),
+        swap(opposite, 1),
+    ]
 
 
 def plus(a, b):
@@ -62,30 +70,34 @@
             middle = held.shape[0] // 2
             held = plus(held[:middle], swap(held[middle:], bit))
         return held
-    pair, sent, theirs = parts
-    rows = pair.shape[0] // 2
-    got = swap(theirs, 1)
-    returned = cross(plus(sent[2 * rows :], got[2 * rows :]), 1)
-    beside = plus(sent[: 2 * rows], got[: 2 * rows])
-    beside = jnp.concatenate([plus(beside[:rows], returned), beside[rows:]], axis=0)
-    pair = plus(pair, cross(beside, 0))
-    return plus(pair[:rows], swap(pair[rows:], 1))
-
-
-def expert_kernel(parts, steps, place, tags_ref, router_ref, *refs):
-    rows_refs = refs[:parts]
-    gate_ref, up_ref, down_ref = refs[parts : parts + 3]
-    part_refs = refs[parts + 3 : 2 * parts + 3]
-    turned_ref, rows_all, weight_ref, hidden_ref = refs[2 * parts + 3 :]
-    step = pl.program_id(0)
-    wide = gate_ref.shape[1]
-
-    @pl.when(step == 0)
+    own, mate, beside, beside_mate, opposite, *theirs = parts
+    opposite = plus(opposite, swap(theirs[2], 1))
+    returned = cross(opposite, 1)
+    beside_mate = plus(beside_mate, swap(theirs[1], 1))
+    mate = plus(mate, cross(beside_mate, 0))
+    beside = plus(plus(beside, swap(theirs[0], 1)), returned)
+    own = plus(own, swap(mate, 1))
+    return plus(own, cross(beside, 0))
+
+
+def rise_kernel(parts, planes, place, router_ref, *refs):
+    tag_refs, rows_refs = refs[:parts], refs[parts : 2 * parts]
+    gate_ref, up_ref, hidden_ref, turned_ref, rows_all, weight_ref, tags_ref = refs[2 * parts :]
+
+    @pl.when(pl.program_id(0) == 0)
     def _():
         at = 0
         for ref in rows_refs:
             rows_all[at : at + ref.shape[0]] = ref[...]
             at += ref.shape[0]
+        first_plane, last_plane, length = planes
+        at = 0
+        for ref in tag_refs:
+            for base in range(0, ref.shape[0], length[0]):
+                for k in range(first_plane, last_plane):
+                    start = base + k * length[1]
+                    tags_ref[at : at + length[1]] = ref[start : start + length[1]]
+                    at += length[1]
         logits = jnp.dot(rows_all[...], router_ref[...], preferred_element_type=jnp.float32)
         lane = lax.broadcasted_iota(jnp.int32, logits.shape, 1).astype(jnp.float32)
         tags = tags_ref[...].astype(jnp.float32)
@@ -97,71 +109,145 @@
         weight = jnp.where(one == mine, gate, 0.0) + jnp.where(two == mine, 1.0 - gate, 0.0)
         weight_ref[...] = jnp.broadcast_to(weight, weight_ref.shape)
 
-    @pl.when(step < steps)
-    def _():
-        rows = rows_all[...]
-        gate = jnp.dot(rows, gate_ref[...], preferred_element_type=jnp.float32)
-        up = jnp.dot(rows, up_ref[...], preferred_element_type=jnp.float32)
-        hidden = gate / (1.0 + jnp.exp(-gate)) * up * weight_ref[:, :1]
-        hidden = hidden.astype(jnp.bfloat16)
-        hidden_ref[:, pl.ds(pl.multiple_of(step * wide, wide), wide)] = hidden
-        turned_ref[...] = hidden.T
-
-    @pl.when(step >= steps)
-    def _():
-        part = jnp.dot(hidden_ref[...], down_ref[...], preferred_element_type=jnp.float32)
-        part = part.astype(jnp.bfloat16)
-        at = 0
-        for ref in part_refs:
-            ref[...] = part[at : at + ref.shape[0]]
-            at += ref.shape[0]
-
-
-def expert(place, tags, router, rows, gate_mat, up_mat, down_mat):
+    rows = rows_all[...]
+    gate = jnp.dot(rows, gate_ref[...], preferred_element_type=jnp.float32)
+    up = jnp.dot(rows, up_ref[...], preferred_element_type=jnp.float32)
+    hidden = gate / (1.0 + jnp.exp(-gate)) * up * weight_ref[:, :1]
+    hidden = hidden.astype(jnp.bfloat16)
+    hidden_ref[...] = hidden
+    turned_ref[...] = hidden.T
+
+
+def rise(place, grads, planes, router, rows, gate_mat, up_mat):
     width, units = gate_mat.shape
-    experts = router.shape[1]
-    router = jnp.pad(router, ((0, 0), (0, HEAD_SIZE - experts)))
+    tag = lambda g: pl.BlockSpec(
+        (g.shape[0], HEAD_SIZE),
+        lambda i, place: (0, width // HEAD_SIZE),
+        pipeline_mode=pl.Buffered(1),
+    )
     count = sum(r.shape[0] for r in rows)
-    wide, broad = min(256, units), min(1024, width)
-    steps, turns = units // wide, width // broad
+    wide = min(256, units)
     whole = lambda shape: pl.BlockSpec(
         shape, lambda i, place: (0, 0), pipeline_mode=pl.Buffered(1)
     )
-    late = lambda i, place: (0, jnp.maximum(i - steps, 0))
-    early = lambda i, place: (0, jnp.minimum(i, steps - 1))
+    column = lambda i, place: (0, i)
     return pl.pallas_call(
-        functools.partial(expert_kernel, len(rows), steps),
-        out_shape=[jax.ShapeDtypeStruct(r.shape, jnp.bfloat16) for r in rows]
-        + [jax.ShapeDtypeStruct((units, count), jnp.bfloat16)],
+        functools.partial(rise_kernel, len(rows), planes),
+        out_shape=[
+            jax.ShapeDtypeStruct((count, units), jnp.bfloat16),
+            jax.ShapeDtypeStruct((units, count), jnp.bfloat16),
+        ],
         grid_spec=pltpu.PrefetchScalarGridSpec(
             num_scalar_prefetch=1,
-            grid=(steps + turns,),
-            in_specs=[whole(tags.shape), whole(router.shape)]
+            grid=(units // wide,),
+            in_specs=[whole(router.shape)]
+            + [tag(g) for g in grads]
             + [whole(r.shape) for r in rows]
-            + [pl.BlockSpec((width, wide), early)] * 2
-            + [pl.BlockSpec((units, broad), late)],
-            out_specs=[pl.BlockSpec((r.shape[0], broad), late) for r in rows]
-            + [pl.BlockSpec((wide, count), lambda i, place: (jnp.minimum(i, steps - 1), 0))],
+            + [pl.BlockSpec((width, wide), column)] * 2,
+            out_specs=[
+                pl.BlockSpec((count, wide), column),
+                pl.BlockSpec((wide, count), lambda i, place: (i, 0)),
+            ],
             scratch_shapes=[
                 pltpu.VMEM((count, width), jnp.bfloat16),
                 pltpu.VMEM((count, HEAD_SIZE), jnp.float32),
-                pltpu.VMEM((count, units), jnp.bfloat16),
+                pltpu.VMEM((count, HEAD_SIZE), jnp.bfloat16),
             ],
         ),
-        compiler_params=pltpu.CompilerParams(vmem_limit_bytes=36 << 20),
+        compiler_params=pltpu.CompilerParams(vmem_limit_bytes=28 << 20),
         cost_estimate=pl.CostEstimate(
-            flops=6 * count * width * units,
+            flops=4 * count * width * units,
             transcendentals=count * units,
-            bytes_accessed=2 * (3 * width * units + 2 * count * width),
-        ),
-        name="expert",
-    )(place, tags, router, *rows, gate_mat, up_mat, down_mat)
+            bytes_accessed=2 * (2 * width * units + count * width),
+        ),
+        name="rise",
+    )(place, router, *grads, *rows, gate_mat, up_mat)
+
+
+def fall_kernel(hidden_ref, down_ref, *part_refs):
+    part = jnp.dot(hidden_ref[...], down_ref[...], preferred_element_type=jnp.float32)
+    part = part.astype(jnp.bfloat16)
+    at = 0
+    for ref in part_refs:
+        ref[...] = part[at : at + ref.shape[0]]
+        at += ref.shape[0]
+
+
+def fall(hidden, down_mat, counts):
+    units, width = down_mat.shape
+    broad = min(1024, width)
+    column = lambda i: (0, i)
+    return pl.pallas_call(
+        fall_kernel,
+        out_shape=[jax.ShapeDtypeStruct((c, width), jnp.bfloat16) for c in counts],
+        grid=(width // broad,),
+        in_specs=[
+            pl.BlockSpec(hidden.shape, lambda i: (0, 0), pipeline_mode=pl.Buffered(1)),
+            pl.BlockSpec((units, broad), column),
+        ],
+        out_specs=[pl.BlockSpec((c, broad), column) for c in counts],
+        compiler_params=pltpu.CompilerParams(vmem_limit_bytes=20 << 20),
+        cost_estimate=pl.CostEstimate(
+            flops=2 * sum(counts) * width * units,
+            transcendentals=0,
+            bytes_accessed=2 * (width * units + sum(counts) * width),
+        ),
+        name="fall",
+    )(hidden, down_mat)
+
+
+def project_kernel(planes, place, attn_ref, proj_ref, residual_ref, own_ref, *refs):
+    share_refs, sums_ref = refs[:-1], refs[-1]
+    rows = own_ref.shape[0]
+    sums_ref[...] = jnp.dot(attn_ref[...], proj_ref[...], preferred_element_type=jnp.float32)
+    for k in range(planes):
+        start = pl.multiple_of((place[0] ^ k) * rows, rows)
+        share = sums_ref[pl.ds(start, rows), :]
+        if k:
+            share_refs[k - 1][...] = share.astype(share_refs[k - 1].dtype)
+        else:
+            own_ref[...] = share + residual_ref[...].astype(jnp.float32)
+
+
+def project(place, attn, out_proj, residual):
+    rows, width = residual.shape
+    tokens = attn.shape[0]
+    planes = tokens // rows
+    broad = min(1024, width)
+    column = lambda i, place: (0, i)
+    small = pl.BlockSpec((rows, broad), column)
+    return pl.pallas_call(
+        functools.partial(project_kernel, planes),
+        out_shape=[jax.ShapeDtypeStruct((rows, width), jnp.float32)]
+        + [
+            jax.ShapeDtypeStruct((rows, width), jnp.bfloat16 if k % 2 else jnp.float32)
+            for k in range(1, planes)
+        ],
+        grid_spec=pltpu.PrefetchScalarGridSpec(
+            num_scalar_prefetch=1,
+            grid=(width // broad,),
+            in_specs=[
+                pl.BlockSpec(attn.shape, lambda i, place: (0, 0)),
+                pl.BlockSpec((out_proj.shape[0], broad), column),
+                small,
+            ],
+            out_specs=[small] * planes,
+            scratch_shapes=[pltpu.VMEM((tokens, broad), jnp.float32)],
+        ),
+        compiler_params=pltpu.CompilerParams(vmem_limit_bytes=16 << 20),
+        cost_estimate=pl.CostEstimate(
+            flops=2 * tokens * out_proj.shape[0] * width,
+            transcendentals=0,
+            bytes_accessed=2 * out_proj.shape[0] * width,
+        ),
+        name="project",
+    )(place, attn, out_proj, residual)
 
 
 def outer_kernel(parts, pieces, blocks, *refs):
     grad_refs = refs[:parts]
     turned_refs = refs[parts : parts + pieces]
-    out_ref, grads_ref = refs[parts + pieces :]
+    out_ref, grads_ref = refs[-2:]
     length = grads_ref.shape[1] // blocks
     block = 0
     for ref in grad_refs:
@@ -180,29 +266,34 @@
     out_ref[...] = total
 
 
-def outer(grads, turned, blocks, width):
+def outer(grads, turned, blocks, width, half, filled):
     units, count = turned[0].shape
-    broad = min(512, width)
+    broad = min(512, width // 2)
     pieces = len(turned)
+    steps = width // 2 // broad
+    column = lambda i: (0, i + half * steps)
+    more = [] if filled is None else [filled]
     return pl.pallas_call(
         functools.partial(outer_kernel, len(grads), pieces, blocks),
         out_shape=jax.ShapeDtypeStruct((units, width), jnp.float32),
-        grid=(width // broad,),
-        in_specs=[pl.BlockSpec((g.shape[0], broad), lambda i: (0, i)) for g in grads]
+        grid=(steps,),
+        in_specs=[pl.BlockSpec((g.shape[0], broad), column) for g in grads]
         + [
             pl.BlockSpec((units, count), lambda i: (0, 0), pipeline_mode=pl.Buffered(1))
             for _ in turned
-        ],
-        out_specs=pl.BlockSpec((units, broad), lambda i: (0, i)),
+        ]
+        + [pl.BlockSpec(memory_space=pl.ANY)] * len(more),
+        out_specs=pl.BlockSpec((units, broad), column),
+        input_output_aliases={len(grads) + pieces: 0} if more else {},
         scratch_shapes=[pltpu.VMEM((pieces, count, broad), jnp.bfloat16)],
         compiler_params=pltpu.CompilerParams(vmem_limit_bytes=24 << 20),
         cost_estimate=pl.CostEstimate(
-            flops=2 * units * count * pieces * width,
+            flops=units * count * pieces * width,
             transcendentals=0,
-            bytes_accessed=4 * units * width + 4 * count * pieces * width,
+            bytes_accessed=2 * units * width + 2 * count * pieces * width,
         ),
         name="outer",
-    )(*grads, *turned)
+    )(*grads, *turned, *more)
 
 
 def attend_kernel(slots, cached, window_free, start, final, *refs):
@@ -371,32 +462,25 @@
     parity = here % 2
     near = jnp.where(parity == 0, bits[0], bits[1])
     far = jnp.where(parity == 0, bits[1], bits[0])
-    mate = swap(own, 1)
-    pair = jnp.concatenate([own, mate], axis=0)
-    beside = cross(pair, 0)
-    opposite = cross(beside[:2], 1)
-    mate_beside = swap(beside, 1)
-    mate_opposite = swap(opposite, 1)
-    slot = lambda a, i: ((a, 2 * i), (a, 2 * i + 1))
-    state = stage([slot(pair, 0), slot(pair, 1)], places([0, 1]), state=None, final=False)
+    blocks = gather(own)
+    slots = [((b, 0), (b, 1)) for b in blocks]
+    across = near ^ far
+    state = stage(slots[:2], places([0, 1]), state=None, final=False)
     state = stage(
-        [slot(beside, 0), slot(beside, 1), slot(mate_beside, 0), slot(mate_beside, 1)],
+        [slots[2], slots[3], slots[5], slots[6]],
         places([near, near ^ 1, far ^ 1, far]),
         state=state,
         final=False,
     )
     return stage(
-        [slot(opposite, 0), slot(mate_opposite, 0)],
-        places([near ^ far, near ^ far ^ 1]),
-        state=state,
-        final=True,
-    )
-
-
-def planes_of(value):
+        [slots[4], slots[7]], places([across, across ^ 1]), state=state, final=True
+    )
+
+
+def planes_of(value, relay):
     blocks = [value]
     for k in range(1, lax.axis_size("exp")):
-        source, bits = (value, k) if k == 1 or k % 2 == 0 else (blocks[k - 1], 1)
+        source, bits = (blocks[k - 1], 1) if relay and k > 1 and k % 2 else (value, k)
         blocks.append(swap_plane(source, bits))
     return blocks
 
@@ -418,45 +502,46 @@
     ctx_size = lax.axis_size("ctx")
     planes = lax.axis_size("exp")
     plane = lax.axis_index("exp")
+    experts = router.shape[1]
     row_count, width = residual.shape
 
     tags = jnp.pad(expert_ids.astype(jnp.bfloat16), ((0, 0), (0, HEAD_SIZE - 2)))
-    tagged = planes_of(jnp.concatenate([cotangent, tags], axis=1))
+    tagged = planes_of(jnp.concatenate([cotangent, tags], axis=1), False)
     grads = gather(jnp.concatenate(tagged, axis=0))
-    ids = jnp.concatenate([g[:, width:] for g in grads], axis=0)
-    ids = ids.reshape(ctx_size, planes, row_count, HEAD_SIZE)
+    tall_router = jnp.pad(router, ((0, 0), (0, HEAD_SIZE - experts)))
+    query, tall_router = lax.optimization_barrier((query, tall_router))
 
     attn = attention(query, keys_values, cache)
 
-    partial = jnp.dot(attn, out_proj, preferred_element_type=jnp.float32)
-    partial = partial.reshape(planes, row_count, width)
-
-    def share(k):
-        return lax.dynamic_index_in_dim(partial, plane ^ k, 0, keepdims=False)
-
-    hidden_one = residual.astype(jnp.float32) + share(0)
+    place = jnp.full((1,), plane, jnp.int32)
+    hidden_one, *shares = project(
+        place, attn, pltpu.with_memory_space_constraint(out_proj, pltpu.HBM), residual
+    )
     for k in range(0, planes, 2):
-        both = swap_plane(share(k + 1).astype(jnp.bfloat16), 1)
+        both = swap_plane(shares[k], 1)
         if k:
-            both = swap_plane((share(k) + both.astype(jnp.float32)).astype(jnp.bfloat16), k)
+            both = (shares[k - 1] + both.astype(jnp.float32)).astype(jnp.bfloat16)
+            both = swap_plane(both, k)
         hidden_one = hidden_one + both.astype(jnp.float32)
     mean_square = jnp.mean(hidden_one * hidden_one, axis=-1, keepdims=True)
     normed = (hidden_one * lax.rsqrt(mean_square + EPSILON) * norm_gain).astype(jnp.bfloat16)
 
-    gate_mat = w_gate[0]
-    up_mat = w_up[0]
-    down_mat = w_down[0]
-    place = jnp.full((1,), plane, jnp.int32)
-    blocks = planes_of(normed)
-    turned = []
+    in_place = lambda a: pltpu.with_memory_space_constraint(a, pltpu.HBM)
+    gate_mat = in_place(w_gate[0])
+    up_mat = in_place(w_up[0])
+    down_mat = in_place(w_down[0])
+    blocks = planes_of(normed, True)
+    hidden, turned, counts = [], [], []
+    for k in range(0, planes, 2):
+        rows = gather(jnp.concatenate(blocks[k : k + 2], axis=0))
+        piece = (k, k + 2, (planes * row_count, row_count))
+        plain, flipped = rise(place, grads, piece, tall_router, rows, gate_mat, up_mat)
+        hidden.append(plain)
+        turned.append(flipped)
+        counts.append([r.shape[0] for r in rows])
     layer = hidden_one
     for k in range(0, planes, 2):
-        rows = gather(jnp.concatenate(blocks[k : k + 2], axis=0))
-        tags = ids[:, k : k + 2].reshape(-1, HEAD_SIZE)
-        *parts, turned_piece = expert(
-            place, tags, router, rows, gate_mat, up_mat, down_mat
-        )
-        turned.append(turned_piece)
+        parts = fall(hidden[k // 2], down_mat, counts[k // 2])
         summed = scatter(parts)
         both = plus(summed[:row_count], swap_plane(summed[row_count:], 1))
         if k:
@@ -464,7 +549,8 @@
         layer = layer + both.astype(jnp.float32)
     layer_out = layer.astype(jnp.bfloat16)
 
-    gradient = outer(grads, turned, ctx_size, width)
+    gradient = outer(grads, turned, ctx_size, width, 0, None)
+    gradient = outer(grads, turned, ctx_size, width, 1, gradient)
     return (layer_out, gradient[None])
 
 

time: 267 us -> 265 us (level)
  local copies, waits for them, and re-layouts: 19.8 us -> 5.15 us
  waiting for transfers between devices: 120 us -> 129 us
  starting transfers between devices: 38.4 us -> 46.3 us
  Pallas kernels: 70.7 us -> 77.8 us
  other arithmetic: 10.5 us -> 4.92 us
  matrix products: 4.74 us -> 0 us
    ppermute x12 -> x18, waiting for transfers between devices: 66.5 us -> 77.3 us  [cross(): return lax.ppermute(value, 'ctx', pairs)]
    ppermute x13 -> x24, waiting for transfers between devices: 6.41 us -> 0.93 us  [swap(): lax.ppermute(value, 'ctx', [(i, i ^ bit) for i in range(lax.axis_size('ct...]
    ppermute x12 -> x18, starting transfers between devices: 18.8 us -> 24.1 us  [cross(): return lax.ppermute(value, 'ctx', pairs)]
    unnamed x42 -> x19, local copies, waits for them, and re-layouts: 8.45 us -> 3.24 us
    pallas_call x2 -> x5, Pallas kernels: 42.9 us -> 47.8 us  [the longest x2 28.2 us: rise(): pl.pallas_call(functools.partial(rise_kernel, len(rows), planes), out_sha...]
    dot_general x1 -> x0, matrix products: 4.74 us -> none  [on_device(): partial = jnp.dot(attn, out_proj, preferred_element_type=jnp.float32)]
    slice x12 -> x0, local copies, waits for them, and re-layouts: 4.66 us -> none  [the longest x1 1.78 us: attention(): opposite = cross(beside[:2], 1)]
    ppermute x12, waiting for transfers between devices: 47.4 us -> 51.1 us  [swap_plane(): lax.ppermute(value, 'exp', [(i, i ^ bits) for i in range(lax.axis_size('e...]
  transfers between devices with their start and end apart: 37 -> 54, of which waited for: 20 -> 24; matrix products, arithmetic and copies ran while one was open for 11% -> 2% of each run, Pallas kernels for 27% -> 26%
where the time goes in v1:
time: 265 us; the launch traced here: 264 us
  waiting for transfers between devices  129 us (49%)
  Pallas kernels  77.8 us (29%)
  starting transfers between devices  46.3 us (17%)
  local copies, waits for them, and re-layouts  5.15 us (2%)
  other arithmetic  4.92 us (2%)
    ppermute x18, waiting for transfers between devices, cross(): return lax.ppermute(value, 'ctx', pairs)  77.3 us
    ppermute x12, waiting for transfers between devices, swap_plane(): lax.ppermute(value, 'exp', [(i, i ^ bits) for i in range(lax.axis_size('e...  51.1 us
    pallas_call x2, Pallas kernels, rise(): pl.pallas_call(functools.partial(rise_kernel, len(rows), planes), out_sha...  28.2 us
    ppermute x18, starting transfers between devices, cross(): return lax.ppermute(value, 'ctx', pairs)  24.1 us
    ppermute x12, starting transfers between devices, swap_plane(): lax.ppermute(value, 'exp', [(i, i ^ bits) for i in range(lax.axis_size('e...  16.9 us
    pallas_call x2, Pallas kernels, outer(): pl.pallas_call(functools.partial(outer_kernel, len(grads), pieces, blocks...  15.1 us
    pallas_call x3, Pallas kernels, attend(): pl.pallas_call(functools.partial(attend_kernel, slots, cached, window_fre...  14.8 us
    pallas_call x2, Pallas kernels, fall(): pl.pallas_call(fall_kernel, out_shape=[jax.ShapeDtypeStruct((c, width), j...  14.5 us
  transfers between devices with their start and end apart: 54, of which 24 were waited for; matrix products, arithmetic and copies ran while one was open for 2% of the time, Pallas kernels for 26%

profile of v1, /device:TPU:0, one launch (start us, length us, event | category | flops | bytes accessed | tf_op | source)
XLA Modules:
  0.0 264.5 jit_solution(3261012625128854346)
XLA Ops:
  0.6 1.0 constant_dynamic-update-slice_fusion.1
  1.6 0.9 constant_dynamic-update-slice_fusion.refs_2_.refs_4_
  3.1 2.6 collective-permute-start
  5.6 1.6 collective-permute-start.4
  7.3 4.1 %collective-permute-done.refs_2_.refs_6_ = bf16[2,384,256]{2,1,0:T(8,128)(2,1)S(1)} collective-permute-done((bf16[2,384,256]{2,1,0:T(8,128)(2,1)S(1)}, bf16[2,384,256]{2,1,0:T(8,128)(2,1)S(1)}, u32[]{:S(2)}, u32[]{:S(2)}) %collective-permute-start) | collective-permute-done | bytes 393248 | tf_op jit(solution)/shard_map/ppermute | solution.py:35
  11.4 2.0 collective-permute-start.1
  13.5 3.9 %collective-permute-done.4.refs_3_.refs_7_ = bf16[2,384,256]{2,1,0:T(8,128)(2,1)S(1)} collective-permute-done((bf16[2,384,256]{2,1,0:T(8,128)(2,1)S(1)}, bf16[2,384,256]{2,1,0:T(8,128)(2,1)S(1)}, u32[]{:S(2)}, u32[]{:S(2)}) %collective-permute-start.4) | collective-permute-done | bytes 393248 | tf_op jit(solution)/shard_map/ppermute | solution.py:35
  17.4 2.3 collective-permute-done.1.refs_2_.refs_4_
  19.8 0.7 convert_element_type.179
  20.6 1.3 copy.17
  22.1 0.6 stack.67.refs_0_
  22.7 0.6 pad_add_fusion.refs_0_
  23.3 0.6 pad_add_fusion.1.refs_0_
  23.9 4.2 %attend.3 = (f32[2,512,128]{2,1,0:T(8,128)}, f32[2,512,128]{2,1,0:T(8,128)}, f32[2,512,128]{2,1,0:T(8,128)}) custom-call(s32[4]{0:T(128)} %pad_add_fusion.1.refs_0_, bf16[128,1024]{1,0:T(8,128)(2,1)} %refs_1_.2, bf16[2,384,256]{2,1,0:T(8,128)(2,1)} %copy-done.2, bf16[2,384,256]{2,1,0:T(8,128)(2,1)} %copy-done.5, bf16[2,384,256]{2,1,0:T(8,128)(2,1)} %copy-done.2, ...), custom_call_target="tpu_custom_call" | custom-call | flops 402653184 | bytes 1572864 | tf_op jit(solution)/shard_map/attend/pallas_call | solution.py:418
  28.1 5.9 %attend.4 = (f32[2,512,128]{2,1,0:T(8,128)}, f32[2,512,128]{2,1,0:T(8,128)}, f32[2,512,128]{2,1,0:T(8,128)}) custom-call(s32[8]{0:T(128)} %stack.67.refs_0_, bf16[128,1024]{1,0:T(8,128)(2,1)} %refs_1_.2, bf16[2,384,256]{2,1,0:T(8,128)(2,1)} %copy-done.3, bf16[2,384,256]{2,1,0:T(8,128)(2,1)} %copy-done.4, ...), custom_call_target="tpu_custom_call" | custom-call | flops 805306368 | bytes 3145728 | tf_op jit(solution)/shard_map/attend/pallas_call | solution.py:418
  34.1 4.8 %attend.5.attn_ref = bf16[128,1024]{1,0:T(8,128)(2,1)} custom-call(s32[4]{0:T(128)} %pad_add_fusion.refs_0_, bf16[128,1024]{1,0:T(8,128)(2,1)} %refs_1_.2, bf16[2,384,256]{2,1,0:T(8,128)(2,1)} %collective-permute-done.1.refs_2_.refs_4_, bf16[2,384,256]{2,1,0:T(8,128)(2,1)} %collective-permute-done.2.refs_3_.refs_5_, ...), custom_call_target="tpu_custom_call" | custom-call | flops 402653184 | bytes 1572864 | tf_op jit(solution)/shard_map/attend/pallas_call | solution.py:418
  38.9 0.9 copy-done
  39.8 5.1 %project.1 = (f32[32,4096]{1,0:T(8,128)S(1)}, bf16[32,4096]{1,0:T(8,128)(2,1)S(1)}, f32[32,4096]{1,0:T(8,128)S(1)}, bf16[32,4096]{1,0:T(8,128)(2,1)S(1)}) custom-call(s32[1]{0:T(128)} %bitcast.place, bf16[128,1024]{1,0:T(8,128)(2,1)S(1)} %copy-done, bf16[1024,4096]{1,0:T(8,128)(2,1)} %proj_ref.1, bf16[32,4096]{1,0:T(8,128)(2,1)S(1)} %copy-done.1), custom_call_target="tpu_custom_call" | custom-call | flops 1073741824 | bytes 8388608 | tf_op jit(solution)/shard_map/project/pallas_call | solution.py:219
  44.9 2.1 collective-permute-start.8
  47.0 2.5 collective-permute-start.12
  49.8 1.7 collective-permute-start.10
  51.8 2.4 collective-permute-done.8
  54.2 7.6 %collective-permute-start.9 = (bf16[32,4096]{1,0:T(8,128)(2,1)S(1)}, bf16[32,4096]{1,0:T(8,128)(2,1)S(1)}, u32[]{:S(2)}, u32[]{:S(2)}) collective-permute-start(bf16[32,4096]{1,0:T(8,128)(2,1)S(1)} %add_convert_fusion.17), channel_id=1, source_target_pairs={{0,2},{1,3},{2,0},{3,1},{4,6},{5,7},{6,4},{7,5},{8,10},{9,11},{10,... | collective-permute-start | bytes 786440 | tf_op jit(solution)/shard_map/ppermute | solution.py:23
  61.8 0.7 collective-permute-done.12
  62.5 12.0 %collective-permute-done.11 = bf16[32,4224]{1,0:T(8,128)(2,1)S(1)} collective-permute-done((bf16[32,4224]{1,0:T(8,128)(2,1)S(1)}, bf16[32,4224]{1,0:T(8,128)(2,1)S(1)}, u32[]{:S(2)}, u32[]{:S(2)}) %collective-permute-start.11) | collective-permute-done | bytes 270368 | tf_op jit(solution)/shard_map/ppermute | solution.py:23
  74.6 1.6 collective-permute-start.14
  76.1 5.8 %collective-permute-done.7 = bf16[32,4096]{1,0:T(8,128)(2,1)S(1)} collective-permute-done((bf16[32,4096]{1,0:T(8,128)(2,1)S(1)}, bf16[32,4096]{1,0:T(8,128)(2,1)S(1)}, u32[]{:S(2)}, u32[]{:S(2)}) %collective-permute-start.7) | collective-permute-done | bytes 262176 | tf_op jit(solution)/shard_map/ppermute | solution.py:23
  81.9 2.9 %collective-permute-done.9 = bf16[32,4096]{1,0:T(8,128)(2,1)S(1)} collective-permute-done((bf16[32,4096]{1,0:T(8,128)(2,1)S(1)}, bf16[32,4096]{1,0:T(8,128)(2,1)S(1)}, u32[]{:S(2)}, u32[]{:S(2)}) %collective-permute-start.9) | collective-permute-done | bytes 262176 | tf_op jit(solution)/shard_map/ppermute | solution.py:23
  85.6 4.2 %collective-permute-done.14.refs_2_ = bf16[128,4224]{1,0:T(8,128)(2,1)S(1)} collective-permute-done((bf16[128,4224]{1,0:T(8,128)(2,1)S(1)}, bf16[128,4224]{1,0:T(8,128)(2,1)S(1)}, u32[]{:S(2)}, u32[]{:S(2)}) %collective-permute-start.14) | collective-permute-done | bytes 1081376 | tf_op jit(solution)/shard_map/ppermute | solution.py:35
  89.8 1.5 collective-permute-start.16
  91.3 1.5 collective-permute-start.15
  93.0 0.6 collective-permute-start.22
  93.6 13.9 %collective-permute-done.36 = bf16[32,4096]{1,0:T(8,128)(2,1)S(1)} collective-permute-done((bf16[32,4096]{1,0:T(8,128)(2,1)S(1)}, bf16[32,4096]{1,0:T(8,128)(2,1)S(1)}, u32[]{:S(2)}, u32[]{:S(2)}) %collective-permute-start.36) | collective-permute-done | bytes 262176 | tf_op jit(solution)/shard_map/ppermute | solution.py:23
  107.5 7.9 %collective-permute-done.37 = bf16[32,4096]{1,0:T(8,128)(2,1)S(1)} collective-permute-done((bf16[32,4096]{1,0:T(8,128)(2,1)S(1)}, bf16[32,4096]{1,0:T(8,128)(2,1)S(1)}, u32[]{:S(2)}, u32[]{:S(2)}) %collective-permute-start.37) | collective-permute-done | bytes 262176 | tf_op jit(solution)/shard_map/ppermute | solution.py:23
  115.5 0.6 collective-permute-start.39
  116.3 5.4 %collective-permute-done.22.refs_10_ = bf16[64,4096]{1,0:T(8,128)(2,1)S(1)} collective-permute-done((bf16[64,4096]{1,0:T(8,128)(2,1)S(1)}, bf16[64,4096]{1,0:T(8,128)(2,1)S(1)}, u32[]{:S(2)}, u32[]{:S(2)}) %collective-permute-start.22) | collective-permute-done | bytes 524320 | tf_op jit(solution)/shard_map/ppermute | solution.py:35
  122.8 4.5 %collective-permute-done.39.refs_10_ = bf16[64,4096]{1,0:T(8,128)(2,1)S(1)} collective-permute-done((bf16[64,4096]{1,0:T(8,128)(2,1)S(1)}, bf16[64,4096]{1,0:T(8,128)(2,1)S(1)}, u32[]{:S(2)}, u32[]{:S(2)}) %collective-permute-start.39) | collective-permute-done | bytes 524320 | tf_op jit(solution)/shard_map/ppermute | solution.py:35
  127.3 1.5 collective-permute-start.24
  128.8 1.5 collective-permute-start.23
  130.8 10.9 %collective-permute-done.24.refs_12_ = bf16[64,4096]{1,0:T(8,128)(2,1)S(1)} collective-permute-done((bf16[64,4096]{1,0:T(8,128)(2,1)S(1)}, bf16[64,4096]{1,0:T(8,128)(2,1)S(1)}, u32[]{:S(2)}, u32[]{:S(2)}) %collective-permute-start.24) | collective-permute-done | bytes 524320 | tf_op jit(solution)/shard_map/ppermute | solution.py:35
  141.7 1.4 collective-permute-start.40
  143.6 9.1 %collective-permute-done.41.refs_12_ = bf16[64,4096]{1,0:T(8,128)(2,1)S(1)} collective-permute-done((bf16[64,4096]{1,0:T(8,128)(2,1)S(1)}, bf16[64,4096]{1,0:T(8,128)(2,1)S(1)}, u32[]{:S(2)}, u32[]{:S(2)}) %collective-permute-start.41) | collective-permute-done | bytes 524320 | tf_op jit(solution)/shard_map/ppermute | solution.py:35
  153.8 0.9 collective-permute-done.26.refs_14_
  154.7 14.0 %rise.2 = (bf16[512,1024]{1,0:T(8,128)(2,1)S(1)}, bf16[1024,512]{1,0:T(8,128)(2,1)S(1)}) custom-call(s32[1]{0:T(128)} %bitcast.place, bf16[4096,128]{1,0:T(8,128)(2,1)S(1)} %pad.8.router_ref, bf16[128,4224]{1,0:T(8,128)(2,1)S(1)} %pad_maximum_fusion.refs_0_, bf16[128,4224]{1,0:T(8,128)(2,1)S(1)} %collective-permute-done.13.refs_1_, ...), custom_call_target="tpu_custom_call" | custom-call | flops 8589934592 | bytes 20971520 | tf_op jit(solution)/shard_map/rise/pallas_call | solution.py:134
  168.7 7.3 %fall.2 = (bf16[64,4096]{1,0:T(8,128)(2,1)S(1)}, bf16[64,4096]{1,0:T(8,128)(2,1)S(1)}, bf16[64,4096]{1,0:T(8,128)(2,1)S(1)}, bf16[64,4096]{1,0:T(8,128)(2,1)S(1)...) custom-call(bf16[512,1024]{1,0:T(8,128)(2,1)S(1)} %get-tuple-element, ...), custom_call_target="tpu_custom_call" | custom-call | flops 4294967296 | bytes 12582912 | tf_op jit(solution)/shard_map/fall/pallas_call | solution.py:180
  176.7 14.2 %rise.3 = (bf16[512,1024]{1,0:T(8,128)(2,1)S(1)}, bf16[1024,512]{1,0:T(8,128)(2,1)S(1)}) custom-call(s32[1]{0:T(128)} %bitcast.place, bf16[4096,128]{1,0:T(8,128)(2,1)S(1)} %pad.8.router_ref, bf16[128,4224]{1,0:T(8,128)(2,1)S(1)} %pad_maximum_fusion.refs_0_, bf16[128,4224]{1,0:T(8,128)(2,1)S(1)} %collective-permute-done.13.refs_1_, ...), custom_call_target="tpu_custom_call" | custom-call | flops 8589934592 | bytes 20971520 | tf_op jit(solution)/shard_map/rise/pallas_call | solution.py:134
  190.9 7.3 %fall.3 = (bf16[64,4096]{1,0:T(8,128)(2,1)S(1)}, bf16[64,4096]{1,0:T(8,128)(2,1)S(1)}, bf16[64,4096]{1,0:T(8,128)(2,1)S(1)}, bf16[64,4096]{1,0:T(8,128)(2,1)S(1)...) custom-call(bf16[512,1024]{1,0:T(8,128)(2,1)S(1)} %get-tuple-element, ...), custom_call_target="tpu_custom_call" | custom-call | flops 4294967296 | bytes 12582912 | tf_op jit(solution)/shard_map/fall/pallas_call | solution.py:180
  198.8 7.6 %outer.2.refs_10_ = f32[1024,4096]{1,0:T(8,128)} custom-call(bf16[128,4224]{1,0:T(8,128)(2,1)S(1)} %pad_maximum_fusion.refs_0_, bf16[128,4224]{1,0:T(8,128)(2,1)S(1)} %collective-permute-done.13.refs_1_, bf16[128,4224]{1,0:T(8,128)(2,1)S(1)} %collective-permute-done.14.refs_2_, bf16[128,4224]{1,0:T(8,128)(2,1)S(1)} %collective-permute-done.15.refs_3_, ...), custom_call_target="tpu_custom_call" | custom-call | flops 4294967296 | bytes 16777216 | tf_op jit(solution)/shard_map/outer/pallas_call | solution.py:276
  206.8 1.0 collective-permute-start.29
  208.0 1.4 collective-permute-start.33
  209.5 1.1 collective-permute-start.46
  210.8 10.5 %collective-permute-done.29 = bf16[64,4096]{1,0:T(8,128)(2,1)S(1)} collective-permute-done((bf16[64,4096]{1,0:T(8,128)(2,1)S(1)}, bf16[64,4096]{1,0:T(8,128)(2,1)S(1)}, u32[]{:S(2)}, u32[]{:S(2)}) %collective-permute-start.29) | collective-permute-done | bytes 524320 | tf_op jit(solution)/shard_map/ppermute | solution.py:35
  221.3 1.5 collective-permute-start.50
  223.0 9.6 %collective-permute-done.46 = bf16[64,4096]{1,0:T(8,128)(2,1)S(1)} collective-permute-done((bf16[64,4096]{1,0:T(8,128)(2,1)S(1)}, bf16[64,4096]{1,0:T(8,128)(2,1)S(1)}, u32[]{:S(2)}, u32[]{:S(2)}) %collective-permute-start.46) | collective-permute-done | bytes 524320 | tf_op jit(solution)/shard_map/ppermute | solution.py:35
  233.5 1.1 collective-permute-start.51
  234.7 1.1 collective-permute-start.34
  235.8 6.9 %collective-permute-done.51 = bf16[64,4096]{1,0:T(8,128)(2,1)S(1)} collective-permute-done((bf16[64,4096]{1,0:T(8,128)(2,1)S(1)}, bf16[64,4096]{1,0:T(8,128)(2,1)S(1)}, u32[]{:S(2)}, u32[]{:S(2)}) %collective-permute-start.51) | collective-permute-done | bytes 524320 | tf_op jit(solution)/shard_map/ppermute | solution.py:35
  243.0 5.3 %collective-permute-done.34 = bf16[64,4096]{1,0:T(8,128)(2,1)S(1)} collective-permute-done((bf16[64,4096]{1,0:T(8,128)(2,1)S(1)}, bf16[64,4096]{1,0:T(8,128)(2,1)S(1)}, u32[]{:S(2)}, u32[]{:S(2)}) %collective-permute-start.34) | collective-permute-done | bytes 524320 | tf_op jit(solution)/shard_map/ppermute | solution.py:35
  248.7 1.7 collective-permute-done.52
  250.5 1.8 collective-permute-start.53
  252.3 7.6 %outer.3 = f32[1024,4096]{1,0:T(8,128)} custom-call(bf16[128,4224]{1,0:T(8,128)(2,1)S(1)} %pad_maximum_fusion.refs_0_, bf16[128,4224]{1,0:T(8,128)(2,1)S(1)} %collective-permute-done.13.refs_1_, bf16[128,4224]{1,0:T(8,128)(2,1)S(1)} %collective-permute-done.14.refs_2_, ...), custom_call_target="tpu_custom_call", output_to_operand_aliasing={{}: (10, {})} | custom-call | flops 4294967296 | bytes 16777216 | tf_op jit(solution)/shard_map/outer/pallas_call | solution.py:276
  259.8 1.1 collective-permute-done.35
  260.9 2.7 %collective-permute-done.53 = bf16[32,4096]{1,0:T(8,128)(2,1)S(1)} collective-permute-done((bf16[32,4096]{1,0:T(8,128)(2,1)S(1)}, bf16[32,4096]{1,0:T(8,128)(2,1)S(1)}, u32[]{:S(2)}, u32[]{:S(2)}) %collective-permute-start.53) | collective-permute-done | bytes 262176 | tf_op jit(solution)/shard_map/ppermute | solution.py:23
  263.6 0.9 add_convert_fusion.14
  (103 shorter events, 10.0 us)
Async XLA Ops:
  2.5 21.4 %copy-start.2 = (bf16[2,384,256]{2,1,0:T(8,128)(2,1)}, bf16[2,384,256]{2,1,0:T(8,128)(2,1)S(1)}, u32[]{:S(2)}) copy-start(bf16[2,384,256]{2,1,0:T(8,128)(2,1)S(1)} %constant_dynamic-update-slice_fusion.refs_2_.refs_4_) | copy-start | bytes 1179652
  2.5 3.1 %collective-permute-start.3 = (bf16[2,384,256]{2,1,0:T(8,128)(2,1)S(1)}, bf16[2,384,256]{2,1,0:T(8,128)(2,1)S(1)}, u32[]{:S(2)}, u32[]{:S(2)}) collective-permute-start(bf16[2,384,256]{2,1,0:T(8,128)(2,1)S(1)} %constant_dynamic-update-slice_fusion.refs_2_.refs_4_), channel_id=1, source_target_pairs={{0,4},{4,0},{8,12},{12,8},{16,20},{20,16},{24,28},{28,24},{1,5},{5... | collective-permute-start | bytes 1179656 | tf_op jit(solution)/shard_map/ppermute | solution.py:19
  3.1 8.3 %collective-permute-start = (bf16[2,384,256]{2,1,0:T(8,128)(2,1)S(1)}, bf16[2,384,256]{2,1,0:T(8,128)(2,1)S(1)}, u32[]{:S(2)}, u32[]{:S(2)}) collective-permute-start(bf16[2,384,256]{2,1,0:T(8,128)(2,1)S(1)} %constant_dynamic-update-slice_fusion.refs_2_.refs_4_), channel_id=1, source_target_pairs={{0,8},{4,20},{8,0},{12,28},{16,24},{20,4},{24,16},{28,12},{1,9},{5... | collective-permute-start | bytes 1179656 | tf_op jit(solution)/shard_map/ppermute | solution.py:35
  5.6 14.1 %copy-start.5 = (bf16[2,384,256]{2,1,0:T(8,128)(2,1)}, bf16[2,384,256]{2,1,0:T(8,128)(2,1)S(1)}, u32[]{:S(2)}) copy-start(bf16[2,384,256]{2,1,0:T(8,128)(2,1)S(1)} %collective-permute-done.3.refs_3_.refs_5_) | copy-start | bytes 1179652
  5.6 11.7 %collective-permute-start.4 = (bf16[2,384,256]{2,1,0:T(8,128)(2,1)S(1)}, bf16[2,384,256]{2,1,0:T(8,128)(2,1)S(1)}, u32[]{:S(2)}, u32[]{:S(2)}) collective-permute-start(bf16[2,384,256]{2,1,0:T(8,128)(2,1)S(1)} %collective-permute-done.3.refs_3_.refs_5_), channel_id=1, source_target_pairs={{0,8},{4,20},{8,0},{12,28},{16,24},{20,4},{24,16},{28,12},{1,9},{5... | collective-permute-start | bytes 1179656 | tf_op jit(solution)/shard_map/ppermute | solution.py:35
  11.4 16.7 %copy-start.3 = (bf16[2,384,256]{2,1,0:T(8,128)(2,1)}, bf16[2,384,256]{2,1,0:T(8,128)(2,1)S(1)}, u32[]{:S(2)}) copy-start(bf16[2,384,256]{2,1,0:T(8,128)(2,1)S(1)} %collective-permute-done.refs_2_.refs_6_) | copy-start | bytes 1179652
  11.4 8.3 %collective-permute-start.1 = (bf16[2,384,256]{2,1,0:T(8,128)(2,1)S(1)}, bf16[2,384,256]{2,1,0:T(8,128)(2,1)}, u32[]{:S(2)}, u32[]{:S(2)}) collective-permute-start(bf16[2,384,256]{2,1,0:T(8,128)(2,1)S(1)} %collective-permute-done.refs_2_.refs_6_), channel_id=1, source_target_pairs={{0,16},{4,12},{8,24},{12,4},{16,0},{20,28},{24,8},{28,20},{1,17},{... | collective-permute-start | bytes 1179656 | tf_op jit(solution)/shard_map/ppermute | solution.py:35
  13.4 14.7 %collective-permute-start.5 = (bf16[2,384,256]{2,1,0:T(8,128)(2,1)S(1)}, bf16[2,384,256]{2,1,0:T(8,128)(2,1)}, u32[]{:S(2)}, u32[]{:S(2)}) collective-permute-start(bf16[2,384,256]{2,1,0:T(8,128)(2,1)S(1)} %collective-permute-done.refs_2_.refs_6_), channel_id=1, source_target_pairs={{0,4},{4,0},{8,12},{12,8},{16,20},{20,16},{24,28},{28,24},{1,5},{5... | collective-permute-start | bytes 1179656 | tf_op jit(solution)/shard_map/ppermute | solution.py:19
  17.3 10.8 %copy-start.4 = (bf16[2,384,256]{2,1,0:T(8,128)(2,1)}, bf16[2,384,256]{2,1,0:T(8,128)(2,1)S(1)}, u32[]{:S(2)}) copy-start(bf16[2,384,256]{2,1,0:T(8,128)(2,1)S(1)} %collective-permute-done.4.refs_3_.refs_7_) | copy-start | bytes 1179652
  17.3 10.8 %collective-permute-start.6 = (bf16[2,384,256]{2,1,0:T(8,128)(2,1)S(1)}, bf16[2,384,256]{2,1,0:T(8,128)(2,1)}, u32[]{:S(2)}, u32[]{:S(2)}) collective-permute-start(bf16[2,384,256]{2,1,0:T(8,128)(2,1)S(1)} %collective-permute-done.4.refs_3_.refs_7_), channel_id=1, source_target_pairs={{0,4},{4,0},{8,12},{12,8},{16,20},{20,16},{24,28},{28,24},{1,5},{5... | collective-permute-start | bytes 1179656 | tf_op jit(solution)/shard_map/ppermute | solution.py:19
  19.7 14.4 %collective-permute-start.2 = (bf16[2,384,256]{2,1,0:T(8,128)(2,1)}, bf16[2,384,256]{2,1,0:T(8,128)(2,1)}, u32[]{:S(2)}, u32[]{:S(2)}) collective-permute-start(bf16[2,384,256]{2,1,0:T(8,128)(2,1)} %collective-permute-done.1.refs_2_.refs_4_), channel_id=1, source_target_pairs={{0,4},{4,0},{8,12},{12,8},{16,20},{20,16},{24,28},{28,24},{1,5},{5... | collective-permute-start | bytes 1179656 | tf_op jit(solution)/shard_map/ppermute | solution.py:19
  34.0 4.8 %copy-start.1 = (bf16[32,4096]{1,0:T(8,128)(2,1)S(1)}, bf16[32,4096]{1,0:T(8,128)(2,1)}, u32[]{:S(2)}) copy-start(bf16[32,4096]{1,0:T(8,128)(2,1)} %residual_ref.1) | copy-start | bytes 786436
  38.8 1.0 copy-start
  39.8 7.2 %copy-start.6 = (bf16[32,4096]{1,0:T(8,128)(2,1)S(1)}, bf16[32,4096]{1,0:T(8,128)(2,1)}, u32[]{:S(2)}) copy-start(bf16[32,4096]{1,0:T(8,128)(2,1)} %param.23) | copy-start | bytes 786436
  44.9 9.3 %collective-permute-start.8 = (bf16[32,4096]{1,0:T(8,128)(2,1)S(1)}, bf16[32,4096]{1,0:T(8,128)(2,1)S(1)}, u32[]{:S(2)}, u32[]{:S(2)}) collective-permute-start(bf16[32,4096]{1,0:T(8,128)(2,1)S(1)} %get-tuple-element.44), channel_id=1, source_target_pairs={{0,1},{1,0},{2,3},{3,2},{4,5},{5,4},{6,7},{7,6},{8,9},{9,8},{10,11... | collective-permute-start | bytes 786440 | tf_op jit(solution)/shard_map/ppermute | solution.py:23
  47.0 38.1 %copy-start.7 = (f32[4096]{0:T(1024)S(1)}, f32[4096]{0:T(1024)}, u32[]{:S(2)}) copy-start(f32[4096]{0:T(1024)} %param.17) | copy-start | bytes 49156
  47.0 15.5 %collective-permute-start.12 = (bf16[32,4224]{1,0:T(8,128)(2,1)S(1)}, bf16[32,4224]{1,0:T(8,128)(2,1)S(1)}, u32[]{:S(2)}, u32[]{:S(2)}) collective-permute-start(bf16[32,4224]{1,0:T(8,128)(2,1)S(1)} %pad_maximum_fusion.2), channel_id=1, source_target_pairs={{0,3},{1,2},{2,1},{3,0},{4,7},{5,6},{6,5},{7,4},{8,11},{9,10},{10,... | collective-permute-start | bytes 811016 | tf_op jit(solution)/shard_map/ppermute | solution.py:23
  49.6 24.9 %collective-permute-start.11 = (bf16[32,4224]{1,0:T(8,128)(2,1)S(1)}, bf16[32,4224]{1,0:T(8,128)(2,1)S(1)}, u32[]{:S(2)}, u32[]{:S(2)}) collective-permute-start(bf16[32,4224]{1,0:T(8,128)(2,1)S(1)} %pad_maximum_fusion.2), channel_id=1, source_target_pairs={{0,2},{1,3},{2,0},{3,1},{4,6},{5,7},{6,4},{7,5},{8,10},{9,11},{10,... | collective-permute-start | bytes 811016 | tf_op jit(solution)/shard_map/ppermute | solution.py:23
  49.8 24.7 %collective-permute-start.10 = (bf16[32,4224]{1,0:T(8,128)(2,1)S(1)}, bf16[32,4224]{1,0:T(8,128)(2,1)S(1)}, u32[]{:S(2)}, u32[]{:S(2)}) collective-permute-start(bf16[32,4224]{1,0:T(8,128)(2,1)S(1)} %pad_maximum_fusion.2), channel_id=1, source_target_pairs={{0,1},{1,0},{2,3},{3,2},{4,5},{5,4},{6,7},{7,6},{8,9},{9,8},{10,11... | collective-permute-start | bytes 811016 | tf_op jit(solution)/shard_map/ppermute | solution.py:23
  51.5 30.4 %collective-permute-start.7 = (bf16[32,4096]{1,0:T(8,128)(2,1)S(1)}, bf16[32,4096]{1,0:T(8,128)(2,1)S(1)}, u32[]{:S(2)}, u32[]{:S(2)}) collective-permute-start(bf16[32,4096]{1,0:T(8,128)(2,1)S(1)} %get-tuple-element.42), channel_id=1, source_target_pairs={{0,1},{1,0},{2,3},{3,2},{4,5},{5,4},{6,7},{7,6},{8,9},{9,8},{10,11... | collective-permute-start | bytes 786440 | tf_op jit(solution)/shard_map/ppermute | solution.py:23
  54.2 30.7 %collective-permute-start.9 = (bf16[32,4096]{1,0:T(8,128)(2,1)S(1)}, bf16[32,4096]{1,0:T(8,128)(2,1)S(1)}, u32[]{:S(2)}, u32[]{:S(2)}) collective-permute-start(bf16[32,4096]{1,0:T(8,128)(2,1)S(1)} %add_convert_fusion.17), channel_id=1, source_target_pairs={{0,2},{1,3},{2,0},{3,1},{4,6},{5,7},{6,4},{7,5},{8,10},{9,11},{10,... | collective-permute-start | bytes 786440 | tf_op jit(solution)/shard_map/ppermute | solution.py:23
  74.6 15.2 %collective-permute-start.14 = (bf16[128,4224]{1,0:T(8,128)(2,1)S(1)}, bf16[128,4224]{1,0:T(8,128)(2,1)S(1)}, u32[]{:S(2)}, u32[]{:S(2)}) collective-permute-start(bf16[128,4224]{1,0:T(8,128)(2,1)S(1)} %pad_maximum_fusion.refs_0_), channel_id=1, source_target_pairs={{0,8},{4,20},{8,0},{12,28},{16,24},{20,4},{24,16},{28,12},{1,9},{5... | collective-permute-start | bytes 3244040 | tf_op jit(solution)/shard_map/ppermute | solution.py:35
  76.1 15.2 %collective-permute-start.13 = (bf16[128,4224]{1,0:T(8,128)(2,1)S(1)}, bf16[128,4224]{1,0:T(8,128)(2,1)S(1)}, u32[]{:S(2)}, u32[]{:S(2)}) collective-permute-start(bf16[128,4224]{1,0:T(8,128)(2,1)S(1)} %pad_maximum_fusion.refs_0_), channel_id=1, source_target_pairs={{0,4},{4,0},{8,12},{12,8},{16,20},{20,16},{24,28},{28,24},{1,5},{5... | collective-permute-start | bytes 3244040 | tf_op jit(solution)/shard_map/ppermute | solution.py:19
  85.2 7.7 %collective-permute-start.20 = (bf16[32,4096]{1,0:T(8,128)(2,1)S(1)}, bf16[32,4096]{1,0:T(8,128)(2,1)S(1)}, u32[]{:S(2)}, u32[]{:S(2)}) collective-permute-start(bf16[32,4096]{1,0:T(8,128)(2,1)S(1)} %multiply_convert_fusion), channel_id=1, source_target_pairs={{0,1},{1,0},{2,3},{3,2},{4,5},{5,4},{6,7},{7,6},{8,9},{9,8},{10,11... | collective-permute-start | bytes 786440 | tf_op jit(solution)/shard_map/ppermute | solution.py:23
  89.8 25.7 %collective-permute-start.17 = (bf16[128,4224]{1,0:T(8,128)(2,1)S(1)}, bf16[128,4224]{1,0:T(8,128)(2,1)S(1)}, u32[]{:S(2)}, u32[]{:S(2)}) collective-permute-start(bf16[128,4224]{1,0:T(8,128)(2,1)S(1)} %collective-permute-done.14.refs_2_), channel_id=1, source_target_pairs={{0,4},{4,0},{8,12},{12,8},{16,20},{20,16},{24,28},{28,24},{1,5},{5... | collective-permute-start | bytes 3244040 | tf_op jit(solution)/shard_map/ppermute | solution.py:19
  89.8 26.3 %collective-permute-start.16 = (bf16[128,4224]{1,0:T(8,128)(2,1)S(1)}, bf16[128,4224]{1,0:T(8,128)(2,1)S(1)}, u32[]{:S(2)}, u32[]{:S(2)}) collective-permute-start(bf16[128,4224]{1,0:T(8,128)(2,1)S(1)} %collective-permute-done.14.refs_2_), channel_id=1, source_target_pairs={{0,16},{4,12},{8,24},{12,4},{16,0},{20,28},{24,8},{28,20},{1,17},{... | collective-permute-start | bytes 3244040 | tf_op jit(solution)/shard_map/ppermute | solution.py:35
  91.3 31.0 %collective-permute-start.15 = (bf16[128,4224]{1,0:T(8,128)(2,1)S(1)}, bf16[128,4224]{1,0:T(8,128)(2,1)S(1)}, u32[]{:S(2)}, u32[]{:S(2)}) collective-permute-start(bf16[128,4224]{1,0:T(8,128)(2,1)S(1)} %collective-permute-done.13.refs_1_), channel_id=1, source_target_pairs={{0,8},{4,20},{8,0},{12,28},{16,24},{20,4},{24,16},{28,12},{1,9},{5... | collective-permute-start | bytes 3244040 | tf_op jit(solution)/shard_map/ppermute | solution.py:35
  92.8 14.7 %collective-permute-start.36 = (bf16[32,4096]{1,0:T(8,128)(2,1)S(1)}, bf16[32,4096]{1,0:T(8,128)(2,1)S(1)}, u32[]{:S(2)}, u32[]{:S(2)}) collective-permute-start(bf16[32,4096]{1,0:T(8,128)(2,1)S(1)} %multiply_convert_fusion), channel_id=1, source_target_pairs={{0,2},{1,3},{2,0},{3,1},{4,6},{5,7},{6,4},{7,5},{8,10},{9,11},{10,... | collective-permute-start | bytes 786440 | tf_op jit(solution)/shard_map/ppermute | solution.py:23
  93.0 28.7 %collective-permute-start.22 = (bf16[64,4096]{1,0:T(8,128)(2,1)S(1)}, bf16[64,4096]{1,0:T(8,128)(2,1)S(1)}, u32[]{:S(2)}, u32[]{:S(2)}) collective-permute-start(bf16[64,4096]{1,0:T(8,128)(2,1)S(1)} %pad_maximum_fusion.1.refs_8_), channel_id=1, source_target_pairs={{0,8},{4,20},{8,0},{12,28},{16,24},{20,4},{24,16},{28,12},{1,9},{5... | collective-permute-start | bytes 1572872 | tf_op jit(solution)/shard_map/ppermute | solution.py:35
  107.5 7.9 %collective-permute-start.37 = (bf16[32,4096]{1,0:T(8,128)(2,1)S(1)}, bf16[32,4096]{1,0:T(8,128)(2,1)S(1)}, u32[]{:S(2)}, u32[]{:S(2)}) collective-permute-start(bf16[32,4096]{1,0:T(8,128)(2,1)S(1)} %collective-permute-done.36), channel_id=1, source_target_pairs={{0,1},{1,0},{2,3},{3,2},{4,5},{5,4},{6,7},{7,6},{8,9},{9,8},{10,11... | collective-permute-start | bytes 786440 | tf_op jit(solution)/shard_map/ppermute | solution.py:23
  115.4 6.8 %collective-permute-start.21 = (bf16[64,4096]{1,0:T(8,128)(2,1)S(1)}, bf16[64,4096]{1,0:T(8,128)(2,1)S(1)}, u32[]{:S(2)}, u32[]{:S(2)}) collective-permute-start(bf16[64,4096]{1,0:T(8,128)(2,1)S(1)} %pad_maximum_fusion.1.refs_8_), channel_id=1, source_target_pairs={{0,4},{4,0},{8,12},{12,8},{16,20},{20,16},{24,28},{28,24},{1,5},{5... | collective-permute-start | bytes 1572872 | tf_op jit(solution)/shard_map/ppermute | solution.py:19
  115.5 11.8 %collective-permute-start.39 = (bf16[64,4096]{1,0:T(8,128)(2,1)S(1)}, bf16[64,4096]{1,0:T(8,128)(2,1)S(1)}, u32[]{:S(2)}, u32[]{:S(2)}) collective-permute-start(bf16[64,4096]{1,0:T(8,128)(2,1)S(1)} %constant_dynamic-update-slice_fusion.2.refs_8_), channel_id=1, source_target_pairs={{0,8},{4,20},{8,0},{12,28},{16,24},{20,4},{24,16},{28,12},{1,9},{5... | collective-permute-start | bytes 1572872 | tf_op jit(solution)/shard_map/ppermute | solution.py:35
  116.1 12.8 %collective-permute-start.38 = (bf16[64,4096]{1,0:T(8,128)(2,1)S(1)}, bf16[64,4096]{1,0:T(8,128)(2,1)S(1)}, u32[]{:S(2)}, u32[]{:S(2)}) collective-permute-start(bf16[64,4096]{1,0:T(8,128)(2,1)S(1)} %constant_dynamic-update-slice_fusion.2.refs_8_), channel_id=1, source_target_pairs={{0,4},{4,0},{8,12},{12,8},{16,20},{20,16},{24,28},{28,24},{1,5},{5... | collective-permute-start | bytes 1572872 | tf_op jit(solution)/shard_map/ppermute | solution.py:19
  121.7 8.6 %collective-permute-start.25 = (bf16[64,4096]{1,0:T(8,128)(2,1)S(1)}, bf16[64,4096]{1,0:T(8,128)(2,1)S(1)}, u32[]{:S(2)}, u32[]{:S(2)}) collective-permute-start(bf16[64,4096]{1,0:T(8,128)(2,1)S(1)} %collective-permute-done.22.refs_10_), channel_id=1, source_target_pairs={{0,4},{4,0},{8,12},{12,8},{16,20},{20,16},{24,28},{28,24},{1,5},{5... | collective-permute-start | bytes 1572872 | tf_op jit(solution)/shard_map/ppermute | solution.py:19
  122.3 31.0 %collective-permute-start.19 = (bf16[128,4224]{1,0:T(8,128)(2,1)S(1)}, bf16[128,4224]{1,0:T(8,128)(2,1)S(1)}, u32[]{:S(2)}, u32[]{:S(2)}) collective-permute-start(bf16[128,4224]{1,0:T(8,128)(2,1)S(1)} %collective-permute-done.16.refs_4_), channel_id=1, source_target_pairs={{0,4},{4,0},{8,12},{12,8},{16,20},{20,16},{24,28},{28,24},{1,5},{5... | collective-permute-start | bytes 3244040 | tf_op jit(solution)/shard_map/ppermute | solution.py:19
  122.3 31.1 %collective-permute-start.18 = (bf16[128,4224]{1,0:T(8,128)(2,1)S(1)}, bf16[128,4224]{1,0:T(8,128)(2,1)S(1)}, u32[]{:S(2)}, u32[]{:S(2)}) collective-permute-start(bf16[128,4224]{1,0:T(8,128)(2,1)S(1)} %collective-permute-done.15.refs_3_), channel_id=1, source_target_pairs={{0,4},{4,0},{8,12},{12,8},{16,20},{20,16},{24,28},{28,24},{1,5},{5... | collective-permute-start | bytes 3244040 | tf_op jit(solution)/shard_map/ppermute | solution.py:19
  127.3 14.4 %collective-permute-start.24 = (bf16[64,4096]{1,0:T(8,128)(2,1)S(1)}, bf16[64,4096]{1,0:T(8,128)(2,1)S(1)}, u32[]{:S(2)}, u32[]{:S(2)}) collective-permute-start(bf16[64,4096]{1,0:T(8,128)(2,1)S(1)} %collective-permute-done.22.refs_10_), channel_id=1, source_target_pairs={{0,16},{4,12},{8,24},{12,4},{16,0},{20,28},{24,8},{28,20},{1,17},{... | collective-permute-start | bytes 1572872 | tf_op jit(solution)/shard_map/ppermute | solution.py:35
  128.8 14.8 %collective-permute-start.23 = (bf16[64,4096]{1,0:T(8,128)(2,1)S(1)}, bf16[64,4096]{1,0:T(8,128)(2,1)S(1)}, u32[]{:S(2)}, u32[]{:S(2)}) collective-permute-start(bf16[64,4096]{1,0:T(8,128)(2,1)S(1)} %collective-permute-done.21.refs_9_), channel_id=1, source_target_pairs={{0,8},{4,20},{8,0},{12,28},{16,24},{20,4},{24,16},{28,12},{1,9},{5... | collective-permute-start | bytes 1572872 | tf_op jit(solution)/shard_map/ppermute | solution.py:35
  130.3 22.4 %collective-permute-start.41 = (bf16[64,4096]{1,0:T(8,128)(2,1)S(1)}, bf16[64,4096]{1,0:T(8,128)(2,1)S(1)}, u32[]{:S(2)}, u32[]{:S(2)}) collective-permute-start(bf16[64,4096]{1,0:T(8,128)(2,1)S(1)} %collective-permute-done.39.refs_10_), channel_id=1, source_target_pairs={{0,16},{4,12},{8,24},{12,4},{16,0},{20,28},{24,8},{28,20},{1,17},{... | collective-permute-start | bytes 1572872 | tf_op jit(solution)/shard_map/ppermute | solution.py:35
  141.7 11.0 %collective-permute-start.40 = (bf16[64,4096]{1,0:T(8,128)(2,1)S(1)}, bf16[64,4096]{1,0:T(8,128)(2,1)S(1)}, u32[]{:S(2)}, u32[]{:S(2)}) collective-permute-start(bf16[64,4096]{1,0:T(8,128)(2,1)S(1)} %collective-permute-done.38.refs_9_), channel_id=1, source_target_pairs={{0,8},{4,20},{8,0},{12,28},{16,24},{20,4},{24,16},{28,12},{1,9},{5... | collective-permute-start | bytes 1572872 | tf_op jit(solution)/shard_map/ppermute | solution.py:35
  143.6 10.2 %collective-permute-start.27 = (bf16[64,4096]{1,0:T(8,128)(2,1)S(1)}, bf16[64,4096]{1,0:T(8,128)(2,1)S(1)}, u32[]{:S(2)}, u32[]{:S(2)}) collective-permute-start(bf16[64,4096]{1,0:T(8,128)(2,1)S(1)} %collective-permute-done.24.refs_12_), channel_id=1, source_target_pairs={{0,4},{4,0},{8,12},{12,8},{16,20},{20,16},{24,28},{28,24},{1,5},{5... | collective-permute-start | bytes 1572872 | tf_op jit(solution)/shard_map/ppermute | solution.py:19
  152.7 1.9 collective-permute-start.26
  152.8 23.8 %collective-permute-start.42 = (bf16[64,4096]{1,0:T(8,128)(2,1)S(1)}, bf16[64,4096]{1,0:T(8,128)(2,1)S(1)}, u32[]{:S(2)}, u32[]{:S(2)}) collective-permute-start(bf16[64,4096]{1,0:T(8,128)(2,1)S(1)} %collective-permute-done.39.refs_10_), channel_id=1, source_target_pairs={{0,4},{4,0},{8,12},{12,8},{16,20},{20,16},{24,28},{28,24},{1,5},{5... | collective-permute-start | bytes 1572872 | tf_op jit(solution)/shard_map/ppermute | solution.py:19
  153.3 23.4 %collective-permute-start.44 = (bf16[64,4096]{1,0:T(8,128)(2,1)S(1)}, bf16[64,4096]{1,0:T(8,128)(2,1)S(1)}, u32[]{:S(2)}, u32[]{:S(2)}) collective-permute-start(bf16[64,4096]{1,0:T(8,128)(2,1)S(1)} %collective-permute-done.41.refs_12_), channel_id=1, source_target_pairs={{0,4},{4,0},{8,12},{12,8},{16,20},{20,16},{24,28},{28,24},{1,5},{5... | collective-permute-start | bytes 1572872 | tf_op jit(solution)/shard_map/ppermute | solution.py:19
  153.3 23.3 %collective-permute-start.43 = (bf16[64,4096]{1,0:T(8,128)(2,1)S(1)}, bf16[64,4096]{1,0:T(8,128)(2,1)S(1)}, u32[]{:S(2)}, u32[]{:S(2)}) collective-permute-start(bf16[64,4096]{1,0:T(8,128)(2,1)S(1)} %collective-permute-done.40.refs_11_), channel_id=1, source_target_pairs={{0,4},{4,0},{8,12},{12,8},{16,20},{20,16},{24,28},{28,24},{1,5},{5... | collective-permute-start | bytes 1572872 | tf_op jit(solution)/shard_map/ppermute | solution.py:19
  176.0 30.4 %collective-permute-start.28 = (bf16[64,4096]{1,0:T(8,128)(2,1)S(1)}, bf16[64,4096]{1,0:T(8,128)(2,1)S(1)}, u32[]{:S(2)}, u32[]{:S(2)}) collective-permute-start(bf16[64,4096]{1,0:T(8,128)(2,1)S(1)} %get-tuple-element.50), channel_id=1, source_target_pairs={{0,4},{4,0},{8,12},{12,8},{16,20},{20,16},{24,28},{28,24},{1,5},{5... | collective-permute-start | bytes 1572872 | tf_op jit(solution)/shard_map/ppermute | solution.py:19
  176.2 58.4 %collective-permute-start.31 = (bf16[64,4096]{1,0:T(8,128)(2,1)S(1)}, bf16[64,4096]{1,0:T(8,128)(2,1)S(1)}, u32[]{:S(2)}, u32[]{:S(2)}) collective-permute-start(bf16[64,4096]{1,0:T(8,128)(2,1)S(1)} %get-tuple-element.52), channel_id=1, source_target_pairs={{0,4},{4,0},{8,12},{12,8},{16,20},{20,16},{24,28},{28,24},{1,5},{5... | collective-permute-start | bytes 1572872 | tf_op jit(solution)/shard_map/ppermute | solution.py:19
  176.5 30.3 %collective-permute-start.32 = (bf16[64,4096]{1,0:T(8,128)(2,1)S(1)}, bf16[64,4096]{1,0:T(8,128)(2,1)S(1)}, u32[]{:S(2)}, u32[]{:S(2)}) collective-permute-start(bf16[64,4096]{1,0:T(8,128)(2,1)S(1)} %get-tuple-element.54), channel_id=1, source_target_pairs={{0,4},{4,0},{8,12},{12,8},{16,20},{20,16},{24,28},{28,24},{1,5},{5... | collective-permute-start | bytes 1572872 | tf_op jit(solution)/shard_map/ppermute | solution.py:19
  198.2 9.8 %collective-permute-start.45 = (bf16[64,4096]{1,0:T(8,128)(2,1)S(1)}, bf16[64,4096]{1,0:T(8,128)(2,1)S(1)}, u32[]{:S(2)}, u32[]{:S(2)}) collective-permute-start(bf16[64,4096]{1,0:T(8,128)(2,1)S(1)} %get-tuple-element.59), channel_id=1, source_target_pairs={{0,4},{4,0},{8,12},{12,8},{16,20},{20,16},{24,28},{28,24},{1,5},{5... | collective-permute-start | bytes 1572872 | tf_op jit(solution)/shard_map/ppermute | solution.py:19
  198.6 34.1 %collective-permute-start.48 = (bf16[64,4096]{1,0:T(8,128)(2,1)S(1)}, bf16[64,4096]{1,0:T(8,128)(2,1)S(1)}, u32[]{:S(2)}, u32[]{:S(2)}) collective-permute-start(bf16[64,4096]{1,0:T(8,128)(2,1)S(1)} %get-tuple-element.61), channel_id=1, source_target_pairs={{0,4},{4,0},{8,12},{12,8},{16,20},{20,16},{24,28},{28,24},{1,5},{5... | collective-permute-start | bytes 1572872 | tf_op jit(solution)/shard_map/ppermute | solution.py:19
  206.3 3.2 %collective-permute-start.49 = (bf16[64,4096]{1,0:T(8,128)(2,1)S(1)}, bf16[64,4096]{1,0:T(8,128)(2,1)S(1)}, u32[]{:S(2)}, u32[]{:S(2)}) collective-permute-start(bf16[64,4096]{1,0:T(8,128)(2,1)S(1)} %get-tuple-element.63), channel_id=1, source_target_pairs={{0,4},{4,0},{8,12},{12,8},{16,20},{20,16},{24,28},{28,24},{1,5},{5... | collective-permute-start | bytes 1572872 | tf_op jit(solution)/shard_map/ppermute | solution.py:19
  206.8 14.5 %collective-permute-start.29 = (bf16[64,4096]{1,0:T(8,128)(2,1)S(1)}, bf16[64,4096]{1,0:T(8,128)(2,1)S(1)}, u32[]{:S(2)}, u32[]{:S(2)}) collective-permute-start(bf16[64,4096]{1,0:T(8,128)(2,1)S(1)} %add_convert_fusion.13), channel_id=1, source_target_pairs={{0,8},{4,20},{8,0},{12,28},{16,24},{20,4},{24,16},{28,12},{1,9},{5... | collective-permute-start | bytes 1572872 | tf_op jit(solution)/shard_map/ppermute | solution.py:35
  208.0 26.5 %collective-permute-start.33 = (bf16[64,4096]{1,0:T(8,128)(2,1)S(1)}, bf16[64,4096]{1,0:T(8,128)(2,1)S(1)}, u32[]{:S(2)}, u32[]{:S(2)}) collective-permute-start(bf16[64,4096]{1,0:T(8,128)(2,1)S(1)} %add_convert_fusion.9), channel_id=1, source_target_pairs={{0,16},{4,12},{8,24},{12,4},{16,0},{20,28},{24,8},{28,20},{1,17},{... | collective-permute-start | bytes 1572872 | tf_op jit(solution)/shard_map/ppermute | solution.py:35
  209.5 23.0 %collective-permute-start.46 = (bf16[64,4096]{1,0:T(8,128)(2,1)S(1)}, bf16[64,4096]{1,0:T(8,128)(2,1)S(1)}, u32[]{:S(2)}, u32[]{:S(2)}) collective-permute-start(bf16[64,4096]{1,0:T(8,128)(2,1)S(1)} %add_convert_fusion.6), channel_id=1, source_target_pairs={{0,8},{4,20},{8,0},{12,28},{16,24},{20,4},{24,16},{28,12},{1,9},{5... | collective-permute-start | bytes 1572872 | tf_op jit(solution)/shard_map/ppermute | solution.py:35
  221.3 12.0 %collective-permute-start.50 = (bf16[64,4096]{1,0:T(8,128)(2,1)S(1)}, bf16[64,4096]{1,0:T(8,128)(2,1)S(1)}, u32[]{:S(2)}, u32[]{:S(2)}) collective-permute-start(bf16[64,4096]{1,0:T(8,128)(2,1)S(1)} %add_convert_fusion.2), channel_id=1, source_target_pairs={{0,16},{4,12},{8,24},{12,4},{16,0},{20,28},{24,8},{28,20},{1,17},{... | collective-permute-start | bytes 1572872 | tf_op jit(solution)/shard_map/ppermute | solution.py:35
  232.6 10.5 %collective-permute-start.30 = (bf16[64,4096]{1,0:T(8,128)(2,1)S(1)}, bf16[64,4096]{1,0:T(8,128)(2,1)S(1)}, u32[]{:S(2)}, u32[]{:S(2)}) collective-permute-start(bf16[64,4096]{1,0:T(8,128)(2,1)S(1)} %add_convert_fusion.12), channel_id=1, source_target_pairs={{0,4},{4,0},{8,12},{12,8},{16,20},{20,16},{24,28},{28,24},{1,5},{5... | collective-permute-start | bytes 1572872 | tf_op jit(solution)/shard_map/ppermute | solution.py:19
  232.7 3.1 %collective-permute-start.47 = (bf16[64,4096]{1,0:T(8,128)(2,1)S(1)}, bf16[64,4096]{1,0:T(8,128)(2,1)S(1)}, u32[]{:S(2)}, u32[]{:S(2)}) collective-permute-start(bf16[64,4096]{1,0:T(8,128)(2,1)S(1)} %add_convert_fusion.5), channel_id=1, source_target_pairs={{0,4},{4,0},{8,12},{12,8},{16,20},{20,16},{24,28},{28,24},{1,5},{5... | collective-permute-start | bytes 1572872 | tf_op jit(solution)/shard_map/ppermute | solution.py:19
  233.5 9.2 %collective-permute-start.51 = (bf16[64,4096]{1,0:T(8,128)(2,1)S(1)}, bf16[64,4096]{1,0:T(8,128)(2,1)S(1)}, u32[]{:S(2)}, u32[]{:S(2)}) collective-permute-start(bf16[64,4096]{1,0:T(8,128)(2,1)S(1)} %add_convert_fusion.1), channel_id=1, source_target_pairs={{0,8},{4,20},{8,0},{12,28},{16,24},{20,4},{24,16},{28,12},{1,9},{5... | collective-permute-start | bytes 1572872 | tf_op jit(solution)/shard_map/ppermute | solution.py:35
  234.7 13.6 %collective-permute-start.34 = (bf16[64,4096]{1,0:T(8,128)(2,1)S(1)}, bf16[64,4096]{1,0:T(8,128)(2,1)S(1)}, u32[]{:S(2)}, u32[]{:S(2)}) collective-permute-start(bf16[64,4096]{1,0:T(8,128)(2,1)S(1)} %add_convert_fusion.8), channel_id=1, source_target_pairs={{0,8},{4,20},{8,0},{12,28},{16,24},{20,4},{24,16},{28,12},{1,9},{5... | collective-permute-start | bytes 1572872 | tf_op jit(solution)/shard_map/ppermute | solution.py:35
  242.9 7.4 %collective-permute-start.52 = (bf16[32,4096]{1,0:T(8,128)(2,1)S(1)}, bf16[32,4096]{1,0:T(8,128)(2,1)S(1)}, u32[]{:S(2)}, u32[]{:S(2)}) collective-permute-start(bf16[32,4096]{1,0:T(8,128)(2,1)S(1)} %slice.19), channel_id=1, source_target_pairs={{0,1},{1,0},{2,3},{3,2},{4,5},{5,4},{6,7},{7,6},{8,9},{9,8},{10,11... | collective-permute-start | bytes 786440 | tf_op jit(solution)/shard_map/ppermute | solution.py:23
  248.6 12.4 %collective-permute-start.35 = (bf16[32,4096]{1,0:T(8,128)(2,1)S(1)}, bf16[32,4096]{1,0:T(8,128)(2,1)S(1)}, u32[]{:S(2)}, u32[]{:S(2)}) collective-permute-start(bf16[32,4096]{1,0:T(8,128)(2,1)S(1)} %slice.17), channel_id=1, source_target_pairs={{0,1},{1,0},{2,3},{3,2},{4,5},{5,4},{6,7},{7,6},{8,9},{9,8},{10,11... | collective-permute-start | bytes 786440 | tf_op jit(solution)/shard_map/ppermute | solution.py:23
  250.5 13.1 %collective-permute-start.53 = (bf16[32,4096]{1,0:T(8,128)(2,1)S(1)}, bf16[32,4096]{1,0:T(8,128)(2,1)S(1)}, u32[]{:S(2)}, u32[]{:S(2)}) collective-permute-start(bf16[32,4096]{1,0:T(8,128)(2,1)S(1)} %add_convert_fusion.15), channel_id=1, source_target_pairs={{0,2},{1,3},{2,0},{3,1},{4,6},{5,7},{6,4},{7,5},{8,10},{9,11},{10,... | collective-permute-start | bytes 786440 | tf_op jit(solution)/shard_map/ppermute | solution.py:23

commit v2 on v1

--- a/solution.py
+++ b/solution.py
@@ -78,6 +78,34 @@
     beside = plus(plus(beside, swap(theirs[0], 1)), returned)
     own = plus(own, swap(mate, 1))
     return plus(own, cross(beside, 0))
+
+
+def widen_kernel(small_ref, wide_ref):
+    wide_ref[...] = jnp.zeros_like(wide_ref)
+    wide_ref[:, : small_ref.shape[1]] = small_ref[...]
+
+
+def widen(router):
+    return pl.pallas_call(
+        widen_kernel,
+        out_shape=jax.ShapeDtypeStruct((router.shape[0], HEAD_SIZE), router.dtype),
+        name="widen",
+    )(router)
+
+
+def relay_kernel(in_ref, out_ref):
+    out_ref[0] = in_ref[0]
+
+
+def relay(place):
+    spec = pl.BlockSpec(memory_space=pltpu.SMEM)
+    return pl.pallas_call(
+        relay_kernel,
+        out_shape=jax.ShapeDtypeStruct(place.shape, place.dtype),
+        in_specs=[spec],
+        out_specs=spec,
+        name="relay",
+    )(place)
 
 
 def rise_kernel(parts, planes, place, router_ref, *refs):
@@ -466,14 +494,11 @@
     slots = [((b, 0), (b, 1)) for b in blocks]
     across = near ^ far
     state = stage(slots[:2], places([0, 1]), state=None, final=False)
-    state = stage(
-        [slots[2], slots[3], slots[5], slots[6]],
-        places([near, near ^ 1, far ^ 1, far]),
+    return stage(
+        [slots[2], slots[3], slots[5], slots[6], slots[4], slots[7]],
+        places([near, near ^ 1, far ^ 1, far, across, across ^ 1]),
         state=state,
-        final=False,
-    )
-    return stage(
-        [slots[4], slots[7]], places([across, across ^ 1]), state=state, final=True
+        final=True,
     )
 
 
@@ -502,14 +527,12 @@
     ctx_size = lax.axis_size("ctx")
     planes = lax.axis_size("exp")
     plane = lax.axis_index("exp")
-    experts = router.shape[1]
     row_count, width = residual.shape
 
     tags = jnp.pad(expert_ids.astype(jnp.bfloat16), ((0, 0), (0, HEAD_SIZE - 2)))
     tagged = planes_of(jnp.concatenate([cotangent, tags], axis=1), False)
     grads = gather(jnp.concatenate(tagged, axis=0))
-    tall_router = jnp.pad(router, ((0, 0), (0, HEAD_SIZE - experts)))
-    query, tall_router = lax.optimization_barrier((query, tall_router))
+    tall_router = widen(router)
 
     attn = attention(query, keys_values, cache)
 
@@ -531,6 +554,7 @@
     up_mat = in_place(w_up[0])
     down_mat = in_place(w_down[0])
     blocks = planes_of(normed, True)
+    place = relay(place)
     hidden, turned, counts = [], [], []
     for k in range(0, planes, 2):
         rows = gather(jnp.concatenate(blocks[k : k + 2], axis=0))

time: 265 us -> 274 us (1.034)
  local copies, waits for them, and re-layouts: 5.15 us -> 17.7 us
  waiting for transfers between devices: 129 us -> 120 us
  Pallas kernels: 77.8 us -> 81.6 us
    unnamed x19 -> x71, local copies, waits for them, and re-layouts: 3.24 us -> 16.1 us
    ppermute x18, waiting for transfers between devices: 77.3 us -> 70.2 us  [cross(): return lax.ppermute(value, 'ctx', pairs)]
    pallas_call x0 -> x2, Pallas kernels: none -> 3.12 us  [the longest x1 2.61 us: widen(): pl.pallas_call(widen_kernel, out_shape=jax.ShapeDtypeStruct((router.shape...]
    pallas_call x3 -> x2, Pallas kernels: 14.8 us -> 11.7 us  [attend(): pl.pallas_call(functools.partial(attend_kernel, slots, cached, window_fre...]
  transfers between devices with their start and end apart: 54 -> 54, of which waited for: 24 -> 23; matrix products, arithmetic and copies ran while one was open for 2% -> 2% of each run, Pallas kernels for 26% -> 25%
where the time goes in v2:
time: 274 us
  waiting for transfers between devices  120 us (44%)
  Pallas kernels  81.6 us (30%)
  starting transfers between devices  48.7 us (18%)
  local copies, waits for them, and re-layouts  17.7 us (6%)
  other arithmetic  4.32 us (2%)
    ppermute x18, waiting for transfers between devices, cross(): return lax.ppermute(value, 'ctx', pairs)  70.2 us
    ppermute x12, waiting for transfers between devices, swap_plane(): lax.ppermute(value, 'exp', [(i, i ^ bits) for i in range(lax.axis_size('e...  49.8 us
    pallas_call x2, Pallas kernels, rise(): pl.pallas_call(functools.partial(rise_kernel, len(rows), planes), out_sha...  30.5 us
    ppermute x18, starting transfers between devices, cross(): return lax.ppermute(value, 'ctx', pairs)  26.2 us
    ppermute x12, starting transfers between devices, swap_plane(): lax.ppermute(value, 'exp', [(i, i ^ bits) for i in range(lax.axis_size('e...  17.2 us
    pallas_call x2, Pallas kernels, outer(): pl.pallas_call(functools.partial(outer_kernel, len(grads), pieces, blocks...  16.4 us
    unnamed x71, local copies, waits for them, and re-layouts  16.1 us
    pallas_call x2, Pallas kernels, fall(): pl.pallas_call(fall_kernel, out_shape=[jax.ShapeDtypeStruct((c, width), j...  14.8 us
  transfers between devices with their start and end apart: 54, of which 23 were waited for; matrix products, arithmetic and copies ran while one was open for 2% of the time, Pallas kernels for 25%

profile of v2, /device:TPU:0, one launch (start us, length us, event | category | flops | bytes accessed | tf_op | source)
XLA Modules:
  0.0 273.5 jit_solution(14612423957927007396)
XLA Ops:
  0.6 1.0 constant_dynamic-update-slice_fusion.1
  1.6 0.9 constant_dynamic-update-slice_fusion.refs_2_.refs_4_
  3.1 2.6 collective-permute-start
  5.6 1.6 collective-permute-start.2
  7.3 4.1 %collective-permute-done.refs_2_.refs_8_ = bf16[2,384,256]{2,1,0:T(8,128)(2,1)S(1)} collective-permute-done((bf16[2,384,256]{2,1,0:T(8,128)(2,1)S(1)}, bf16[2,384,256]{2,1,0:T(8,128)(2,1)S(1)}, u32[]{:S(2)}, u32[]{:S(2)}) %collective-permute-start) | collective-permute-done | bytes 393248 | tf_op jit(solution)/shard_map/ppermute | solution.py:35
  11.4 2.0 collective-permute-start.5
  13.5 3.9 %collective-permute-done.2.refs_3_.refs_9_ = bf16[2,384,256]{2,1,0:T(8,128)(2,1)S(1)} collective-permute-done((bf16[2,384,256]{2,1,0:T(8,128)(2,1)S(1)}, bf16[2,384,256]{2,1,0:T(8,128)(2,1)S(1)}, u32[]{:S(2)}, u32[]{:S(2)}) %collective-permute-start.2) | collective-permute-done | bytes 393248 | tf_op jit(solution)/shard_map/ppermute | solution.py:35
  17.4 2.2 collective-permute-done.5.refs_6_.refs_12_
  21.7 4.2 %attend.2 = (f32[2,512,128]{2,1,0:T(8,128)}, f32[2,512,128]{2,1,0:T(8,128)}, f32[2,512,128]{2,1,0:T(8,128)}) custom-call(s32[4]{0:T(128)} %pad_add_fusion.refs_0_, bf16[128,1024]{1,0:T(8,128)(2,1)} %refs_1_.3, bf16[2,384,256]{2,1,0:T(8,128)(2,1)} %copy-done.21, bf16[2,384,256]{2,1,0:T(8,128)(2,1)} %copy-done.24, bf16[2,384,256]{2,1,0:T(8,128)(2,1)} %copy-done.21, ...), custom_call_target="tpu_custom_call" | custom-call | flops 402653184 | bytes 1572864 | tf_op jit(solution)/shard_map/attend/pallas_call | solution.py:446
  26.9 7.6 %attend.3.attn_ref = bf16[128,1024]{1,0:T(8,128)(2,1)} custom-call(s32[12]{0:T(128)} %stack.63.refs_0_, bf16[128,1024]{1,0:T(8,128)(2,1)} %refs_1_.3, bf16[2,384,256]{2,1,0:T(8,128)(2,1)} %copy-done.25, bf16[2,384,256]{2,1,0:T(8,128)(2,1)} %copy-done.26, bf16[2,384,256]{2,1,0:T(8,128)(2,1)} %copy-done.28, bf16[2,384,256]{2,1,0:T(8,128)(2,1)} %copy-done.29, ...), custom_call_target="tpu_custom_call" | custom-call | flops 1207959552 | bytes 4718592 | tf_op jit(solution)/shard_map/attend/pallas_call | solution.py:446
  34.5 0.9 copy-done.6
  35.4 5.1 %project.1 = (f32[32,4096]{1,0:T(8,128)S(1)}, bf16[32,4096]{1,0:T(8,128)(2,1)S(1)}, f32[32,4096]{1,0:T(8,128)S(1)}, bf16[32,4096]{1,0:T(8,128)(2,1)S(1)}) custom-call(s32[1]{0:T(128)} %bitcast.place.in_ref, bf16[128,1024]{1,0:T(8,128)(2,1)S(1)} %copy-done.6, bf16[1024,4096]{1,0:T(8,128)(2,1)} %proj_ref.1, bf16[32,4096]{1,0:T(8,128)(2,1)S(1)} %copy-done.8), custom_call_target="tpu_custom_call" | custom-call | flops 1073741824 | bytes 8388608 | tf_op jit(solution)/shard_map/project/pallas_call | solution.py:247
  40.5 2.1 collective-permute-start.8
  42.6 2.5 collective-permute-start.12
  45.4 1.7 collective-permute-start.10
  47.4 2.4 collective-permute-done.8
  49.8 7.6 %collective-permute-start.9 = (bf16[32,4096]{1,0:T(8,128)(2,1)S(1)}, bf16[32,4096]{1,0:T(8,128)(2,1)S(1)}, u32[]{:S(2)}, u32[]{:S(2)}) collective-permute-start(bf16[32,4096]{1,0:T(8,128)(2,1)S(1)} %add_convert_fusion.17), channel_id=1, source_target_pairs={{0,2},{1,3},{2,0},{3,1},{4,6},{5,7},{6,4},{7,5},{8,10},{9,11},{10,... | collective-permute-start | bytes 786440 | tf_op jit(solution)/shard_map/ppermute | solution.py:23
  58.1 12.0 %collective-permute-done.11 = bf16[32,4224]{1,0:T(8,128)(2,1)S(1)} collective-permute-done((bf16[32,4224]{1,0:T(8,128)(2,1)S(1)}, bf16[32,4224]{1,0:T(8,128)(2,1)S(1)}, u32[]{:S(2)}, u32[]{:S(2)}) %collective-permute-start.11) | collective-permute-done | bytes 270368 | tf_op jit(solution)/shard_map/ppermute | solution.py:23
  70.2 1.5 collective-permute-start.14
  71.7 5.8 %collective-permute-done.7 = bf16[32,4096]{1,0:T(8,128)(2,1)S(1)} collective-permute-done((bf16[32,4096]{1,0:T(8,128)(2,1)S(1)}, bf16[32,4096]{1,0:T(8,128)(2,1)S(1)}, u32[]{:S(2)}, u32[]{:S(2)}) %collective-permute-start.7) | collective-permute-done | bytes 262176 | tf_op jit(solution)/shard_map/ppermute | solution.py:23
  77.5 2.9 %collective-permute-done.9 = bf16[32,4096]{1,0:T(8,128)(2,1)S(1)} collective-permute-done((bf16[32,4096]{1,0:T(8,128)(2,1)S(1)}, bf16[32,4096]{1,0:T(8,128)(2,1)S(1)}, u32[]{:S(2)}, u32[]{:S(2)}) %collective-permute-start.9) | collective-permute-done | bytes 262176 | tf_op jit(solution)/shard_map/ppermute | solution.py:23
  81.2 4.2 %collective-permute-done.14.refs_2_ = bf16[128,4224]{1,0:T(8,128)(2,1)S(1)} collective-permute-done((bf16[128,4224]{1,0:T(8,128)(2,1)S(1)}, bf16[128,4224]{1,0:T(8,128)(2,1)S(1)}, u32[]{:S(2)}, u32[]{:S(2)}) %collective-permute-start.14) | collective-permute-done | bytes 1081376 | tf_op jit(solution)/shard_map/ppermute | solution.py:35
  85.4 1.5 collective-permute-start.16
  86.9 1.5 collective-permute-start.15
  89.2 13.9 %collective-permute-done.36 = bf16[32,4096]{1,0:T(8,128)(2,1)S(1)} collective-permute-done((bf16[32,4096]{1,0:T(8,128)(2,1)S(1)}, bf16[32,4096]{1,0:T(8,128)(2,1)S(1)}, u32[]{:S(2)}, u32[]{:S(2)}) %collective-permute-start.36) | collective-permute-done | bytes 262176 | tf_op jit(solution)/shard_map/ppermute | solution.py:23
  103.1 7.9 %collective-permute-done.37 = bf16[32,4096]{1,0:T(8,128)(2,1)S(1)} collective-permute-done((bf16[32,4096]{1,0:T(8,128)(2,1)S(1)}, bf16[32,4096]{1,0:T(8,128)(2,1)S(1)}, u32[]{:S(2)}, u32[]{:S(2)}) %collective-permute-start.37) | collective-permute-done | bytes 262176 | tf_op jit(solution)/shard_map/ppermute | solution.py:23
  111.1 1.0 copy-done.3
  113.6 3.7 %collective-permute-done.22.refs_10_ = bf16[64,4096]{1,0:T(8,128)(2,1)S(1)} collective-permute-done((bf16[64,4096]{1,0:T(8,128)(2,1)S(1)}, bf16[64,4096]{1,0:T(8,128)(2,1)S(1)}, u32[]{:S(2)}, u32[]{:S(2)}) %collective-permute-start.22) | collective-permute-done | bytes 524320 | tf_op jit(solution)/shard_map/ppermute | solution.py:35
  118.4 4.5 %collective-permute-done.39.refs_10_ = bf16[64,4096]{1,0:T(8,128)(2,1)S(1)} collective-permute-done((bf16[64,4096]{1,0:T(8,128)(2,1)S(1)}, bf16[64,4096]{1,0:T(8,128)(2,1)S(1)}, u32[]{:S(2)}, u32[]{:S(2)}) %collective-permute-start.39) | collective-permute-done | bytes 524320 | tf_op jit(solution)/shard_map/ppermute | solution.py:35
  122.9 1.5 collective-permute-start.24
  124.4 0.8 copy-done.13
  125.3 1.5 collective-permute-start.23
  126.8 0.8 copy-done.15
  127.5 0.8 copy-done.19
  128.8 7.9 %collective-permute-done.24.refs_12_ = bf16[64,4096]{1,0:T(8,128)(2,1)} collective-permute-done((bf16[64,4096]{1,0:T(8,128)(2,1)S(1)}, bf16[64,4096]{1,0:T(8,128)(2,1)}, u32[]{:S(2)}, u32[]{:S(2)}) %collective-permute-start.24) | collective-permute-done | bytes 524320 | tf_op jit(solution)/shard_map/ppermute | solution.py:35
  136.7 2.2 collective-permute-start.40
  138.9 1.3 collective-permute-done.23.refs_11_
  140.2 7.7 %collective-permute-done.41.refs_12_ = bf16[64,4096]{1,0:T(8,128)(2,1)S(1)} collective-permute-done((bf16[64,4096]{1,0:T(8,128)(2,1)S(1)}, bf16[64,4096]{1,0:T(8,128)(2,1)S(1)}, u32[]{:S(2)}, u32[]{:S(2)}) %collective-permute-start.41) | collective-permute-done | bytes 524320 | tf_op jit(solution)/shard_map/ppermute | solution.py:35
  149.1 1.4 copy.17.small_ref
  150.5 2.6 widen.1.router_ref
  154.2 1.2 copy-done.1
  155.4 1.2 copy-done.4
  156.6 1.2 copy-done.7
  157.9 1.0 copy-done.14
  158.9 1.0 copy-done.16
  159.9 1.0 copy-done.20
  161.0 15.3 %rise.2 = (bf16[512,1024]{1,0:T(8,128)(2,1)S(1)}, bf16[1024,512]{1,0:T(8,128)(2,1)S(1)}) custom-call(s32[1]{0:T(128)} %relay.1.place, bf16[4096,128]{1,0:T(8,128)(2,1)S(1)} %copy-done.7, bf16[128,4224]{1,0:T(8,128)(2,1)S(1)} %pad_maximum_fusion.refs_0_, bf16[128,4224]{1,0:T(8,128)(2,1)S(1)} %copy-done.1, ...), custom_call_target="tpu_custom_call" | custom-call | flops 8589934592 | bytes 20971520 | tf_op jit(solution)/shard_map/rise/pallas_call | solution.py:162
  176.4 7.4 %fall.2 = (bf16[64,4096]{1,0:T(8,128)(2,1)S(1)}, bf16[64,4096]{1,0:T(8,128)(2,1)S(1)}, bf16[64,4096]{1,0:T(8,128)(2,1)S(1)}, bf16[64,4096]{1,0:T(8,128)(2,1)S(1)...) custom-call(bf16[512,1024]{1,0:T(8,128)(2,1)S(1)} %get-tuple-element, ...), custom_call_target="tpu_custom_call" | custom-call | flops 4294967296 | bytes 12582912 | tf_op jit(solution)/shard_map/fall/pallas_call | solution.py:208
  184.4 15.2 %rise.3 = (bf16[512,1024]{1,0:T(8,128)(2,1)S(1)}, bf16[1024,512]{1,0:T(8,128)(2,1)S(1)}) custom-call(s32[1]{0:T(128)} %relay.1.place, bf16[4096,128]{1,0:T(8,128)(2,1)S(1)} %copy-done.7, bf16[128,4224]{1,0:T(8,128)(2,1)S(1)} %pad_maximum_fusion.refs_0_, bf16[128,4224]{1,0:T(8,128)(2,1)S(1)} %copy-done.1, ...), custom_call_target="tpu_custom_call" | custom-call | flops 8589934592 | bytes 20971520 | tf_op jit(solution)/shard_map/rise/pallas_call | solution.py:162
  199.6 7.4 %fall.3 = (bf16[64,4096]{1,0:T(8,128)(2,1)S(1)}, bf16[64,4096]{1,0:T(8,128)(2,1)S(1)}, bf16[64,4096]{1,0:T(8,128)(2,1)S(1)}, bf16[64,4096]{1,0:T(8,128)(2,1)S(1)...) custom-call(bf16[512,1024]{1,0:T(8,128)(2,1)S(1)} %get-tuple-element, ...), custom_call_target="tpu_custom_call" | custom-call | flops 4294967296 | bytes 12582912 | tf_op jit(solution)/shard_map/fall/pallas_call | solution.py:208
  207.6 8.2 %outer.2.refs_10_ = f32[1024,4096]{1,0:T(8,128)} custom-call(bf16[128,4224]{1,0:T(8,128)(2,1)S(1)} %pad_maximum_fusion.refs_0_, bf16[128,4224]{1,0:T(8,128)(2,1)S(1)} %copy-done.2, bf16[128,4224]{1,0:T(8,128)(2,1)S(1)} %collective-permute-done.14.refs_2_, bf16[128,4224]{1,0:T(8,128)(2,1)} %collective-permute-done.15.refs_3_, ...), custom_call_target="tpu_custom_call" | custom-call | flops 4294967296 | bytes 16777216 | tf_op jit(solution)/shard_map/outer/pallas_call | solution.py:304
  216.4 2.3 collective-permute-start.29
  218.8 1.6 collective-permute-start.33
  220.8 9.8 %collective-permute-done.29 = bf16[64,4096]{1,0:T(8,128)(2,1)S(1)} collective-permute-done((bf16[64,4096]{1,0:T(8,128)(2,1)S(1)}, bf16[64,4096]{1,0:T(8,128)(2,1)S(1)}, u32[]{:S(2)}, u32[]{:S(2)}) %collective-permute-start.29) | collective-permute-done | bytes 524320 | tf_op jit(solution)/shard_map/ppermute | solution.py:35
  230.6 2.2 collective-permute-start.50
  232.9 8.8 %collective-permute-done.46 = bf16[64,4096]{1,0:T(8,128)(2,1)S(1)} collective-permute-done((bf16[64,4096]{1,0:T(8,128)(2,1)S(1)}, bf16[64,4096]{1,0:T(8,128)(2,1)S(1)}, u32[]{:S(2)}, u32[]{:S(2)}) %collective-permute-start.46) | collective-permute-done | bytes 524320 | tf_op jit(solution)/shard_map/ppermute | solution.py:35
  242.6 2.4 collective-permute-start.51
  245.3 6.9 %collective-permute-done.51 = bf16[64,4096]{1,0:T(8,128)(2,1)S(1)} collective-permute-done((bf16[64,4096]{1,0:T(8,128)(2,1)S(1)}, bf16[64,4096]{1,0:T(8,128)(2,1)S(1)}, u32[]{:S(2)}, u32[]{:S(2)}) %collective-permute-start.51) | collective-permute-done | bytes 524320 | tf_op jit(solution)/shard_map/ppermute | solution.py:35
  252.5 5.3 %collective-permute-done.34 = bf16[64,4096]{1,0:T(8,128)(2,1)S(1)} collective-permute-done((bf16[64,4096]{1,0:T(8,128)(2,1)S(1)}, bf16[64,4096]{1,0:T(8,128)(2,1)S(1)}, u32[]{:S(2)}, u32[]{:S(2)}) %collective-permute-start.34) | collective-permute-done | bytes 524320 | tf_op jit(solution)/shard_map/ppermute | solution.py:35
  258.1 1.5 collective-permute-done.52
  259.7 2.0 collective-permute-start.53
  261.7 8.2 %outer.3 = f32[1024,4096]{1,0:T(8,128)} custom-call(bf16[128,4224]{1,0:T(8,128)(2,1)S(1)} %pad_maximum_fusion.refs_0_, bf16[128,4224]{1,0:T(8,128)(2,1)S(1)} %copy-done.2, bf16[128,4224]{1,0:T(8,128)(2,1)S(1)} %collective-permute-done.14.refs_2_, bf16[128,4224]{1,0:T(8,128)(2,1)} %collective-permute-done.15.refs_3_, ...), custom_call_target="tpu_custom_call", output_to_operand_aliasing={{}: (10, {})} | custom-call | flops 4294967296 | bytes 16777216 | tf_op jit(solution)/shard_map/outer/pallas_call | solution.py:304
  270.4 2.3 collective-permute-done.53
  272.6 0.9 add_convert_fusion.14
  (154 shorter events, 16.8 us)
Async XLA Ops:
  2.5 19.2 %copy-start.21 = (bf16[2,384,256]{2,1,0:T(8,128)(2,1)}, bf16[2,384,256]{2,1,0:T(8,128)(2,1)S(1)}, u32[]{:S(2)}) copy-start(bf16[2,384,256]{2,1,0:T(8,128)(2,1)S(1)} %constant_dynamic-update-slice_fusion.refs_2_.refs_4_) | copy-start | bytes 1179652
  2.5 3.1 %collective-permute-start.1 = (bf16[2,384,256]{2,1,0:T(8,128)(2,1)S(1)}, bf16[2,384,256]{2,1,0:T(8,128)(2,1)S(1)}, u32[]{:S(2)}, u32[]{:S(2)}) collective-permute-start(bf16[2,384,256]{2,1,0:T(8,128)(2,1)S(1)} %constant_dynamic-update-slice_fusion.refs_2_.refs_4_), channel_id=1, source_target_pairs={{0,4},{4,0},{8,12},{12,8},{16,20},{20,16},{24,28},{28,24},{1,5},{5... | collective-permute-start | bytes 1179656 | tf_op jit(solution)/shard_map/ppermute | solution.py:19
  3.1 8.3 %collective-permute-start = (bf16[2,384,256]{2,1,0:T(8,128)(2,1)S(1)}, bf16[2,384,256]{2,1,0:T(8,128)(2,1)S(1)}, u32[]{:S(2)}, u32[]{:S(2)}) collective-permute-start(bf16[2,384,256]{2,1,0:T(8,128)(2,1)S(1)} %constant_dynamic-update-slice_fusion.refs_2_.refs_4_), channel_id=1, source_target_pairs={{0,8},{4,20},{8,0},{12,28},{16,24},{20,4},{24,16},{28,12},{1,9},{5... | collective-permute-start | bytes 1179656 | tf_op jit(solution)/shard_map/ppermute | solution.py:35
  5.6 16.1 %copy-start.24 = (bf16[2,384,256]{2,1,0:T(8,128)(2,1)}, bf16[2,384,256]{2,1,0:T(8,128)(2,1)S(1)}, u32[]{:S(2)}) copy-start(bf16[2,384,256]{2,1,0:T(8,128)(2,1)S(1)} %collective-permute-done.1.refs_3_.refs_5_) | copy-start | bytes 1179652
  5.6 11.7 %collective-permute-start.2 = (bf16[2,384,256]{2,1,0:T(8,128)(2,1)S(1)}, bf16[2,384,256]{2,1,0:T(8,128)(2,1)S(1)}, u32[]{:S(2)}, u32[]{:S(2)}) collective-permute-start(bf16[2,384,256]{2,1,0:T(8,128)(2,1)S(1)} %collective-permute-done.1.refs_3_.refs_5_), channel_id=1, source_target_pairs={{0,8},{4,20},{8,0},{12,28},{16,24},{20,4},{24,16},{28,12},{1,9},{5... | collective-permute-start | bytes 1179656 | tf_op jit(solution)/shard_map/ppermute | solution.py:35
  11.4 14.5 %copy-start.25 = (bf16[2,384,256]{2,1,0:T(8,128)(2,1)}, bf16[2,384,256]{2,1,0:T(8,128)(2,1)S(1)}, u32[]{:S(2)}) copy-start(bf16[2,384,256]{2,1,0:T(8,128)(2,1)S(1)} %collective-permute-done.refs_2_.refs_8_) | copy-start | bytes 1179652
  11.4 8.2 %collective-permute-start.5 = (bf16[2,384,256]{2,1,0:T(8,128)(2,1)S(1)}, bf16[2,384,256]{2,1,0:T(8,128)(2,1)S(1)}, u32[]{:S(2)}, u32[]{:S(2)}) collective-permute-start(bf16[2,384,256]{2,1,0:T(8,128)(2,1)S(1)} %collective-permute-done.refs_2_.refs_8_), channel_id=1, source_target_pairs={{0,16},{4,12},{8,24},{12,4},{16,0},{20,28},{24,8},{28,20},{1,17},{... | collective-permute-start | bytes 1179656 | tf_op jit(solution)/shard_map/ppermute | solution.py:35
  13.4 12.4 %collective-permute-start.3 = (bf16[2,384,256]{2,1,0:T(8,128)(2,1)S(1)}, bf16[2,384,256]{2,1,0:T(8,128)(2,1)S(1)}, u32[]{:S(2)}, u32[]{:S(2)}) collective-permute-start(bf16[2,384,256]{2,1,0:T(8,128)(2,1)S(1)} %collective-permute-done.refs_2_.refs_8_), channel_id=1, source_target_pairs={{0,4},{4,0},{8,12},{12,8},{16,20},{20,16},{24,28},{28,24},{1,5},{5... | collective-permute-start | bytes 1179656 | tf_op jit(solution)/shard_map/ppermute | solution.py:19
  17.3 8.6 %copy-start.26 = (bf16[2,384,256]{2,1,0:T(8,128)(2,1)}, bf16[2,384,256]{2,1,0:T(8,128)(2,1)S(1)}, u32[]{:S(2)}) copy-start(bf16[2,384,256]{2,1,0:T(8,128)(2,1)S(1)} %collective-permute-done.2.refs_3_.refs_9_) | copy-start | bytes 1179652
  17.3 8.5 %collective-permute-start.4 = (bf16[2,384,256]{2,1,0:T(8,128)(2,1)S(1)}, bf16[2,384,256]{2,1,0:T(8,128)(2,1)S(1)}, u32[]{:S(2)}, u32[]{:S(2)}) collective-permute-start(bf16[2,384,256]{2,1,0:T(8,128)(2,1)S(1)} %collective-permute-done.2.refs_3_.refs_9_), channel_id=1, source_target_pairs={{0,4},{4,0},{8,12},{12,8},{16,20},{20,16},{24,28},{28,24},{1,5},{5... | collective-permute-start | bytes 1179656 | tf_op jit(solution)/shard_map/ppermute | solution.py:19
  19.6 6.3 %collective-permute-start.6 = (bf16[2,384,256]{2,1,0:T(8,128)(2,1)S(1)}, bf16[2,384,256]{2,1,0:T(8,128)(2,1)S(1)}, u32[]{:S(2)}, u32[]{:S(2)}) collective-permute-start(bf16[2,384,256]{2,1,0:T(8,128)(2,1)S(1)} %collective-permute-done.5.refs_6_.refs_12_), channel_id=1, source_target_pairs={{0,4},{4,0},{8,12},{12,8},{16,20},{20,16},{24,28},{28,24},{1,5},{5... | collective-permute-start | bytes 1179656 | tf_op jit(solution)/shard_map/ppermute | solution.py:19
  40.5 9.2 %collective-permute-start.8 = (bf16[32,4096]{1,0:T(8,128)(2,1)S(1)}, bf16[32,4096]{1,0:T(8,128)(2,1)S(1)}, u32[]{:S(2)}, u32[]{:S(2)}) collective-permute-start(bf16[32,4096]{1,0:T(8,128)(2,1)S(1)} %get-tuple-element.35), channel_id=1, source_target_pairs={{0,1},{1,0},{2,3},{3,2},{4,5},{5,4},{6,7},{7,6},{8,9},{9,8},{10,11... | collective-permute-start | bytes 786440 | tf_op jit(solution)/shard_map/ppermute | solution.py:23
  42.6 38.1 %copy-start.33 = (f32[4096]{0:T(1024)S(1)}, f32[4096]{0:T(1024)}, u32[]{:S(2)}) copy-start(f32[4096]{0:T(1024)} %param.17) | copy-start | bytes 49156
  42.6 15.5 %collective-permute-start.12 = (bf16[32,4224]{1,0:T(8,128)(2,1)S(1)}, bf16[32,4224]{1,0:T(8,128)(2,1)S(1)}, u32[]{:S(2)}, u32[]{:S(2)}) collective-permute-start(bf16[32,4224]{1,0:T(8,128)(2,1)S(1)} %pad_maximum_fusion.2), channel_id=1, source_target_pairs={{0,3},{1,2},{2,1},{3,0},{4,7},{5,6},{6,5},{7,4},{8,11},{9,10},{10,... | collective-permute-start | bytes 811016 | tf_op jit(solution)/shard_map/ppermute | solution.py:23
  45.2 24.9 %collective-permute-start.11 = (bf16[32,4224]{1,0:T(8,128)(2,1)S(1)}, bf16[32,4224]{1,0:T(8,128)(2,1)S(1)}, u32[]{:S(2)}, u32[]{:S(2)}) collective-permute-start(bf16[32,4224]{1,0:T(8,128)(2,1)S(1)} %pad_maximum_fusion.2), channel_id=1, source_target_pairs={{0,2},{1,3},{2,0},{3,1},{4,6},{5,7},{6,4},{7,5},{8,10},{9,11},{10,... | collective-permute-start | bytes 811016 | tf_op jit(solution)/shard_map/ppermute | solution.py:23
  45.4 24.7 %collective-permute-start.10 = (bf16[32,4224]{1,0:T(8,128)(2,1)S(1)}, bf16[32,4224]{1,0:T(8,128)(2,1)S(1)}, u32[]{:S(2)}, u32[]{:S(2)}) collective-permute-start(bf16[32,4224]{1,0:T(8,128)(2,1)S(1)} %pad_maximum_fusion.2), channel_id=1, source_target_pairs={{0,1},{1,0},{2,3},{3,2},{4,5},{5,4},{6,7},{7,6},{8,9},{9,8},{10,11... | collective-permute-start | bytes 811016 | tf_op jit(solution)/shard_map/ppermute | solution.py:23
  47.1 30.5 %collective-permute-start.7 = (bf16[32,4096]{1,0:T(8,128)(2,1)S(1)}, bf16[32,4096]{1,0:T(8,128)(2,1)S(1)}, u32[]{:S(2)}, u32[]{:S(2)}) collective-permute-start(bf16[32,4096]{1,0:T(8,128)(2,1)S(1)} %get-tuple-element.33), channel_id=1, source_target_pairs={{0,1},{1,0},{2,3},{3,2},{4,5},{5,4},{6,7},{7,6},{8,9},{9,8},{10,11... | collective-permute-start | bytes 786440 | tf_op jit(solution)/shard_map/ppermute | solution.py:23
  49.8 30.7 %collective-permute-start.9 = (bf16[32,4096]{1,0:T(8,128)(2,1)S(1)}, bf16[32,4096]{1,0:T(8,128)(2,1)S(1)}, u32[]{:S(2)}, u32[]{:S(2)}) collective-permute-start(bf16[32,4096]{1,0:T(8,128)(2,1)S(1)} %add_convert_fusion.17), channel_id=1, source_target_pairs={{0,2},{1,3},{2,0},{3,1},{4,6},{5,7},{6,4},{7,5},{8,10},{9,11},{10,... | collective-permute-start | bytes 786440 | tf_op jit(solution)/shard_map/ppermute | solution.py:23
  70.2 15.2 %collective-permute-start.14 = (bf16[128,4224]{1,0:T(8,128)(2,1)S(1)}, bf16[128,4224]{1,0:T(8,128)(2,1)S(1)}, u32[]{:S(2)}, u32[]{:S(2)}) collective-permute-start(bf16[128,4224]{1,0:T(8,128)(2,1)S(1)} %pad_maximum_fusion.refs_0_), channel_id=1, source_target_pairs={{0,8},{4,20},{8,0},{12,28},{16,24},{20,4},{24,16},{28,12},{1,9},{5... | collective-permute-start | bytes 3244040 | tf_op jit(solution)/shard_map/ppermute | solution.py:35
  71.7 15.2 %collective-permute-start.13 = (bf16[128,4224]{1,0:T(8,128)(2,1)S(1)}, bf16[128,4224]{1,0:T(8,128)(2,1)S(1)}, u32[]{:S(2)}, u32[]{:S(2)}) collective-permute-start(bf16[128,4224]{1,0:T(8,128)(2,1)S(1)} %pad_maximum_fusion.refs_0_), channel_id=1, source_target_pairs={{0,4},{4,0},{8,12},{12,8},{16,20},{20,16},{24,28},{28,24},{1,5},{5... | collective-permute-start | bytes 3244040 | tf_op jit(solution)/shard_map/ppermute | solution.py:19
  80.5 8.1 %copy-start.22 = (bf16[32,4096]{1,0:T(8,128)(2,1)}, bf16[32,4096]{1,0:T(8,128)(2,1)S(1)}, u32[]{:S(2)}) copy-start(bf16[32,4096]{1,0:T(8,128)(2,1)S(1)} %collective-permute-done.9) | copy-start | bytes 786436
  80.5 68.7 %copy-start.32 = (bf16[4096,4]{0,1:T(4,128)(2,1)S(1)}, bf16[4096,4]{0,1:T(4,128)(2,1)}, u32[]{:S(2)}) copy-start(bf16[4096,4]{0,1:T(4,128)(2,1)} %param.18) | copy-start | bytes 98308
  80.8 7.7 %collective-permute-start.20 = (bf16[32,4096]{1,0:T(8,128)(2,1)S(1)}, bf16[32,4096]{1,0:T(8,128)(2,1)S(1)}, u32[]{:S(2)}, u32[]{:S(2)}) collective-permute-start(bf16[32,4096]{1,0:T(8,128)(2,1)S(1)} %multiply_convert_fusion), channel_id=1, source_target_pairs={{0,1},{1,0},{2,3},{3,2},{4,5},{5,4},{6,7},{7,6},{8,9},{9,8},{10,11... | collective-permute-start | bytes 786440 | tf_op jit(solution)/shard_map/ppermute | solution.py:23
  85.4 25.7 %collective-permute-start.17 = (bf16[128,4224]{1,0:T(8,128)(2,1)S(1)}, bf16[128,4224]{1,0:T(8,128)(2,1)S(1)}, u32[]{:S(2)}, u32[]{:S(2)}) collective-permute-start(bf16[128,4224]{1,0:T(8,128)(2,1)S(1)} %collective-permute-done.14.refs_2_), channel_id=1, source_target_pairs={{0,4},{4,0},{8,12},{12,8},{16,20},{20,16},{24,28},{28,24},{1,5},{5... | collective-permute-start | bytes 3244040 | tf_op jit(solution)/shard_map/ppermute | solution.py:19
  85.4 27.2 %collective-permute-start.16 = (bf16[128,4224]{1,0:T(8,128)(2,1)S(1)}, bf16[128,4224]{1,0:T(8,128)(2,1)}, u32[]{:S(2)}, u32[]{:S(2)}) collective-permute-start(bf16[128,4224]{1,0:T(8,128)(2,1)S(1)} %collective-permute-done.14.refs_2_), channel_id=1, source_target_pairs={{0,16},{4,12},{8,24},{12,4},{16,0},{20,28},{24,8},{28,20},{1,17},{... | collective-permute-start | bytes 3244040 | tf_op jit(solution)/shard_map/ppermute | solution.py:35
  86.9 25.7 %copy-start = (bf16[128,4224]{1,0:T(8,128)(2,1)}, bf16[128,4224]{1,0:T(8,128)(2,1)S(1)}, u32[]{:S(2)}) copy-start(bf16[128,4224]{1,0:T(8,128)(2,1)S(1)} %collective-permute-done.13.refs_1_) | copy-start | bytes 3244036
  86.9 31.0 %collective-permute-start.15 = (bf16[128,4224]{1,0:T(8,128)(2,1)S(1)}, bf16[128,4224]{1,0:T(8,128)(2,1)}, u32[]{:S(2)}, u32[]{:S(2)}) collective-permute-start(bf16[128,4224]{1,0:T(8,128)(2,1)S(1)} %collective-permute-done.13.refs_1_), channel_id=1, source_target_pairs={{0,8},{4,20},{8,0},{12,28},{16,24},{20,4},{24,16},{28,12},{1,9},{5... | collective-permute-start | bytes 3244040 | tf_op jit(solution)/shard_map/ppermute | solution.py:35
  88.4 14.7 %collective-permute-start.36 = (bf16[32,4096]{1,0:T(8,128)(2,1)S(1)}, bf16[32,4096]{1,0:T(8,128)(2,1)S(1)}, u32[]{:S(2)}, u32[]{:S(2)}) collective-permute-start(bf16[32,4096]{1,0:T(8,128)(2,1)S(1)} %multiply_convert_fusion), channel_id=1, source_target_pairs={{0,2},{1,3},{2,0},{3,1},{4,6},{5,7},{6,4},{7,5},{8,10},{9,11},{10,... | collective-permute-start | bytes 786440 | tf_op jit(solution)/shard_map/ppermute | solution.py:23
  88.6 28.7 %collective-permute-start.22 = (bf16[64,4096]{1,0:T(8,128)(2,1)S(1)}, bf16[64,4096]{1,0:T(8,128)(2,1)S(1)}, u32[]{:S(2)}, u32[]{:S(2)}) collective-permute-start(bf16[64,4096]{1,0:T(8,128)(2,1)S(1)} %pad_maximum_fusion.1.refs_8_), channel_id=1, source_target_pairs={{0,8},{4,20},{8,0},{12,28},{16,24},{20,4},{24,16},{28,12},{1,9},{5... | collective-permute-start | bytes 1572872 | tf_op jit(solution)/shard_map/ppermute | solution.py:35
  103.1 7.9 %collective-permute-start.37 = (bf16[32,4096]{1,0:T(8,128)(2,1)S(1)}, bf16[32,4096]{1,0:T(8,128)(2,1)S(1)}, u32[]{:S(2)}, u32[]{:S(2)}) collective-permute-start(bf16[32,4096]{1,0:T(8,128)(2,1)S(1)} %collective-permute-done.36), channel_id=1, source_target_pairs={{0,1},{1,0},{2,3},{3,2},{4,5},{5,4},{6,7},{7,6},{8,9},{9,8},{10,11... | collective-permute-start | bytes 786440 | tf_op jit(solution)/shard_map/ppermute | solution.py:23
  111.0 6.9 %collective-permute-start.21 = (bf16[64,4096]{1,0:T(8,128)(2,1)S(1)}, bf16[64,4096]{1,0:T(8,128)(2,1)S(1)}, u32[]{:S(2)}, u32[]{:S(2)}) collective-permute-start(bf16[64,4096]{1,0:T(8,128)(2,1)S(1)} %pad_maximum_fusion.1.refs_8_), channel_id=1, source_target_pairs={{0,4},{4,0},{8,12},{12,8},{16,20},{20,16},{24,28},{28,24},{1,5},{5... | collective-permute-start | bytes 1572872 | tf_op jit(solution)/shard_map/ppermute | solution.py:19
  112.1 10.9 %collective-permute-start.39 = (bf16[64,4096]{1,0:T(8,128)(2,1)S(1)}, bf16[64,4096]{1,0:T(8,128)(2,1)S(1)}, u32[]{:S(2)}, u32[]{:S(2)}) collective-permute-start(bf16[64,4096]{1,0:T(8,128)(2,1)S(1)} %constant_dynamic-update-slice_fusion.2.refs_8_), channel_id=1, source_target_pairs={{0,8},{4,20},{8,0},{12,28},{16,24},{20,4},{24,16},{28,12},{1,9},{5... | collective-permute-start | bytes 1572872 | tf_op jit(solution)/shard_map/ppermute | solution.py:35
  112.6 12.7 %collective-permute-start.38 = (bf16[64,4096]{1,0:T(8,128)(2,1)S(1)}, bf16[64,4096]{1,0:T(8,128)(2,1)}, u32[]{:S(2)}, u32[]{:S(2)}) collective-permute-start(bf16[64,4096]{1,0:T(8,128)(2,1)S(1)} %constant_dynamic-update-slice_fusion.2.refs_8_), channel_id=1, source_target_pairs={{0,4},{4,0},{8,12},{12,8},{16,20},{20,16},{24,28},{28,24},{1,5},{5... | collective-permute-start | bytes 1572872 | tf_op jit(solution)/shard_map/ppermute | solution.py:19
  117.3 10.2 %collective-permute-start.25 = (bf16[64,4096]{1,0:T(8,128)(2,1)S(1)}, bf16[64,4096]{1,0:T(8,128)(2,1)S(1)}, u32[]{:S(2)}, u32[]{:S(2)}) collective-permute-start(bf16[64,4096]{1,0:T(8,128)(2,1)S(1)} %collective-permute-done.22.refs_10_), channel_id=1, source_target_pairs={{0,4},{4,0},{8,12},{12,8},{16,20},{20,16},{24,28},{28,24},{1,5},{5... | collective-permute-start | bytes 1572872 | tf_op jit(solution)/shard_map/ppermute | solution.py:19
  117.9 35.7 %collective-permute-start.19 = (bf16[128,4224]{1,0:T(8,128)(2,1)}, bf16[128,4224]{1,0:T(8,128)(2,1)}, u32[]{:S(2)}, u32[]{:S(2)}) collective-permute-start(bf16[128,4224]{1,0:T(8,128)(2,1)} %collective-permute-done.16.refs_4_), channel_id=1, source_target_pairs={{0,4},{4,0},{8,12},{12,8},{16,20},{20,16},{24,28},{28,24},{1,5},{5... | collective-permute-start | bytes 3244040 | tf_op jit(solution)/shard_map/ppermute | solution.py:19
  117.9 35.8 %collective-permute-start.18 = (bf16[128,4224]{1,0:T(8,128)(2,1)}, bf16[128,4224]{1,0:T(8,128)(2,1)}, u32[]{:S(2)}, u32[]{:S(2)}) collective-permute-start(bf16[128,4224]{1,0:T(8,128)(2,1)} %collective-permute-done.15.refs_3_), channel_id=1, source_target_pairs={{0,4},{4,0},{8,12},{12,8},{16,20},{20,16},{24,28},{28,24},{1,5},{5... | collective-permute-start | bytes 3244040 | tf_op jit(solution)/shard_map/ppermute | solution.py:19
  122.9 13.7 %collective-permute-start.24 = (bf16[64,4096]{1,0:T(8,128)(2,1)S(1)}, bf16[64,4096]{1,0:T(8,128)(2,1)}, u32[]{:S(2)}, u32[]{:S(2)}) collective-permute-start(bf16[64,4096]{1,0:T(8,128)(2,1)S(1)} %collective-permute-done.22.refs_10_), channel_id=1, source_target_pairs={{0,16},{4,12},{8,24},{12,4},{16,0},{20,28},{24,8},{28,20},{1,17},{... | collective-permute-start | bytes 1572872 | tf_op jit(solution)/shard_map/ppermute | solution.py:35
  125.3 14.9 %collective-permute-start.23 = (bf16[64,4096]{1,0:T(8,128)(2,1)S(1)}, bf16[64,4096]{1,0:T(8,128)(2,1)}, u32[]{:S(2)}, u32[]{:S(2)}) collective-permute-start(bf16[64,4096]{1,0:T(8,128)(2,1)S(1)} %collective-permute-done.21.refs_9_), channel_id=1, source_target_pairs={{0,8},{4,20},{8,0},{12,28},{16,24},{20,4},{24,16},{28,12},{1,9},{5... | collective-permute-start | bytes 1572872 | tf_op jit(solution)/shard_map/ppermute | solution.py:35
  128.3 19.5 %collective-permute-start.41 = (bf16[64,4096]{1,0:T(8,128)(2,1)S(1)}, bf16[64,4096]{1,0:T(8,128)(2,1)S(1)}, u32[]{:S(2)}, u32[]{:S(2)}) collective-permute-start(bf16[64,4096]{1,0:T(8,128)(2,1)S(1)} %collective-permute-done.39.refs_10_), channel_id=1, source_target_pairs={{0,16},{4,12},{8,24},{12,4},{16,0},{20,28},{24,8},{28,20},{1,17},{... | collective-permute-start | bytes 1572872 | tf_op jit(solution)/shard_map/ppermute | solution.py:35
  136.7 16.4 %collective-permute-start.40 = (bf16[64,4096]{1,0:T(8,128)(2,1)}, bf16[64,4096]{1,0:T(8,128)(2,1)}, u32[]{:S(2)}, u32[]{:S(2)}) collective-permute-start(bf16[64,4096]{1,0:T(8,128)(2,1)} %collective-permute-done.38.refs_9_), channel_id=1, source_target_pairs={{0,8},{4,20},{8,0},{12,28},{16,24},{20,4},{24,16},{28,12},{1,9},{5... | collective-permute-start | bytes 1572872 | tf_op jit(solution)/shard_map/ppermute | solution.py:35
  140.2 14.0 %collective-permute-start.27 = (bf16[64,4096]{1,0:T(8,128)(2,1)}, bf16[64,4096]{1,0:T(8,128)(2,1)}, u32[]{:S(2)}, u32[]{:S(2)}) collective-permute-start(bf16[64,4096]{1,0:T(8,128)(2,1)} %collective-permute-done.24.refs_12_), channel_id=1, source_target_pairs={{0,4},{4,0},{8,12},{12,8},{16,20},{20,16},{24,28},{28,24},{1,5},{5... | collective-permute-start | bytes 1572872 | tf_op jit(solution)/shard_map/ppermute | solution.py:19
  148.6 5.6 %collective-permute-start.26 = (bf16[64,4096]{1,0:T(8,128)(2,1)}, bf16[64,4096]{1,0:T(8,128)(2,1)}, u32[]{:S(2)}, u32[]{:S(2)}) collective-permute-start(bf16[64,4096]{1,0:T(8,128)(2,1)} %collective-permute-done.23.refs_11_), channel_id=1, source_target_pairs={{0,4},{4,0},{8,12},{12,8},{16,20},{20,16},{24,28},{28,24},{1,5},{5... | collective-permute-start | bytes 1572872 | tf_op jit(solution)/shard_map/ppermute | solution.py:19
  153.1 31.2 %collective-permute-start.42 = (bf16[64,4096]{1,0:T(8,128)(2,1)}, bf16[64,4096]{1,0:T(8,128)(2,1)S(1)}, u32[]{:S(2)}, u32[]{:S(2)}) collective-permute-start(bf16[64,4096]{1,0:T(8,128)(2,1)} %copy-done.11), channel_id=1, source_target_pairs={{0,4},{4,0},{8,12},{12,8},{16,20},{20,16},{24,28},{28,24},{1,5},{5... | collective-permute-start | bytes 1572872 | tf_op jit(solution)/shard_map/ppermute | solution.py:19
  153.6 30.8 %collective-permute-start.44 = (bf16[64,4096]{1,0:T(8,128)(2,1)}, bf16[64,4096]{1,0:T(8,128)(2,1)S(1)}, u32[]{:S(2)}, u32[]{:S(2)}) collective-permute-start(bf16[64,4096]{1,0:T(8,128)(2,1)} %copy-done.17), channel_id=1, source_target_pairs={{0,4},{4,0},{8,12},{12,8},{16,20},{20,16},{24,28},{28,24},{1,5},{5... | collective-permute-start | bytes 1572872 | tf_op jit(solution)/shard_map/ppermute | solution.py:19
  153.7 30.7 %collective-permute-start.43 = (bf16[64,4096]{1,0:T(8,128)(2,1)}, bf16[64,4096]{1,0:T(8,128)(2,1)S(1)}, u32[]{:S(2)}, u32[]{:S(2)}) collective-permute-start(bf16[64,4096]{1,0:T(8,128)(2,1)} %collective-permute-done.40.refs_11_), channel_id=1, source_target_pairs={{0,4},{4,0},{8,12},{12,8},{16,20},{20,16},{24,28},{28,24},{1,5},{5... | collective-permute-start | bytes 1572872 | tf_op jit(solution)/shard_map/ppermute | solution.py:19
  176.3 8.1 %copy-start.10 = (bf16[64,4096]{1,0:T(8,128)(2,1)S(1)}, bf16[64,4096]{1,0:T(8,128)(2,1)}, u32[]{:S(2)}) copy-start(bf16[64,4096]{1,0:T(8,128)(2,1)} %copy-done.9) | copy-start | bytes 1572868
  183.7 32.1 %collective-permute-start.28 = (bf16[64,4096]{1,0:T(8,128)(2,1)S(1)}, bf16[64,4096]{1,0:T(8,128)(2,1)S(1)}, u32[]{:S(2)}, u32[]{:S(2)}) collective-permute-start(bf16[64,4096]{1,0:T(8,128)(2,1)S(1)} %get-tuple-element.40), channel_id=1, source_target_pairs={{0,4},{4,0},{8,12},{12,8},{16,20},{20,16},{24,28},{28,24},{1,5},{5... | collective-permute-start | bytes 1572872 | tf_op jit(solution)/shard_map/ppermute | solution.py:19
  183.8 61.2 %collective-permute-start.31 = (bf16[64,4096]{1,0:T(8,128)(2,1)S(1)}, bf16[64,4096]{1,0:T(8,128)(2,1)S(1)}, u32[]{:S(2)}, u32[]{:S(2)}) collective-permute-start(bf16[64,4096]{1,0:T(8,128)(2,1)S(1)} %get-tuple-element.42), channel_id=1, source_target_pairs={{0,4},{4,0},{8,12},{12,8},{16,20},{20,16},{24,28},{28,24},{1,5},{5... | collective-permute-start | bytes 1572872 | tf_op jit(solution)/shard_map/ppermute | solution.py:19
  184.3 32.1 %collective-permute-start.32 = (bf16[64,4096]{1,0:T(8,128)(2,1)S(1)}, bf16[64,4096]{1,0:T(8,128)(2,1)S(1)}, u32[]{:S(2)}, u32[]{:S(2)}) collective-permute-start(bf16[64,4096]{1,0:T(8,128)(2,1)S(1)} %get-tuple-element.44), channel_id=1, source_target_pairs={{0,4},{4,0},{8,12},{12,8},{16,20},{20,16},{24,28},{28,24},{1,5},{5... | collective-permute-start | bytes 1572872 | tf_op jit(solution)/shard_map/ppermute | solution.py:19
  207.0 11.8 %collective-permute-start.45 = (bf16[64,4096]{1,0:T(8,128)(2,1)S(1)}, bf16[64,4096]{1,0:T(8,128)(2,1)S(1)}, u32[]{:S(2)}, u32[]{:S(2)}) collective-permute-start(bf16[64,4096]{1,0:T(8,128)(2,1)S(1)} %get-tuple-element.49), channel_id=1, source_target_pairs={{0,4},{4,0},{8,12},{12,8},{16,20},{20,16},{24,28},{28,24},{1,5},{5... | collective-permute-start | bytes 1572872 | tf_op jit(solution)/shard_map/ppermute | solution.py:19
  207.5 34.3 %collective-permute-start.48 = (bf16[64,4096]{1,0:T(8,128)(2,1)S(1)}, bf16[64,4096]{1,0:T(8,128)(2,1)S(1)}, u32[]{:S(2)}, u32[]{:S(2)}) collective-permute-start(bf16[64,4096]{1,0:T(8,128)(2,1)S(1)} %get-tuple-element.51), channel_id=1, source_target_pairs={{0,4},{4,0},{8,12},{12,8},{16,20},{20,16},{24,28},{28,24},{1,5},{5... | collective-permute-start | bytes 1572872 | tf_op jit(solution)/shard_map/ppermute | solution.py:19
  215.9 4.7 %collective-permute-start.49 = (bf16[64,4096]{1,0:T(8,128)(2,1)S(1)}, bf16[64,4096]{1,0:T(8,128)(2,1)S(1)}, u32[]{:S(2)}, u32[]{:S(2)}) collective-permute-start(bf16[64,4096]{1,0:T(8,128)(2,1)S(1)} %get-tuple-element.53), channel_id=1, source_target_pairs={{0,4},{4,0},{8,12},{12,8},{16,20},{20,16},{24,28},{28,24},{1,5},{5... | collective-permute-start | bytes 1572872 | tf_op jit(solution)/shard_map/ppermute | solution.py:19
  216.4 14.2 %collective-permute-start.29 = (bf16[64,4096]{1,0:T(8,128)(2,1)S(1)}, bf16[64,4096]{1,0:T(8,128)(2,1)S(1)}, u32[]{:S(2)}, u32[]{:S(2)}) collective-permute-start(bf16[64,4096]{1,0:T(8,128)(2,1)S(1)} %add_convert_fusion.13), channel_id=1, source_target_pairs={{0,8},{4,20},{8,0},{12,28},{16,24},{20,4},{24,16},{28,12},{1,9},{5... | collective-permute-start | bytes 1572872 | tf_op jit(solution)/shard_map/ppermute | solution.py:35
  218.8 26.2 %collective-permute-start.33 = (bf16[64,4096]{1,0:T(8,128)(2,1)S(1)}, bf16[64,4096]{1,0:T(8,128)(2,1)S(1)}, u32[]{:S(2)}, u32[]{:S(2)}) collective-permute-start(bf16[64,4096]{1,0:T(8,128)(2,1)S(1)} %add_convert_fusion.9), channel_id=1, source_target_pairs={{0,16},{4,12},{8,24},{12,4},{16,0},{20,28},{24,8},{28,20},{1,17},{... | collective-permute-start | bytes 1572872 | tf_op jit(solution)/shard_map/ppermute | solution.py:35
  220.6 21.1 %collective-permute-start.46 = (bf16[64,4096]{1,0:T(8,128)(2,1)S(1)}, bf16[64,4096]{1,0:T(8,128)(2,1)S(1)}, u32[]{:S(2)}, u32[]{:S(2)}) collective-permute-start(bf16[64,4096]{1,0:T(8,128)(2,1)S(1)} %add_convert_fusion.6), channel_id=1, source_target_pairs={{0,8},{4,20},{8,0},{12,28},{16,24},{20,4},{24,16},{28,12},{1,9},{5... | collective-permute-start | bytes 1572872 | tf_op jit(solution)/shard_map/ppermute | solution.py:35
  230.6 11.8 %collective-permute-start.50 = (bf16[64,4096]{1,0:T(8,128)(2,1)S(1)}, bf16[64,4096]{1,0:T(8,128)(2,1)S(1)}, u32[]{:S(2)}, u32[]{:S(2)}) collective-permute-start(bf16[64,4096]{1,0:T(8,128)(2,1)S(1)} %add_convert_fusion.2), channel_id=1, source_target_pairs={{0,16},{4,12},{8,24},{12,4},{16,0},{20,28},{24,8},{28,20},{1,17},{... | collective-permute-start | bytes 1572872 | tf_op jit(solution)/shard_map/ppermute | solution.py:35
  241.7 10.8 %collective-permute-start.30 = (bf16[64,4096]{1,0:T(8,128)(2,1)S(1)}, bf16[64,4096]{1,0:T(8,128)(2,1)S(1)}, u32[]{:S(2)}, u32[]{:S(2)}) collective-permute-start(bf16[64,4096]{1,0:T(8,128)(2,1)S(1)} %add_convert_fusion.12), channel_id=1, source_target_pairs={{0,4},{4,0},{8,12},{12,8},{16,20},{20,16},{24,28},{28,24},{1,5},{5... | collective-permute-start | bytes 1572872 | tf_op jit(solution)/shard_map/ppermute | solution.py:19
  241.9 3.5 %collective-permute-start.47 = (bf16[64,4096]{1,0:T(8,128)(2,1)S(1)}, bf16[64,4096]{1,0:T(8,128)(2,1)S(1)}, u32[]{:S(2)}, u32[]{:S(2)}) collective-permute-start(bf16[64,4096]{1,0:T(8,128)(2,1)S(1)} %add_convert_fusion.5), channel_id=1, source_target_pairs={{0,4},{4,0},{8,12},{12,8},{16,20},{20,16},{24,28},{28,24},{1,5},{5... | collective-permute-start | bytes 1572872 | tf_op jit(solution)/shard_map/ppermute | solution.py:19
  242.6 9.5 %collective-permute-start.51 = (bf16[64,4096]{1,0:T(8,128)(2,1)S(1)}, bf16[64,4096]{1,0:T(8,128)(2,1)S(1)}, u32[]{:S(2)}, u32[]{:S(2)}) collective-permute-start(bf16[64,4096]{1,0:T(8,128)(2,1)S(1)} %add_convert_fusion.1), channel_id=1, source_target_pairs={{0,8},{4,20},{8,0},{12,28},{16,24},{20,4},{24,16},{28,12},{1,9},{5... | collective-permute-start | bytes 1572872 | tf_op jit(solution)/shard_map/ppermute | solution.py:35
  245.2 12.6 %collective-permute-start.34 = (bf16[64,4096]{1,0:T(8,128)(2,1)S(1)}, bf16[64,4096]{1,0:T(8,128)(2,1)S(1)}, u32[]{:S(2)}, u32[]{:S(2)}) collective-permute-start(bf16[64,4096]{1,0:T(8,128)(2,1)S(1)} %add_convert_fusion.8), channel_id=1, source_target_pairs={{0,8},{4,20},{8,0},{12,28},{16,24},{20,4},{24,16},{28,12},{1,9},{5... | collective-permute-start | bytes 1572872 | tf_op jit(solution)/shard_map/ppermute | solution.py:35
  252.4 7.2 %collective-permute-start.52 = (bf16[32,4096]{1,0:T(8,128)(2,1)S(1)}, bf16[32,4096]{1,0:T(8,128)(2,1)S(1)}, u32[]{:S(2)}, u32[]{:S(2)}) collective-permute-start(bf16[32,4096]{1,0:T(8,128)(2,1)S(1)} %slice.19), channel_id=1, source_target_pairs={{0,1},{1,0},{2,3},{3,2},{4,5},{5,4},{6,7},{7,6},{8,9},{9,8},{10,11... | collective-permute-start | bytes 786440 | tf_op jit(solution)/shard_map/ppermute | solution.py:23
  258.0 12.3 %collective-permute-start.35 = (bf16[32,4096]{1,0:T(8,128)(2,1)S(1)}, bf16[32,4096]{1,0:T(8,128)(2,1)S(1)}, u32[]{:S(2)}, u32[]{:S(2)}) collective-permute-start(bf16[32,4096]{1,0:T(8,128)(2,1)S(1)} %slice.17), channel_id=1, source_target_pairs={{0,1},{1,0},{2,3},{3,2},{4,5},{5,4},{6,7},{7,6},{8,9},{9,8},{10,11... | collective-permute-start | bytes 786440 | tf_op jit(solution)/shard_map/ppermute | solution.py:23
  259.7 13.0 %copy-start.23 = (bf16[32,4096]{1,0:T(8,128)(2,1)S(1)}, bf16[32,4096]{1,0:T(8,128)(2,1)}, u32[]{:S(2)}) copy-start(bf16[32,4096]{1,0:T(8,128)(2,1)} %copy-done.22) | copy-start | bytes 786436
  259.7 13.0 %collective-permute-start.53 = (bf16[32,4096]{1,0:T(8,128)(2,1)S(1)}, bf16[32,4096]{1,0:T(8,128)(2,1)S(1)}, u32[]{:S(2)}, u32[]{:S(2)}) collective-permute-start(bf16[32,4096]{1,0:T(8,128)(2,1)S(1)} %add_convert_fusion.15), channel_id=1, source_target_pairs={{0,2},{1,3},{2,0},{3,1},{4,6},{5,7},{6,4},{7,5},{8,10},{9,11},{10,... | collective-permute-start | bytes 786440 | tf_op jit(solution)/shard_map/ppermute | solution.py:23
  (24 other events, 73.1 us)

commit v3 on v2

--- a/solution.py
+++ b/solution.py
@@ -82,15 +82,32 @@
 
 def widen_kernel(small_ref, wide_ref):
     wide_ref[...] = jnp.zeros_like(wide_ref)
-    wide_ref[:, : small_ref.shape[1]] = small_ref[...]
+    wide_ref[: small_ref.shape[0]] = small_ref[...]
 
 
 def widen(router):
     return pl.pallas_call(
         widen_kernel,
-        out_shape=jax.ShapeDtypeStruct((router.shape[0], HEAD_SIZE), router.dtype),
+        out_shape=jax.ShapeDtypeStruct((16, router.shape[1]), router.dtype),
         name="widen",
     )(router)
+
+
+def pack_kernel(cache_ref, new_ref, held_ref):
+    cached = cache_ref.shape[1]
+    held_ref[:, :cached] = cache_ref[...]
+    held_ref[:, cached:] = new_ref[...]
+
+
+def pack(cache, keys_values):
+    count = cache.shape[1] + keys_values.shape[1]
+    in_place = lambda a: pltpu.with_memory_space_constraint(a, pltpu.HBM)
+    return pl.pallas_call(
+        pack_kernel,
+        out_shape=jax.ShapeDtypeStruct((2, count, cache.shape[2]), cache.dtype),
+        compiler_params=pltpu.CompilerParams(vmem_limit_bytes=8 << 20),
+        name="pack",
+    )(in_place(cache), in_place(keys_values))
 
 
 def relay_kernel(in_ref, out_ref):
@@ -108,25 +125,24 @@
     )(place)
 
 
-def rise_kernel(parts, planes, place, router_ref, *refs):
-    tag_refs, rows_refs = refs[:parts], refs[parts : 2 * parts]
-    gate_ref, up_ref, hidden_ref, turned_ref, rows_all, weight_ref, tags_ref = refs[2 * parts :]
+def rise_kernel(parts, place, router_ref, *refs):
+    rows_refs = refs[:parts]
+    gate_ref, up_ref, hidden_ref, turned_ref, rows_all, weight_ref, tags_ref = refs[parts:]
+    width = rows_all.shape[1]
 
     @pl.when(pl.program_id(0) == 0)
     def _():
         at = 0
         for ref in rows_refs:
-            rows_all[at : at + ref.shape[0]] = ref[...]
+            rows_all[at : at + ref.shape[0]] = ref[:, :width]
+            tags_ref[at : at + ref.shape[0]] = ref[:, width:]
             at += ref.shape[0]
-        first_plane, last_plane, length = planes
-        at = 0
-        for ref in tag_refs:
-            for base in range(0, ref.shape[0], length[0]):
-                for k in range(first_plane, last_plane):
-                    start = base + k * length[1]
-                    tags_ref[at : at + length[1]] = ref[start : start + length[1]]
-                    at += length[1]
-        logits = jnp.dot(rows_all[...], router_ref[...], preferred_element_type=jnp.float32)
+        logits = lax.dot_general(
+            rows_all[...],
+            router_ref[...],
+            (((1,), (1,)), ((), ())),
+            preferred_element_type=jnp.float32,
+        )
         lane = lax.broadcasted_iota(jnp.int32, logits.shape, 1).astype(jnp.float32)
         tags = tags_ref[...].astype(jnp.float32)
         one, two = tags[:, :1], tags[:, 1:2]
@@ -146,13 +162,8 @@
     turned_ref[...] = hidden.T
 
 
-def rise(place, grads, planes, router, rows, gate_mat, up_mat):
+def rise(place, router, rows, gate_mat, up_mat):
     width, units = gate_mat.shape
-    tag = lambda g: pl.BlockSpec(
-        (g.shape[0], HEAD_SIZE),
-        lambda i, place: (0, width // HEAD_SIZE),
-        pipeline_mode=pl.Buffered(1),
-    )
     count = sum(r.shape[0] for r in rows)
     wide = min(256, units)
     whole = lambda shape: pl.BlockSpec(
@@ -160,7 +171,7 @@
     )
     column = lambda i, place: (0, i)
     return pl.pallas_call(
-        functools.partial(rise_kernel, len(rows), planes),
+        functools.partial(rise_kernel, len(rows)),
         out_shape=[
             jax.ShapeDtypeStruct((count, units), jnp.bfloat16),
             jax.ShapeDtypeStruct((units, count), jnp.bfloat16),
@@ -169,7 +180,6 @@
             num_scalar_prefetch=1,
             grid=(units // wide,),
             in_specs=[whole(router.shape)]
-            + [tag(g) for g in grads]
             + [whole(r.shape) for r in rows]
             + [pl.BlockSpec((width, wide), column)] * 2,
             out_specs=[
@@ -189,7 +199,7 @@
             bytes_accessed=2 * (2 * width * units + count * width),
         ),
         name="rise",
-    )(place, router, *grads, *rows, gate_mat, up_mat)
+    )(place, router, *rows, gate_mat, up_mat)
 
 
 def fall_kernel(hidden_ref, down_ref, *part_refs):
@@ -476,7 +486,7 @@
         return jnp.stack(new + old).astype(jnp.int32)
 
     stage = functools.partial(attend, query, cached=cached, window_free=window_free)
-    own = jnp.concatenate([cache, keys_values], axis=1)
+    own = pack(cache, keys_values)
     bits = link_bits()
     if len(bits) != 2:
         held = [(own, 0)]
@@ -529,14 +539,13 @@
     plane = lax.axis_index("exp")
     row_count, width = residual.shape
 
-    tags = jnp.pad(expert_ids.astype(jnp.bfloat16), ((0, 0), (0, HEAD_SIZE - 2)))
-    tagged = planes_of(jnp.concatenate([cotangent, tags], axis=1), False)
-    grads = gather(jnp.concatenate(tagged, axis=0))
-    tall_router = widen(router)
+    grads = gather(jnp.concatenate(planes_of(cotangent, False), axis=0))
 
     attn = attention(query, keys_values, cache)
 
     place = jnp.full((1,), plane, jnp.int32)
+    marked = relay(place)
+    marked = relay(marked)
     hidden_one, *shares = project(
         place, attn, pltpu.with_memory_space_constraint(out_proj, pltpu.HBM), residual
     )
@@ -553,16 +562,21 @@
     gate_mat = in_place(w_gate[0])
     up_mat = in_place(w_up[0])
     down_mat = in_place(w_down[0])
-    blocks = planes_of(normed, True)
-    place = relay(place)
+    tags = jnp.pad(expert_ids.astype(jnp.bfloat16), ((0, 0), (0, HEAD_SIZE - 2)))
+    blocks = planes_of(jnp.concatenate([normed, tags], axis=1), True)
+    tall_router = widen(router.T)
     hidden, turned, counts = [], [], []
     for k in range(0, planes, 2):
-        rows = gather(jnp.concatenate(blocks[k : k + 2], axis=0))
-        piece = (k, k + 2, (planes * row_count, row_count))
-        plain, flipped = rise(place, grads, piece, tall_router, rows, gate_mat, up_mat)
+        if k == 0 and len(link_bits()) == 2:
+            near = zip(gather(blocks[0]), gather(blocks[1]))
+            rows = [part for both in near for part in both]
+        else:
+            rows = gather(jnp.concatenate(blocks[k : k + 2], axis=0))
+        plain, flipped = rise(marked, tall_router, rows, gate_mat, up_mat)
         hidden.append(plain)
         turned.append(flipped)
-        counts.append([r.shape[0] for r in rows])
+        pieces = 8 if len(link_bits()) == 2 else 1
+        counts.append([plain.shape[0] // pieces] * pieces)
     layer = hidden_one
     for k in range(0, planes, 2):
         parts = fall(hidden[k // 2], down_mat, counts[k // 2])

time: 274 us -> 255 us (0.931)
  local copies, waits for them, and re-layouts: 17.7 us -> 4.61 us
  waiting for transfers between devices: 120 us -> 114 us
  Pallas kernels: 81.6 us -> 78.2 us
  starting transfers between devices: 48.7 us -> 51.8 us
    ppermute x12, waiting for transfers between devices: 49.8 us -> 35.7 us  [swap_plane(): lax.ppermute(value, 'exp', [(i, i ^ bits) for i in range(lax.axis_size('e...]
    unnamed x71 -> x30, local copies, waits for them, and re-layouts: 16.1 us -> 3.81 us
    ppermute x18 -> x21, waiting for transfers between devices: 70.2 us -> 74.6 us  [cross(): return lax.ppermute(value, 'ctx', pairs)]
    ppermute x24 -> x28, waiting for transfers between devices: 0.06 us -> 3.9 us  [swap(): lax.ppermute(value, 'ctx', [(i, i ^ bit) for i in range(lax.axis_size('ct...]
    pallas_call x2, Pallas kernels: 16.4 us -> 13.5 us  [outer(): pl.pallas_call(functools.partial(outer_kernel, len(grads), pieces, blocks...]
    ppermute x18 -> x21, starting transfers between devices: 26.2 us -> 28.4 us  [cross(): return lax.ppermute(value, 'ctx', pairs)]
    pallas_call x3 -> x4, Pallas kernels: 33.1 us -> 31.6 us  [the longest x2 29.1 us: rise(): pl.pallas_call(functools.partial(rise_kernel, len(rows)), out_shape=[jax....]
    ppermute x24 -> x28, starting transfers between devices: 5.24 us -> 6.15 us  [swap(): lax.ppermute(value, 'ctx', [(i, i ^ bit) for i in range(lax.axis_size('ct...]
  transfers between devices with their start and end apart: 54 -> 61, of which waited for: 23 -> 22; matrix products, arithmetic and copies ran while one was open for 2% -> 2% of each run, Pallas kernels for 25% -> 30%
where the time goes in v3:
time: 255 us; the launch traced here: 254 us
  waiting for transfers between devices  114 us (45%)
  Pallas kernels  78.2 us (31%)
  starting transfers between devices  51.8 us (20%)
  local copies, waits for them, and re-layouts  4.61 us (2%)
  other arithmetic  4.2 us (2%)
    ppermute x21, waiting for transfers between devices, cross(): return lax.ppermute(value, 'ctx', pairs)  74.6 us
    ppermute x12, waiting for transfers between devices, swap_plane(): lax.ppermute(value, 'exp', [(i, i ^ bits) for i in range(lax.axis_size('e...  35.7 us
    pallas_call x2, Pallas kernels, rise(): pl.pallas_call(functools.partial(rise_kernel, len(rows)), out_shape=[jax....  29.1 us
    ppermute x21, starting transfers between devices, cross(): return lax.ppermute(value, 'ctx', pairs)  28.4 us
    ppermute x12, starting transfers between devices, swap_plane(): lax.ppermute(value, 'exp', [(i, i ^ bits) for i in range(lax.axis_size('e...  17.3 us
    pallas_call x2, Pallas kernels, fall(): pl.pallas_call(fall_kernel, out_shape=[jax.ShapeDtypeStruct((c, width), j...  14.6 us
    pallas_call x2, Pallas kernels, outer(): pl.pallas_call(functools.partial(outer_kernel, len(grads), pieces, blocks...  13.5 us
    pallas_call x2, Pallas kernels, attend(): pl.pallas_call(functools.partial(attend_kernel, slots, cached, window_fre...  11.8 us
  transfers between devices with their start and end apart: 61, of which 22 were waited for; matrix products, arithmetic and copies ran while one was open for 2% of the time, Pallas kernels for 30%

profile of v3, /device:TPU:0, one launch (start us, length us, event | category | flops | bytes accessed | tf_op | source)
XLA Modules:
  0.0 254.1 jit_solution(4171774317023366202)
XLA Ops:
  0.6 1.1 pack.1.refs_2_.refs_4_
  2.3 2.6 %collective-permute-start = (bf16[2,384,256]{2,1,0:T(8,128)(2,1)S(1)}, bf16[2,384,256]{2,1,0:T(8,128)(2,1)S(1)}, u32[]{:S(2)}, u32[]{:S(2)}) collective-permute-start(bf16[2,384,256]{2,1,0:T(8,128)(2,1)S(1)} %pack.1.refs_2_.refs_4_), channel_id=1, source_target_pairs={{0,8},{4,20},{8,0},{12,28},{16,24},{20,4},{24,16},{28,12},{1,9},{5... | collective-permute-start | bytes 1179656 | tf_op jit(solution)/shard_map/ppermute | solution.py:35
  4.8 1.6 collective-permute-start.2
  6.5 4.1 %collective-permute-done.refs_2_.refs_8_ = bf16[2,384,256]{2,1,0:T(8,128)(2,1)S(1)} collective-permute-done((bf16[2,384,256]{2,1,0:T(8,128)(2,1)S(1)}, bf16[2,384,256]{2,1,0:T(8,128)(2,1)S(1)}, u32[]{:S(2)}, u32[]{:S(2)}) %collective-permute-start) | collective-permute-done | bytes 393248 | tf_op jit(solution)/shard_map/ppermute | solution.py:35
  10.6 2.0 collective-permute-start.5
  12.6 3.9 %collective-permute-done.2.refs_3_.refs_9_ = bf16[2,384,256]{2,1,0:T(8,128)(2,1)S(1)} collective-permute-done((bf16[2,384,256]{2,1,0:T(8,128)(2,1)S(1)}, bf16[2,384,256]{2,1,0:T(8,128)(2,1)S(1)}, u32[]{:S(2)}, u32[]{:S(2)}) %collective-permute-start.2) | collective-permute-done | bytes 393248 | tf_op jit(solution)/shard_map/ppermute | solution.py:35
  16.5 2.2 collective-permute-done.5.refs_6_.refs_12_
  18.9 3.1 %collective-permute-start.52 = (bf16[32,4096]{1,0:T(8,128)(2,1)}, bf16[32,4096]{1,0:T(8,128)(2,1)}, u32[]{:S(2)}, u32[]{:S(2)}) collective-permute-start(bf16[32,4096]{1,0:T(8,128)(2,1)} %param.23), channel_id=1, source_target_pairs={{0,2},{1,3},{2,0},{3,1},{4,6},{5,7},{6,4},{7,5},{8,10},{9,11},{10,... | collective-permute-start | bytes 786440 | tf_op jit(solution)/shard_map/ppermute | solution.py:23
  21.9 1.6 collective-permute-start.51
  24.0 1.2 relay.3.place
  25.2 0.7 convert_element_type.178
  26.0 1.4 widen.1.router_ref
  27.4 0.6 stack.63.refs_0_
  28.7 4.2 %attend.2 = (f32[2,512,128]{2,1,0:T(8,128)}, f32[2,512,128]{2,1,0:T(8,128)}, f32[2,512,128]{2,1,0:T(8,128)}) custom-call(s32[4]{0:T(128)} %pad_add_fusion.refs_0_, bf16[128,1024]{1,0:T(8,128)(2,1)} %refs_1_.3, bf16[2,384,256]{2,1,0:T(8,128)(2,1)} %copy-done, bf16[2,384,256]{2,1,0:T(8,128)(2,1)} %copy-done.4, bf16[2,384,256]{2,1,0:T(8,128)(2,1)} %copy-done, ...), custom_call_target="tpu_custom_call" | custom-call | flops 402653184 | bytes 1572864 | tf_op jit(solution)/shard_map/attend/pallas_call | solution.py:456
  33.0 0.6 copy-done.8
  33.9 7.6 %attend.3.attn_ref = bf16[128,1024]{1,0:T(8,128)(2,1)} custom-call(s32[12]{0:T(128)} %stack.63.refs_0_, bf16[128,1024]{1,0:T(8,128)(2,1)} %refs_1_.3, bf16[2,384,256]{2,1,0:T(8,128)(2,1)} %copy-done.5, bf16[2,384,256]{2,1,0:T(8,128)(2,1)} %copy-done.6, bf16[2,384,256]{2,1,0:T(8,128)(2,1)} %copy-done.8, bf16[2,384,256]{2,1,0:T(8,128)(2,1)} %copy-done.9, ...), custom_call_target="tpu_custom_call" | custom-call | flops 1207959552 | bytes 4718592 | tf_op jit(solution)/shard_map/attend/pallas_call | solution.py:456
  41.5 0.9 copy-done.1
  42.4 5.1 %project.1 = (f32[32,4096]{1,0:T(8,128)S(1)}, bf16[32,4096]{1,0:T(8,128)(2,1)S(1)}, f32[32,4096]{1,0:T(8,128)S(1)}, bf16[32,4096]{1,0:T(8,128)(2,1)S(1)}) custom-call(s32[1]{0:T(128)} %bitcast.place.in_ref, bf16[128,1024]{1,0:T(8,128)(2,1)S(1)} %copy-done.1, bf16[1024,4096]{1,0:T(8,128)(2,1)} %proj_ref.1, bf16[32,4096]{1,0:T(8,128)(2,1)S(1)} %copy-done.2), custom_call_target="tpu_custom_call" | custom-call | flops 1073741824 | bytes 8388608 | tf_op jit(solution)/shard_map/project/pallas_call | solution.py:257
  47.5 0.9 collective-permute-start.8
  48.4 1.3 collective-permute-start.7
  49.7 7.1 %collective-permute-done.8 = bf16[32,4096]{1,0:T(8,128)(2,1)S(1)} collective-permute-done((bf16[32,4096]{1,0:T(8,128)(2,1)S(1)}, bf16[32,4096]{1,0:T(8,128)(2,1)S(1)}, u32[]{:S(2)}, u32[]{:S(2)}) %collective-permute-start.8) | collective-permute-done | bytes 262176 | tf_op jit(solution)/shard_map/ppermute | solution.py:23
  56.8 2.4 collective-permute-start.9
  59.2 1.0 constant_dynamic-update-slice_fusion.4
  60.1 5.1 %collective-permute-done.7 = bf16[32,4096]{1,0:T(8,128)(2,1)S(1)} collective-permute-done((bf16[32,4096]{1,0:T(8,128)(2,1)S(1)}, bf16[32,4096]{1,0:T(8,128)(2,1)S(1)}, u32[]{:S(2)}, u32[]{:S(2)}) %collective-permute-start.7) | collective-permute-done | bytes 262176 | tf_op jit(solution)/shard_map/ppermute | solution.py:23
  65.3 5.8 %collective-permute-done.9 = bf16[32,4096]{1,0:T(8,128)(2,1)S(1)} collective-permute-done((bf16[32,4096]{1,0:T(8,128)(2,1)S(1)}, bf16[32,4096]{1,0:T(8,128)(2,1)S(1)}, u32[]{:S(2)}, u32[]{:S(2)}) %collective-permute-start.9) | collective-permute-done | bytes 262176 | tf_op jit(solution)/shard_map/ppermute | solution.py:23
  71.6 5.3 %collective-permute-start.10 = (bf16[32,4224]{1,0:T(8,128)(2,1)S(1)}, bf16[32,4224]{1,0:T(8,128)(2,1)S(1)}, u32[]{:S(2)}, u32[]{:S(2)}) collective-permute-start(bf16[32,4224]{1,0:T(8,128)(2,1)S(1)} %fusion.1.refs_0_), channel_id=1, source_target_pairs={{0,1},{1,0},{2,3},{3,2},{4,5},{5,4},{6,7},{7,6},{8,9},{9,8},{10,11... | collective-permute-start | bytes 811016 | tf_op jit(solution)/shard_map/ppermute | solution.py:23
  76.9 1.0 constant_dynamic-update-slice_fusion.3
  77.8 1.6 collective-permute-start.13
  79.4 2.9 %collective-permute-done.10.refs_1_ = bf16[32,4224]{1,0:T(8,128)(2,1)S(1)} collective-permute-done((bf16[32,4224]{1,0:T(8,128)(2,1)S(1)}, bf16[32,4224]{1,0:T(8,128)(2,1)S(1)}, u32[]{:S(2)}, u32[]{:S(2)}) %collective-permute-start.10) | collective-permute-done | bytes 270368 | tf_op jit(solution)/shard_map/ppermute | solution.py:23
  82.3 3.4 %collective-permute-start.14 = (bf16[32,4224]{1,0:T(8,128)(2,1)S(1)}, bf16[32,4224]{1,0:T(8,128)(2,1)S(1)}, u32[]{:S(2)}, u32[]{:S(2)}) collective-permute-start(bf16[32,4224]{1,0:T(8,128)(2,1)S(1)} %collective-permute-done.10.refs_1_), channel_id=1, source_target_pairs={{0,8},{4,20},{8,0},{12,28},{16,24},{20,4},{24,16},{28,12},{1,9},{5... | collective-permute-start | bytes 811016 | tf_op jit(solution)/shard_map/ppermute | solution.py:35
  86.3 1.5 collective-permute-start.17
  87.8 6.8 %collective-permute-done.34 = bf16[32,4224]{1,0:T(8,128)(2,1)S(1)} collective-permute-done((bf16[32,4224]{1,0:T(8,128)(2,1)S(1)}, bf16[32,4224]{1,0:T(8,128)(2,1)S(1)}, u32[]{:S(2)}, u32[]{:S(2)}) %collective-permute-start.34) | collective-permute-done | bytes 270368 | tf_op jit(solution)/shard_map/ppermute | solution.py:23
  94.6 2.0 collective-permute-start.18
  96.6 1.5 collective-permute-start.16
  98.7 5.0 %collective-permute-done.15.refs_6_ = bf16[32,4224]{1,0:T(8,128)(2,1)S(1)} collective-permute-done((bf16[32,4224]{1,0:T(8,128)(2,1)S(1)}, bf16[32,4224]{1,0:T(8,128)(2,1)S(1)}, u32[]{:S(2)}, u32[]{:S(2)}) %collective-permute-start.15) | collective-permute-done | bytes 270368 | tf_op jit(solution)/shard_map/ppermute | solution.py:35
  104.3 2.4 collective-permute-done.16.refs_7_
  107.5 1.4 collective-permute-start.36
  108.9 14.5 %rise.2 = (bf16[512,1024]{1,0:T(8,128)(2,1)S(1)}, bf16[1024,512]{1,0:T(8,128)(2,1)S(1)}) custom-call(s32[1]{0:T(128)} %relay.3.place, bf16[16,4096]{1,0:T(8,128)(2,1)S(1)} %copy-done.3, bf16[32,4224]{1,0:T(8,128)(2,1)S(1)} %fusion.1.refs_0_, bf16[32,4224]{1,0:T(8,128)(2,1)S(1)} %collective-permute-done.10.refs_1_, ...), custom_call_target="tpu_custom_call" | custom-call | flops 8589934592 | bytes 20971520 | tf_op jit(solution)/shard_map/rise/pallas_call | solution.py:173
  123.4 7.3 %fall.2 = (bf16[64,4096]{1,0:T(8,128)(2,1)S(1)}, bf16[64,4096]{1,0:T(8,128)(2,1)S(1)}, bf16[64,4096]{1,0:T(8,128)(2,1)S(1)}, bf16[64,4096]{1,0:T(8,128)(2,1)S(1)...) custom-call(bf16[512,1024]{1,0:T(8,128)(2,1)S(1)} %get-tuple-element, ...), custom_call_target="tpu_custom_call" | custom-call | flops 4294967296 | bytes 12582912 | tf_op jit(solution)/shard_map/fall/pallas_call | solution.py:218
  131.8 1.7 collective-permute-start.56
  134.0 1.4 collective-permute-start.37
  135.6 32.8 %collective-permute-done.38.refs_4_ = bf16[64,4224]{1,0:T(8,128)(2,1)S(1)} collective-permute-done((bf16[64,4224]{1,0:T(8,128)(2,1)S(1)}, bf16[64,4224]{1,0:T(8,128)(2,1)S(1)}, u32[]{:S(2)}, u32[]{:S(2)}) %collective-permute-start.38) | collective-permute-done | bytes 540704 | tf_op jit(solution)/shard_map/ppermute | solution.py:35
  169.7 0.6 collective-permute-done.41.refs_7_
  170.5 0.6 collective-permute-done.40.refs_6_
  171.6 14.7 %rise.3 = (bf16[512,1024]{1,0:T(8,128)(2,1)S(1)}, bf16[1024,512]{1,0:T(8,128)(2,1)S(1)}) custom-call(s32[1]{0:T(128)} %relay.3.place, bf16[16,4096]{1,0:T(8,128)(2,1)S(1)} %copy-done.3, bf16[64,4224]{1,0:T(8,128)(2,1)S(1)} %constant_dynamic-update-slice_fusion.refs_0_, bf16[64,4224]{1,0:T(8,128)(2,1)S(1)} %collective-permute-done.35.refs_1_, ...), custom_call_target="tpu_custom_call" | custom-call | flops 8589934592 | bytes 20971520 | tf_op jit(solution)/shard_map/rise/pallas_call | solution.py:173
  186.3 7.3 %fall.3 = (bf16[64,4096]{1,0:T(8,128)(2,1)S(1)}, bf16[64,4096]{1,0:T(8,128)(2,1)S(1)}, bf16[64,4096]{1,0:T(8,128)(2,1)S(1)}, bf16[64,4096]{1,0:T(8,128)(2,1)S(1)...) custom-call(bf16[512,1024]{1,0:T(8,128)(2,1)S(1)} %get-tuple-element, ...), custom_call_target="tpu_custom_call" | custom-call | flops 4294967296 | bytes 12582912 | tf_op jit(solution)/shard_map/fall/pallas_call | solution.py:218
  194.4 1.1 collective-permute-done.42
  196.0 1.5 collective-permute-done.46
  197.4 1.4 collective-permute-start.43
  199.0 7.7 %collective-permute-done.43 = bf16[64,4096]{1,0:T(8,128)(2,1)S(1)} collective-permute-done((bf16[64,4096]{1,0:T(8,128)(2,1)S(1)}, bf16[64,4096]{1,0:T(8,128)(2,1)S(1)}, u32[]{:S(2)}, u32[]{:S(2)}) %collective-permute-start.43) | collective-permute-done | bytes 524320 | tf_op jit(solution)/shard_map/ppermute | solution.py:35
  206.6 1.5 collective-permute-start.47
  208.3 1.0 collective-permute-start.26
  209.3 11.7 %collective-permute-done.47 = bf16[64,4096]{1,0:T(8,128)(2,1)S(1)} collective-permute-done((bf16[64,4096]{1,0:T(8,128)(2,1)S(1)}, bf16[64,4096]{1,0:T(8,128)(2,1)S(1)}, u32[]{:S(2)}, u32[]{:S(2)}) %collective-permute-start.47) | collective-permute-done | bytes 524320 | tf_op jit(solution)/shard_map/ppermute | solution.py:35
  221.3 0.9 collective-permute-start.48
  222.9 1.1 collective-permute-start.31
  223.9 6.7 %outer.2.refs_10_ = f32[1024,4096]{1,0:T(8,128)} custom-call(bf16[128,4096]{1,0:T(8,128)(2,1)S(1)} %constant_dynamic-update-slice_fusion.2.refs_0_, bf16[128,4096]{1,0:T(8,128)(2,1)S(1)} %collective-permute-done.54.refs_1_, bf16[128,4096]{1,0:T(8,128)(2,1)S(1)} %collective-permute-done.55.refs_2_, bf16[128,4096]{1,0:T(8,128)(2,1)S(1)} %collective-permute-done.56.refs_3_, ...), custom_call_target="tpu_custom_call" | custom-call | flops 4294967296 | bytes 16777216 | tf_op jit(solution)/shard_map/outer/pallas_call | solution.py:314
  230.9 0.6 collective-permute-start.49
  231.5 4.6 %collective-permute-done.31 = bf16[64,4096]{1,0:T(8,128)(2,1)S(1)} collective-permute-done((bf16[64,4096]{1,0:T(8,128)(2,1)S(1)}, bf16[64,4096]{1,0:T(8,128)(2,1)S(1)}, u32[]{:S(2)}, u32[]{:S(2)}) %collective-permute-start.31) | collective-permute-done | bytes 524320 | tf_op jit(solution)/shard_map/ppermute | solution.py:35
  236.4 0.6 collective-permute-start.32
  237.0 2.8 %collective-permute-done.49 = bf16[32,4096]{1,0:T(8,128)(2,1)S(1)} collective-permute-done((bf16[32,4096]{1,0:T(8,128)(2,1)S(1)}, bf16[32,4096]{1,0:T(8,128)(2,1)S(1)}, u32[]{:S(2)}, u32[]{:S(2)}) %collective-permute-start.49) | collective-permute-done | bytes 262176 | tf_op jit(solution)/shard_map/ppermute | solution.py:23
  239.8 1.4 collective-permute-start.50
  241.2 6.7 %outer.3 = f32[1024,4096]{1,0:T(8,128)} custom-call(bf16[128,4096]{1,0:T(8,128)(2,1)S(1)} %constant_dynamic-update-slice_fusion.2.refs_0_, bf16[128,4096]{1,0:T(8,128)(2,1)S(1)} %collective-permute-done.54.refs_1_, bf16[128,4096]{1,0:T(8,128)(2,1)S(1)} %collective-permute-done.55.refs_2_, ...), custom_call_target="tpu_custom_call", output_to_operand_aliasing={{}: (10, {})} | custom-call | flops 4294967296 | bytes 16777216 | tf_op jit(solution)/shard_map/outer/pallas_call | solution.py:314
  248.5 4.7 %collective-permute-done.50 = bf16[32,4096]{1,0:T(8,128)(2,1)S(1)} collective-permute-done((bf16[32,4096]{1,0:T(8,128)(2,1)S(1)}, bf16[32,4096]{1,0:T(8,128)(2,1)S(1)}, u32[]{:S(2)}, u32[]{:S(2)}) %collective-permute-start.50) | collective-permute-done | bytes 262176 | tf_op jit(solution)/shard_map/ppermute | solution.py:23
  253.2 0.9 add_convert_fusion.14
  (126 shorter events, 12.6 us)
Async XLA Ops:
  0.6 40.8 %copy-start.2 = (bf16[32,4096]{1,0:T(8,128)(2,1)S(1)}, bf16[32,4096]{1,0:T(8,128)(2,1)}, u32[]{:S(2)}) copy-start(bf16[32,4096]{1,0:T(8,128)(2,1)} %residual_ref.1) | copy-start | bytes 786436
  1.7 3.1 %collective-permute-start.1 = (bf16[2,384,256]{2,1,0:T(8,128)(2,1)S(1)}, bf16[2,384,256]{2,1,0:T(8,128)(2,1)S(1)}, u32[]{:S(2)}, u32[]{:S(2)}) collective-permute-start(bf16[2,384,256]{2,1,0:T(8,128)(2,1)S(1)} %pack.1.refs_2_.refs_4_), channel_id=1, source_target_pairs={{0,4},{4,0},{8,12},{12,8},{16,20},{20,16},{24,28},{28,24},{1,5},{5... | collective-permute-start | bytes 1179656 | tf_op jit(solution)/shard_map/ppermute | solution.py:19
  2.3 8.3 %collective-permute-start = (bf16[2,384,256]{2,1,0:T(8,128)(2,1)S(1)}, bf16[2,384,256]{2,1,0:T(8,128)(2,1)S(1)}, u32[]{:S(2)}, u32[]{:S(2)}) collective-permute-start(bf16[2,384,256]{2,1,0:T(8,128)(2,1)S(1)} %pack.1.refs_2_.refs_4_), channel_id=1, source_target_pairs={{0,8},{4,20},{8,0},{12,28},{16,24},{20,4},{24,16},{28,12},{1,9},{5... | collective-permute-start | bytes 1179656 | tf_op jit(solution)/shard_map/ppermute | solution.py:35
  4.8 11.7 %collective-permute-start.2 = (bf16[2,384,256]{2,1,0:T(8,128)(2,1)S(1)}, bf16[2,384,256]{2,1,0:T(8,128)(2,1)S(1)}, u32[]{:S(2)}, u32[]{:S(2)}) collective-permute-start(bf16[2,384,256]{2,1,0:T(8,128)(2,1)S(1)} %collective-permute-done.1.refs_3_.refs_5_), channel_id=1, source_target_pairs={{0,8},{4,20},{8,0},{12,28},{16,24},{20,4},{24,16},{28,12},{1,9},{5... | collective-permute-start | bytes 1179656 | tf_op jit(solution)/shard_map/ppermute | solution.py:35
  10.6 8.2 %collective-permute-start.5 = (bf16[2,384,256]{2,1,0:T(8,128)(2,1)S(1)}, bf16[2,384,256]{2,1,0:T(8,128)(2,1)S(1)}, u32[]{:S(2)}, u32[]{:S(2)}) collective-permute-start(bf16[2,384,256]{2,1,0:T(8,128)(2,1)S(1)} %collective-permute-done.refs_2_.refs_8_), channel_id=1, source_target_pairs={{0,16},{4,12},{8,24},{12,4},{16,0},{20,28},{24,8},{28,20},{1,17},{... | collective-permute-start | bytes 1179656 | tf_op jit(solution)/shard_map/ppermute | solution.py:35
  12.6 20.2 %collective-permute-start.3 = (bf16[2,384,256]{2,1,0:T(8,128)(2,1)S(1)}, bf16[2,384,256]{2,1,0:T(8,128)(2,1)S(1)}, u32[]{:S(2)}, u32[]{:S(2)}) collective-permute-start(bf16[2,384,256]{2,1,0:T(8,128)(2,1)S(1)} %collective-permute-done.refs_2_.refs_8_), channel_id=1, source_target_pairs={{0,4},{4,0},{8,12},{12,8},{16,20},{20,16},{24,28},{28,24},{1,5},{5... | collective-permute-start | bytes 1179656 | tf_op jit(solution)/shard_map/ppermute | solution.py:19
  16.5 16.4 %collective-permute-start.4 = (bf16[2,384,256]{2,1,0:T(8,128)(2,1)S(1)}, bf16[2,384,256]{2,1,0:T(8,128)(2,1)S(1)}, u32[]{:S(2)}, u32[]{:S(2)}) collective-permute-start(bf16[2,384,256]{2,1,0:T(8,128)(2,1)S(1)} %collective-permute-done.2.refs_3_.refs_9_), channel_id=1, source_target_pairs={{0,4},{4,0},{8,12},{12,8},{16,20},{20,16},{24,28},{28,24},{1,5},{5... | collective-permute-start | bytes 1179656 | tf_op jit(solution)/shard_map/ppermute | solution.py:19
  18.8 14.2 %collective-permute-start.6 = (bf16[2,384,256]{2,1,0:T(8,128)(2,1)S(1)}, bf16[2,384,256]{2,1,0:T(8,128)(2,1)S(1)}, u32[]{:S(2)}, u32[]{:S(2)}) collective-permute-start(bf16[2,384,256]{2,1,0:T(8,128)(2,1)S(1)} %collective-permute-done.5.refs_6_.refs_12_), channel_id=1, source_target_pairs={{0,4},{4,0},{8,12},{12,8},{16,20},{20,16},{24,28},{28,24},{1,5},{5... | collective-permute-start | bytes 1179656 | tf_op jit(solution)/shard_map/ppermute | solution.py:19
  18.9 58.0 %collective-permute-start.52 = (bf16[32,4096]{1,0:T(8,128)(2,1)}, bf16[32,4096]{1,0:T(8,128)(2,1)}, u32[]{:S(2)}, u32[]{:S(2)}) collective-permute-start(bf16[32,4096]{1,0:T(8,128)(2,1)} %param.23), channel_id=1, source_target_pairs={{0,2},{1,3},{2,0},{3,1},{4,6},{5,7},{6,4},{7,5},{8,10},{9,11},{10,... | collective-permute-start | bytes 786440 | tf_op jit(solution)/shard_map/ppermute | solution.py:23
  21.9 37.2 %collective-permute-start.51 = (bf16[32,4096]{1,0:T(8,128)(2,1)}, bf16[32,4096]{1,0:T(8,128)(2,1)}, u32[]{:S(2)}, u32[]{:S(2)}) collective-permute-start(bf16[32,4096]{1,0:T(8,128)(2,1)} %param.23), channel_id=1, source_target_pairs={{0,1},{1,0},{2,3},{3,2},{4,5},{5,4},{6,7},{7,6},{8,9},{9,8},{10,11... | collective-permute-start | bytes 786440 | tf_op jit(solution)/shard_map/ppermute | solution.py:23
  32.9 52.8 %collective-permute-start.53 = (bf16[32,4096]{1,0:T(8,128)(2,1)}, bf16[32,4096]{1,0:T(8,128)(2,1)S(1)}, u32[]{:S(2)}, u32[]{:S(2)}) collective-permute-start(bf16[32,4096]{1,0:T(8,128)(2,1)} %param.23), channel_id=1, source_target_pairs={{0,3},{1,2},{2,1},{3,0},{4,7},{5,6},{6,5},{7,4},{8,11},{9,10},{10,... | collective-permute-start | bytes 786440 | tf_op jit(solution)/shard_map/ppermute | solution.py:23
  33.9 37.4 %copy-start.12 = (f32[4096]{0:T(1024)S(1)}, f32[4096]{0:T(1024)}, u32[]{:S(2)}) copy-start(f32[4096]{0:T(1024)} %param.17) | copy-start | bytes 49156
  42.4 66.5 %copy-start.3 = (bf16[16,4096]{1,0:T(8,128)(2,1)S(1)}, bf16[16,4096]{1,0:T(8,128)(2,1)}, u32[]{:S(2)}) copy-start(bf16[16,4096]{1,0:T(8,128)(2,1)} %widen.1.router_ref) | copy-start | bytes 393220
  47.5 9.2 %collective-permute-start.8 = (bf16[32,4096]{1,0:T(8,128)(2,1)S(1)}, bf16[32,4096]{1,0:T(8,128)(2,1)S(1)}, u32[]{:S(2)}, u32[]{:S(2)}) collective-permute-start(bf16[32,4096]{1,0:T(8,128)(2,1)S(1)} %get-tuple-element.35), channel_id=1, source_target_pairs={{0,1},{1,0},{2,3},{3,2},{4,5},{5,4},{6,7},{7,6},{8,9},{9,8},{10,11... | collective-permute-start | bytes 786440 | tf_op jit(solution)/shard_map/ppermute | solution.py:23
  48.4 16.8 %collective-permute-start.7 = (bf16[32,4096]{1,0:T(8,128)(2,1)S(1)}, bf16[32,4096]{1,0:T(8,128)(2,1)S(1)}, u32[]{:S(2)}, u32[]{:S(2)}) collective-permute-start(bf16[32,4096]{1,0:T(8,128)(2,1)S(1)} %get-tuple-element.33), channel_id=1, source_target_pairs={{0,1},{1,0},{2,3},{3,2},{4,5},{5,4},{6,7},{7,6},{8,9},{9,8},{10,11... | collective-permute-start | bytes 786440 | tf_op jit(solution)/shard_map/ppermute | solution.py:23
  56.8 14.3 %collective-permute-start.9 = (bf16[32,4096]{1,0:T(8,128)(2,1)S(1)}, bf16[32,4096]{1,0:T(8,128)(2,1)S(1)}, u32[]{:S(2)}, u32[]{:S(2)}) collective-permute-start(bf16[32,4096]{1,0:T(8,128)(2,1)S(1)} %add_convert_fusion.17), channel_id=1, source_target_pairs={{0,2},{1,3},{2,0},{3,1},{4,6},{5,7},{6,4},{7,5},{8,10},{9,11},{10,... | collective-permute-start | bytes 786440 | tf_op jit(solution)/shard_map/ppermute | solution.py:23
  71.5 14.2 %collective-permute-start.33 = (bf16[32,4224]{1,0:T(8,128)(2,1)S(1)}, bf16[32,4224]{1,0:T(8,128)(2,1)S(1)}, u32[]{:S(2)}, u32[]{:S(2)}) collective-permute-start(bf16[32,4224]{1,0:T(8,128)(2,1)S(1)} %fusion.1.refs_0_), channel_id=1, source_target_pairs={{0,2},{1,3},{2,0},{3,1},{4,6},{5,7},{6,4},{7,5},{8,10},{9,11},{10,... | collective-permute-start | bytes 811016 | tf_op jit(solution)/shard_map/ppermute | solution.py:23
  71.6 10.7 %collective-permute-start.10 = (bf16[32,4224]{1,0:T(8,128)(2,1)S(1)}, bf16[32,4224]{1,0:T(8,128)(2,1)S(1)}, u32[]{:S(2)}, u32[]{:S(2)}) collective-permute-start(bf16[32,4224]{1,0:T(8,128)(2,1)S(1)} %fusion.1.refs_0_), channel_id=1, source_target_pairs={{0,1},{1,0},{2,3},{3,2},{4,5},{5,4},{6,7},{7,6},{8,9},{9,8},{10,11... | collective-permute-start | bytes 811016 | tf_op jit(solution)/shard_map/ppermute | solution.py:23
  77.8 8.0 %collective-permute-start.13 = (bf16[32,4224]{1,0:T(8,128)(2,1)S(1)}, bf16[32,4224]{1,0:T(8,128)(2,1)S(1)}, u32[]{:S(2)}, u32[]{:S(2)}) collective-permute-start(bf16[32,4224]{1,0:T(8,128)(2,1)S(1)} %fusion.1.refs_0_), channel_id=1, source_target_pairs={{0,8},{4,20},{8,0},{12,28},{16,24},{20,4},{24,16},{28,12},{1,9},{5... | collective-permute-start | bytes 811016 | tf_op jit(solution)/shard_map/ppermute | solution.py:35
  79.4 6.9 %collective-permute-start.11 = (bf16[32,4224]{1,0:T(8,128)(2,1)S(1)}, bf16[32,4224]{1,0:T(8,128)(2,1)S(1)}, u32[]{:S(2)}, u32[]{:S(2)}) collective-permute-start(bf16[32,4224]{1,0:T(8,128)(2,1)S(1)} %fusion.1.refs_0_), channel_id=1, source_target_pairs={{0,4},{4,0},{8,12},{12,8},{16,20},{20,16},{24,28},{28,24},{1,5},{5... | collective-permute-start | bytes 811016 | tf_op jit(solution)/shard_map/ppermute | solution.py:19
  82.3 12.3 %collective-permute-start.14 = (bf16[32,4224]{1,0:T(8,128)(2,1)S(1)}, bf16[32,4224]{1,0:T(8,128)(2,1)S(1)}, u32[]{:S(2)}, u32[]{:S(2)}) collective-permute-start(bf16[32,4224]{1,0:T(8,128)(2,1)S(1)} %collective-permute-done.10.refs_1_), channel_id=1, source_target_pairs={{0,8},{4,20},{8,0},{12,28},{16,24},{20,4},{24,16},{28,12},{1,9},{5... | collective-permute-start | bytes 811016 | tf_op jit(solution)/shard_map/ppermute | solution.py:35
  85.7 10.9 %collective-permute-start.12 = (bf16[32,4224]{1,0:T(8,128)(2,1)S(1)}, bf16[32,4224]{1,0:T(8,128)(2,1)S(1)}, u32[]{:S(2)}, u32[]{:S(2)}) collective-permute-start(bf16[32,4224]{1,0:T(8,128)(2,1)S(1)} %collective-permute-done.10.refs_1_), channel_id=1, source_target_pairs={{0,4},{4,0},{8,12},{12,8},{16,20},{20,16},{24,28},{28,24},{1,5},{5... | collective-permute-start | bytes 811016 | tf_op jit(solution)/shard_map/ppermute | solution.py:19
  85.7 8.9 %collective-permute-start.34 = (bf16[32,4224]{1,0:T(8,128)(2,1)S(1)}, bf16[32,4224]{1,0:T(8,128)(2,1)S(1)}, u32[]{:S(2)}, u32[]{:S(2)}) collective-permute-start(bf16[32,4224]{1,0:T(8,128)(2,1)S(1)} %collective-permute-done.33), channel_id=1, source_target_pairs={{0,1},{1,0},{2,3},{3,2},{4,5},{5,4},{6,7},{7,6},{8,9},{9,8},{10,11... | collective-permute-start | bytes 811016 | tf_op jit(solution)/shard_map/ppermute | solution.py:23
  85.8 12.3 %collective-permute-start.19 = (bf16[32,4224]{1,0:T(8,128)(2,1)S(1)}, bf16[32,4224]{1,0:T(8,128)(2,1)S(1)}, u32[]{:S(2)}, u32[]{:S(2)}) collective-permute-start(bf16[32,4224]{1,0:T(8,128)(2,1)S(1)} %collective-permute-done.13.refs_4_), channel_id=1, source_target_pairs={{0,4},{4,0},{8,12},{12,8},{16,20},{20,16},{24,28},{28,24},{1,5},{5... | collective-permute-start | bytes 811016 | tf_op jit(solution)/shard_map/ppermute | solution.py:19
  86.3 11.9 %collective-permute-start.17 = (bf16[32,4224]{1,0:T(8,128)(2,1)S(1)}, bf16[32,4224]{1,0:T(8,128)(2,1)S(1)}, u32[]{:S(2)}, u32[]{:S(2)}) collective-permute-start(bf16[32,4224]{1,0:T(8,128)(2,1)S(1)} %collective-permute-done.13.refs_4_), channel_id=1, source_target_pairs={{0,16},{4,12},{8,24},{12,4},{16,0},{20,28},{24,8},{28,20},{1,17},{... | collective-permute-start | bytes 811016 | tf_op jit(solution)/shard_map/ppermute | solution.py:35
  94.6 9.2 %collective-permute-start.15 = (bf16[32,4224]{1,0:T(8,128)(2,1)S(1)}, bf16[32,4224]{1,0:T(8,128)(2,1)S(1)}, u32[]{:S(2)}, u32[]{:S(2)}) collective-permute-start(bf16[32,4224]{1,0:T(8,128)(2,1)S(1)} %collective-permute-done.11.refs_2_), channel_id=1, source_target_pairs={{0,8},{4,20},{8,0},{12,28},{16,24},{20,4},{24,16},{28,12},{1,9},{5... | collective-permute-start | bytes 811016 | tf_op jit(solution)/shard_map/ppermute | solution.py:35
  94.6 9.4 %collective-permute-start.18 = (bf16[32,4224]{1,0:T(8,128)(2,1)S(1)}, bf16[32,4224]{1,0:T(8,128)(2,1)S(1)}, u32[]{:S(2)}, u32[]{:S(2)}) collective-permute-start(bf16[32,4224]{1,0:T(8,128)(2,1)S(1)} %collective-permute-done.14.refs_5_), channel_id=1, source_target_pairs={{0,16},{4,12},{8,24},{12,4},{16,0},{20,28},{24,8},{28,20},{1,17},{... | collective-permute-start | bytes 811016 | tf_op jit(solution)/shard_map/ppermute | solution.py:35
  96.6 10.1 %collective-permute-start.16 = (bf16[32,4224]{1,0:T(8,128)(2,1)S(1)}, bf16[32,4224]{1,0:T(8,128)(2,1)S(1)}, u32[]{:S(2)}, u32[]{:S(2)}) collective-permute-start(bf16[32,4224]{1,0:T(8,128)(2,1)S(1)} %collective-permute-done.12.refs_3_), channel_id=1, source_target_pairs={{0,8},{4,20},{8,0},{12,28},{16,24},{20,4},{24,16},{28,12},{1,9},{5... | collective-permute-start | bytes 811016 | tf_op jit(solution)/shard_map/ppermute | solution.py:35
  98.2 9.4 %collective-permute-start.20 = (bf16[32,4224]{1,0:T(8,128)(2,1)S(1)}, bf16[32,4224]{1,0:T(8,128)(2,1)S(1)}, u32[]{:S(2)}, u32[]{:S(2)}) collective-permute-start(bf16[32,4224]{1,0:T(8,128)(2,1)S(1)} %collective-permute-done.14.refs_5_), channel_id=1, source_target_pairs={{0,4},{4,0},{8,12},{12,8},{16,20},{20,16},{24,28},{28,24},{1,5},{5... | collective-permute-start | bytes 811016 | tf_op jit(solution)/shard_map/ppermute | solution.py:19
  98.3 8.5 %collective-permute-start.23 = (bf16[32,4224]{1,0:T(8,128)(2,1)S(1)}, bf16[32,4224]{1,0:T(8,128)(2,1)S(1)}, u32[]{:S(2)}, u32[]{:S(2)}) collective-permute-start(bf16[32,4224]{1,0:T(8,128)(2,1)S(1)} %collective-permute-done.17.refs_8_), channel_id=1, source_target_pairs={{0,4},{4,0},{8,12},{12,8},{16,20},{20,16},{24,28},{28,24},{1,5},{5... | collective-permute-start | bytes 811016 | tf_op jit(solution)/shard_map/ppermute | solution.py:19
  103.8 3.2 %collective-permute-start.21 = (bf16[32,4224]{1,0:T(8,128)(2,1)S(1)}, bf16[32,4224]{1,0:T(8,128)(2,1)S(1)}, u32[]{:S(2)}, u32[]{:S(2)}) collective-permute-start(bf16[32,4224]{1,0:T(8,128)(2,1)S(1)} %collective-permute-done.15.refs_6_), channel_id=1, source_target_pairs={{0,4},{4,0},{8,12},{12,8},{16,20},{20,16},{24,28},{28,24},{1,5},{5... | collective-permute-start | bytes 811016 | tf_op jit(solution)/shard_map/ppermute | solution.py:19
  104.0 4.9 %collective-permute-start.24 = (bf16[32,4224]{1,0:T(8,128)(2,1)S(1)}, bf16[32,4224]{1,0:T(8,128)(2,1)S(1)}, u32[]{:S(2)}, u32[]{:S(2)}) collective-permute-start(bf16[32,4224]{1,0:T(8,128)(2,1)S(1)} %collective-permute-done.18.refs_9_), channel_id=1, source_target_pairs={{0,4},{4,0},{8,12},{12,8},{16,20},{20,16},{24,28},{28,24},{1,5},{5... | collective-permute-start | bytes 811016 | tf_op jit(solution)/shard_map/ppermute | solution.py:19
  106.7 2.2 collective-permute-start.22
  106.7 24.5 %collective-permute-start.55 = (bf16[128,4096]{1,0:T(8,128)(2,1)S(1)}, bf16[128,4096]{1,0:T(8,128)(2,1)S(1)}, u32[]{:S(2)}, u32[]{:S(2)}) collective-permute-start(bf16[128,4096]{1,0:T(8,128)(2,1)S(1)} %constant_dynamic-update-slice_fusion.2.refs_0_), channel_id=1, source_target_pairs={{0,8},{4,20},{8,0},{12,28},{16,24},{20,4},{24,16},{28,12},{1,9},{5... | collective-permute-start | bytes 3145736 | tf_op jit(solution)/shard_map/ppermute | solution.py:35
  106.9 24.8 %collective-permute-start.54 = (bf16[128,4096]{1,0:T(8,128)(2,1)S(1)}, bf16[128,4096]{1,0:T(8,128)(2,1)S(1)}, u32[]{:S(2)}, u32[]{:S(2)}) collective-permute-start(bf16[128,4096]{1,0:T(8,128)(2,1)S(1)} %constant_dynamic-update-slice_fusion.2.refs_0_), channel_id=1, source_target_pairs={{0,4},{4,0},{8,12},{12,8},{16,20},{20,16},{24,28},{28,24},{1,5},{5... | collective-permute-start | bytes 3145736 | tf_op jit(solution)/shard_map/ppermute | solution.py:19
  107.5 25.9 %collective-permute-start.36 = (bf16[64,4224]{1,0:T(8,128)(2,1)S(1)}, bf16[64,4224]{1,0:T(8,128)(2,1)S(1)}, u32[]{:S(2)}, u32[]{:S(2)}) collective-permute-start(bf16[64,4224]{1,0:T(8,128)(2,1)S(1)} %constant_dynamic-update-slice_fusion.refs_0_), channel_id=1, source_target_pairs={{0,8},{4,20},{8,0},{12,28},{16,24},{20,4},{24,16},{28,12},{1,9},{5... | collective-permute-start | bytes 1622024 | tf_op jit(solution)/shard_map/ppermute | solution.py:35
  108.9 24.6 %collective-permute-start.35 = (bf16[64,4224]{1,0:T(8,128)(2,1)S(1)}, bf16[64,4224]{1,0:T(8,128)(2,1)S(1)}, u32[]{:S(2)}, u32[]{:S(2)}) collective-permute-start(bf16[64,4224]{1,0:T(8,128)(2,1)S(1)} %constant_dynamic-update-slice_fusion.refs_0_), channel_id=1, source_target_pairs={{0,4},{4,0},{8,12},{12,8},{16,20},{20,16},{24,28},{28,24},{1,5},{5... | collective-permute-start | bytes 1622024 | tf_op jit(solution)/shard_map/ppermute | solution.py:19
  130.7 3.3 %collective-permute-start.25 = (bf16[64,4096]{1,0:T(8,128)(2,1)S(1)}, bf16[64,4096]{1,0:T(8,128)(2,1)S(1)}, u32[]{:S(2)}, u32[]{:S(2)}) collective-permute-start(bf16[64,4096]{1,0:T(8,128)(2,1)S(1)} %get-tuple-element.40), channel_id=1, source_target_pairs={{0,4},{4,0},{8,12},{12,8},{16,20},{20,16},{24,28},{28,24},{1,5},{5... | collective-permute-start | bytes 1572872 | tf_op jit(solution)/shard_map/ppermute | solution.py:19
  131.3 37.8 %collective-permute-start.57 = (bf16[128,4096]{1,0:T(8,128)(2,1)S(1)}, bf16[128,4096]{1,0:T(8,128)(2,1)S(1)}, u32[]{:S(2)}, u32[]{:S(2)}) collective-permute-start(bf16[128,4096]{1,0:T(8,128)(2,1)S(1)} %collective-permute-done.55.refs_2_), channel_id=1, source_target_pairs={{0,16},{4,12},{8,24},{12,4},{16,0},{20,28},{24,8},{28,20},{1,17},{... | collective-permute-start | bytes 3145736 | tf_op jit(solution)/shard_map/ppermute | solution.py:35
  131.8 37.4 %collective-permute-start.56 = (bf16[128,4096]{1,0:T(8,128)(2,1)S(1)}, bf16[128,4096]{1,0:T(8,128)(2,1)S(1)}, u32[]{:S(2)}, u32[]{:S(2)}) collective-permute-start(bf16[128,4096]{1,0:T(8,128)(2,1)S(1)} %collective-permute-done.54.refs_1_), channel_id=1, source_target_pairs={{0,8},{4,20},{8,0},{12,28},{16,24},{20,4},{24,16},{28,12},{1,9},{5... | collective-permute-start | bytes 3145736 | tf_op jit(solution)/shard_map/ppermute | solution.py:35
  133.5 2.1 collective-permute-start.29
  133.5 34.9 %collective-permute-start.38 = (bf16[64,4224]{1,0:T(8,128)(2,1)S(1)}, bf16[64,4224]{1,0:T(8,128)(2,1)S(1)}, u32[]{:S(2)}, u32[]{:S(2)}) collective-permute-start(bf16[64,4224]{1,0:T(8,128)(2,1)S(1)} %collective-permute-done.36.refs_2_), channel_id=1, source_target_pairs={{0,16},{4,12},{8,24},{12,4},{16,0},{20,28},{24,8},{28,20},{1,17},{... | collective-permute-start | bytes 1622024 | tf_op jit(solution)/shard_map/ppermute | solution.py:35
  134.0 34.4 %collective-permute-start.37 = (bf16[64,4224]{1,0:T(8,128)(2,1)S(1)}, bf16[64,4224]{1,0:T(8,128)(2,1)S(1)}, u32[]{:S(2)}, u32[]{:S(2)}) collective-permute-start(bf16[64,4224]{1,0:T(8,128)(2,1)S(1)} %collective-permute-done.35.refs_1_), channel_id=1, source_target_pairs={{0,8},{4,20},{8,0},{12,28},{16,24},{20,4},{24,16},{28,12},{1,9},{5... | collective-permute-start | bytes 1622024 | tf_op jit(solution)/shard_map/ppermute | solution.py:35
  135.6 34.1 %collective-permute-start.39 = (bf16[64,4224]{1,0:T(8,128)(2,1)S(1)}, bf16[64,4224]{1,0:T(8,128)(2,1)S(1)}, u32[]{:S(2)}, u32[]{:S(2)}) collective-permute-start(bf16[64,4224]{1,0:T(8,128)(2,1)S(1)} %collective-permute-done.36.refs_2_), channel_id=1, source_target_pairs={{0,4},{4,0},{8,12},{12,8},{16,20},{20,16},{24,28},{28,24},{1,5},{5... | collective-permute-start | bytes 1622024 | tf_op jit(solution)/shard_map/ppermute | solution.py:19
  168.4 1.9 collective-permute-start.41
  168.4 2.7 %collective-permute-start.40 = (bf16[64,4224]{1,0:T(8,128)(2,1)S(1)}, bf16[64,4224]{1,0:T(8,128)(2,1)S(1)}, u32[]{:S(2)}, u32[]{:S(2)}) collective-permute-start(bf16[64,4224]{1,0:T(8,128)(2,1)S(1)} %collective-permute-done.37.refs_3_), channel_id=1, source_target_pairs={{0,4},{4,0},{8,12},{12,8},{16,20},{20,16},{24,28},{28,24},{1,5},{5... | collective-permute-start | bytes 1622024 | tf_op jit(solution)/shard_map/ppermute | solution.py:19
  169.1 53.2 %collective-permute-start.58 = (bf16[128,4096]{1,0:T(8,128)(2,1)S(1)}, bf16[128,4096]{1,0:T(8,128)(2,1)S(1)}, u32[]{:S(2)}, u32[]{:S(2)}) collective-permute-start(bf16[128,4096]{1,0:T(8,128)(2,1)S(1)} %collective-permute-done.55.refs_2_), channel_id=1, source_target_pairs={{0,4},{4,0},{8,12},{12,8},{16,20},{20,16},{24,28},{28,24},{1,5},{5... | collective-permute-start | bytes 3145736 | tf_op jit(solution)/shard_map/ppermute | solution.py:19
  169.1 53.7 %collective-permute-start.60 = (bf16[128,4096]{1,0:T(8,128)(2,1)S(1)}, bf16[128,4096]{1,0:T(8,128)(2,1)S(1)}, u32[]{:S(2)}, u32[]{:S(2)}) collective-permute-start(bf16[128,4096]{1,0:T(8,128)(2,1)S(1)} %collective-permute-done.57.refs_4_), channel_id=1, source_target_pairs={{0,4},{4,0},{8,12},{12,8},{16,20},{20,16},{24,28},{28,24},{1,5},{5... | collective-permute-start | bytes 3145736 | tf_op jit(solution)/shard_map/ppermute | solution.py:19
  169.6 54.3 %collective-permute-start.59 = (bf16[128,4096]{1,0:T(8,128)(2,1)S(1)}, bf16[128,4096]{1,0:T(8,128)(2,1)S(1)}, u32[]{:S(2)}, u32[]{:S(2)}) collective-permute-start(bf16[128,4096]{1,0:T(8,128)(2,1)S(1)} %collective-permute-done.56.refs_3_), channel_id=1, source_target_pairs={{0,4},{4,0},{8,12},{12,8},{16,20},{20,16},{24,28},{28,24},{1,5},{5... | collective-permute-start | bytes 3145736 | tf_op jit(solution)/shard_map/ppermute | solution.py:19
  170.3 23.2 %collective-permute-start.28 = (bf16[64,4096]{1,0:T(8,128)(2,1)S(1)}, bf16[64,4096]{1,0:T(8,128)(2,1)S(1)}, u32[]{:S(2)}, u32[]{:S(2)}) collective-permute-start(bf16[64,4096]{1,0:T(8,128)(2,1)S(1)} %get-tuple-element.42), channel_id=1, source_target_pairs={{0,4},{4,0},{8,12},{12,8},{16,20},{20,16},{24,28},{28,24},{1,5},{5... | collective-permute-start | bytes 1572872 | tf_op jit(solution)/shard_map/ppermute | solution.py:19
  171.1 22.8 %collective-permute-start.30 = (bf16[64,4096]{1,0:T(8,128)(2,1)S(1)}, bf16[64,4096]{1,0:T(8,128)(2,1)S(1)}, u32[]{:S(2)}, u32[]{:S(2)}) collective-permute-start(bf16[64,4096]{1,0:T(8,128)(2,1)S(1)} %add_convert_fusion.9), channel_id=1, source_target_pairs={{0,16},{4,12},{8,24},{12,4},{16,0},{20,28},{24,8},{28,20},{1,17},{... | collective-permute-start | bytes 1572872 | tf_op jit(solution)/shard_map/ppermute | solution.py:35
  193.6 2.0 collective-permute-start.42
  194.1 14.1 %collective-permute-start.45 = (bf16[64,4096]{1,0:T(8,128)(2,1)S(1)}, bf16[64,4096]{1,0:T(8,128)(2,1)S(1)}, u32[]{:S(2)}, u32[]{:S(2)}) collective-permute-start(bf16[64,4096]{1,0:T(8,128)(2,1)S(1)} %get-tuple-element.51), channel_id=1, source_target_pairs={{0,4},{4,0},{8,12},{12,8},{16,20},{20,16},{24,28},{28,24},{1,5},{5... | collective-permute-start | bytes 1572872 | tf_op jit(solution)/shard_map/ppermute | solution.py:19
  195.5 1.9 collective-permute-start.46
  197.4 9.2 %collective-permute-start.43 = (bf16[64,4096]{1,0:T(8,128)(2,1)S(1)}, bf16[64,4096]{1,0:T(8,128)(2,1)S(1)}, u32[]{:S(2)}, u32[]{:S(2)}) collective-permute-start(bf16[64,4096]{1,0:T(8,128)(2,1)S(1)} %add_convert_fusion.6), channel_id=1, source_target_pairs={{0,8},{4,20},{8,0},{12,28},{16,24},{20,4},{24,16},{28,12},{1,9},{5... | collective-permute-start | bytes 1572872 | tf_op jit(solution)/shard_map/ppermute | solution.py:35
  206.6 14.4 %collective-permute-start.47 = (bf16[64,4096]{1,0:T(8,128)(2,1)S(1)}, bf16[64,4096]{1,0:T(8,128)(2,1)S(1)}, u32[]{:S(2)}, u32[]{:S(2)}) collective-permute-start(bf16[64,4096]{1,0:T(8,128)(2,1)S(1)} %add_convert_fusion.2), channel_id=1, source_target_pairs={{0,16},{4,12},{8,24},{12,4},{16,0},{20,28},{24,8},{28,20},{1,17},{... | collective-permute-start | bytes 1572872 | tf_op jit(solution)/shard_map/ppermute | solution.py:35
  208.3 13.0 %collective-permute-start.26 = (bf16[64,4096]{1,0:T(8,128)(2,1)S(1)}, bf16[64,4096]{1,0:T(8,128)(2,1)S(1)}, u32[]{:S(2)}, u32[]{:S(2)}) collective-permute-start(bf16[64,4096]{1,0:T(8,128)(2,1)S(1)} %add_convert_fusion.13), channel_id=1, source_target_pairs={{0,8},{4,20},{8,0},{12,28},{16,24},{20,4},{24,16},{28,12},{1,9},{5... | collective-permute-start | bytes 1572872 | tf_op jit(solution)/shard_map/ppermute | solution.py:35
  221.1 9.6 %collective-permute-start.44 = (bf16[64,4096]{1,0:T(8,128)(2,1)S(1)}, bf16[64,4096]{1,0:T(8,128)(2,1)S(1)}, u32[]{:S(2)}, u32[]{:S(2)}) collective-permute-start(bf16[64,4096]{1,0:T(8,128)(2,1)S(1)} %add_convert_fusion.5), channel_id=1, source_target_pairs={{0,4},{4,0},{8,12},{12,8},{16,20},{20,16},{24,28},{28,24},{1,5},{5... | collective-permute-start | bytes 1572872 | tf_op jit(solution)/shard_map/ppermute | solution.py:19
  221.3 9.4 %collective-permute-start.48 = (bf16[64,4096]{1,0:T(8,128)(2,1)S(1)}, bf16[64,4096]{1,0:T(8,128)(2,1)S(1)}, u32[]{:S(2)}, u32[]{:S(2)}) collective-permute-start(bf16[64,4096]{1,0:T(8,128)(2,1)S(1)} %add_convert_fusion.1), channel_id=1, source_target_pairs={{0,8},{4,20},{8,0},{12,28},{16,24},{20,4},{24,16},{28,12},{1,9},{5... | collective-permute-start | bytes 1572872 | tf_op jit(solution)/shard_map/ppermute | solution.py:35
  222.3 9.3 %collective-permute-start.27 = (bf16[64,4096]{1,0:T(8,128)(2,1)S(1)}, bf16[64,4096]{1,0:T(8,128)(2,1)S(1)}, u32[]{:S(2)}, u32[]{:S(2)}) collective-permute-start(bf16[64,4096]{1,0:T(8,128)(2,1)S(1)} %add_convert_fusion.12), channel_id=1, source_target_pairs={{0,4},{4,0},{8,12},{12,8},{16,20},{20,16},{24,28},{28,24},{1,5},{5... | collective-permute-start | bytes 1572872 | tf_op jit(solution)/shard_map/ppermute | solution.py:19
  222.9 13.3 %collective-permute-start.31 = (bf16[64,4096]{1,0:T(8,128)(2,1)S(1)}, bf16[64,4096]{1,0:T(8,128)(2,1)S(1)}, u32[]{:S(2)}, u32[]{:S(2)}) collective-permute-start(bf16[64,4096]{1,0:T(8,128)(2,1)S(1)} %add_convert_fusion.8), channel_id=1, source_target_pairs={{0,8},{4,20},{8,0},{12,28},{16,24},{20,4},{24,16},{28,12},{1,9},{5... | collective-permute-start | bytes 1572872 | tf_op jit(solution)/shard_map/ppermute | solution.py:35
  230.9 8.8 %collective-permute-start.49 = (bf16[32,4096]{1,0:T(8,128)(2,1)S(1)}, bf16[32,4096]{1,0:T(8,128)(2,1)S(1)}, u32[]{:S(2)}, u32[]{:S(2)}) collective-permute-start(bf16[32,4096]{1,0:T(8,128)(2,1)S(1)} %slice.19), channel_id=1, source_target_pairs={{0,1},{1,0},{2,3},{3,2},{4,5},{5,4},{6,7},{7,6},{8,9},{9,8},{10,11... | collective-permute-start | bytes 786440 | tf_op jit(solution)/shard_map/ppermute | solution.py:23
  236.4 12.2 %collective-permute-start.32 = (bf16[32,4096]{1,0:T(8,128)(2,1)S(1)}, bf16[32,4096]{1,0:T(8,128)(2,1)S(1)}, u32[]{:S(2)}, u32[]{:S(2)}) collective-permute-start(bf16[32,4096]{1,0:T(8,128)(2,1)S(1)} %slice.17), channel_id=1, source_target_pairs={{0,1},{1,0},{2,3},{3,2},{4,5},{5,4},{6,7},{7,6},{8,9},{9,8},{10,11... | collective-permute-start | bytes 786440 | tf_op jit(solution)/shard_map/ppermute | solution.py:23
  239.8 13.5 %collective-permute-start.50 = (bf16[32,4096]{1,0:T(8,128)(2,1)S(1)}, bf16[32,4096]{1,0:T(8,128)(2,1)S(1)}, u32[]{:S(2)}, u32[]{:S(2)}) collective-permute-start(bf16[32,4096]{1,0:T(8,128)(2,1)S(1)} %add_convert_fusion.15), channel_id=1, source_target_pairs={{0,2},{1,3},{2,0},{3,1},{4,6},{5,7},{6,4},{7,5},{8,10},{9,11},{10,... | collective-permute-start | bytes 786440 | tf_op jit(solution)/shard_map/ppermute | solution.py:23
  (10 other events, 122.9 us)

commit v4 on v3

--- a/solution.py
+++ b/solution.py
@@ -89,6 +89,7 @@
     return pl.pallas_call(
         widen_kernel,
         out_shape=jax.ShapeDtypeStruct((16, router.shape[1]), router.dtype),
+        compiler_params=pltpu.CompilerParams(vmem_limit_bytes=2 << 20),
         name="widen",
     )(router)
 
@@ -121,6 +122,7 @@
         out_shape=jax.ShapeDtypeStruct(place.shape, place.dtype),
         in_specs=[spec],
         out_specs=spec,
+        compiler_params=pltpu.CompilerParams(vmem_limit_bytes=1 << 20),
         name="relay",
     )(place)
 
@@ -466,6 +468,9 @@
         cost_estimate=pl.CostEstimate(
             flops=4 * work, transcendentals=work // HEAD_SIZE, bytes_accessed=work // 64
         ),
+        compiler_params=pltpu.CompilerParams(
+            vmem_limit_bytes=4 * rows * slots * count + (10 << 20)
+        ),
         name="attend",
     )(places, *operands)
 
@@ -539,16 +544,16 @@
     plane = lax.axis_index("exp")
     row_count, width = residual.shape
 
-    grads = gather(jnp.concatenate(planes_of(cotangent, False), axis=0))
-
-    attn = attention(query, keys_values, cache)
+    others = planes_of(cotangent, False)[1:]
+    in_place = lambda a: pltpu.with_memory_space_constraint(a, pltpu.HBM)
+    attn = attention(in_place(query), keys_values, cache)
 
     place = jnp.full((1,), plane, jnp.int32)
     marked = relay(place)
     marked = relay(marked)
-    hidden_one, *shares = project(
-        place, attn, pltpu.with_memory_space_constraint(out_proj, pltpu.HBM), residual
-    )
+    hidden_one, *shares = project(place, attn, in_place(out_proj), in_place(residual))
+    late, hidden_one = lax.optimization_barrier((cotangent, hidden_one))
+    grads = gather(jnp.concatenate([late] + others, axis=0))
     for k in range(0, planes, 2):
         both = swap_plane(shares[k], 1)
         if k:
@@ -558,7 +563,6 @@
     mean_square = jnp.mean(hidden_one * hidden_one, axis=-1, keepdims=True)
     normed = (hidden_one * lax.rsqrt(mean_square + EPSILON) * norm_gain).astype(jnp.bfloat16)
 
-    in_place = lambda a: pltpu.with_memory_space_constraint(a, pltpu.HBM)
     gate_mat = in_place(w_gate[0])
     up_mat = in_place(w_up[0])
     down_mat = in_place(w_down[0])

time: 255 us -> 258 us (1.012)
  waiting for transfers between devices: 114 us -> 133 us
  starting transfers between devices: 51.8 us -> 44 us
  Pallas kernels: 78.2 us -> 74.3 us
    ppermute x12, waiting for transfers between devices: 35.7 us -> 53.2 us  [swap_plane(): lax.ppermute(value, 'exp', [(i, i ^ bits) for i in range(lax.axis_size('e...]
    ppermute x12, starting transfers between devices: 17.3 us -> 12.5 us  [swap_plane(): lax.ppermute(value, 'exp', [(i, i ^ bits) for i in range(lax.axis_size('e...]
    pallas_call x2, Pallas kernels: 11.8 us -> 9.09 us  [attend(): pl.pallas_call(functools.partial(attend_kernel, slots, cached, window_fre...]
  transfers between devices with their start and end apart: 61 -> 61, of which waited for: 22 -> 21; matrix products, arithmetic and copies ran while one was open for 2% -> 2% of each run, Pallas kernels for 30% -> 28%
where the time goes in v4:
time: 258 us
  waiting for transfers between devices  133 us (52%)
  Pallas kernels  74.3 us (29%)
  starting transfers between devices  44 us (17%)
  other arithmetic  3.67 us (1%)
    ppermute x21, waiting for transfers between devices, cross(): return lax.ppermute(value, 'ctx', pairs)  75.7 us
    ppermute x12, waiting for transfers between devices, swap_plane(): lax.ppermute(value, 'exp', [(i, i ^ bits) for i in range(lax.axis_size('e...  53.2 us
    pallas_call x2, Pallas kernels, rise(): pl.pallas_call(functools.partial(rise_kernel, len(rows)), out_shape=[jax....  29.3 us
    ppermute x21, starting transfers between devices, cross(): return lax.ppermute(value, 'ctx', pairs)  26.6 us
    pallas_call x2, Pallas kernels, fall(): pl.pallas_call(fall_kernel, out_shape=[jax.ShapeDtypeStruct((c, width), j...  14.6 us
    pallas_call x2, Pallas kernels, outer(): pl.pallas_call(functools.partial(outer_kernel, len(grads), pieces, blocks...  13.5 us
    ppermute x12, starting transfers between devices, swap_plane(): lax.ppermute(value, 'exp', [(i, i ^ bits) for i in range(lax.axis_size('e...  12.5 us
    pallas_call x2, Pallas kernels, attend(): pl.pallas_call(functools.partial(attend_kernel, slots, cached, window_fre...  9.09 us
  transfers between devices with their start and end apart: 61, of which 21 were waited for; matrix products, arithmetic and copies ran while one was open for 2% of the time, Pallas kernels for 28%

profile of v4, /device:TPU:0, one launch (start us, length us, event | category | flops | bytes accessed | tf_op | source)
XLA Modules:
  0.0 257.9 jit_solution(18273558655781539595)
XLA Ops:
  0.6 1.0 pack.1.refs_2_.refs_4_
  1.6 0.6 collective-permute-start.1
  2.2 2.6 collective-permute-start
  4.8 1.6 collective-permute-start.2
  6.4 4.1 %collective-permute-done.refs_2_.refs_8_ = bf16[2,384,256]{2,1,0:T(8,128)(2,1)S(1)} collective-permute-done((bf16[2,384,256]{2,1,0:T(8,128)(2,1)S(1)}, bf16[2,384,256]{2,1,0:T(8,128)(2,1)S(1)}, u32[]{:S(2)}, u32[]{:S(2)}) %collective-permute-start) | collective-permute-done | bytes 393248 | tf_op jit(solution)/shard_map/ppermute | solution.py:35
  10.5 2.0 collective-permute-start.5
  12.6 3.9 %collective-permute-done.2.refs_3_.refs_9_ = bf16[2,384,256]{2,1,0:T(8,128)(2,1)S(1)} collective-permute-done((bf16[2,384,256]{2,1,0:T(8,128)(2,1)S(1)}, bf16[2,384,256]{2,1,0:T(8,128)(2,1)S(1)}, u32[]{:S(2)}, u32[]{:S(2)}) %collective-permute-start.2) | collective-permute-done | bytes 393248 | tf_op jit(solution)/shard_map/ppermute | solution.py:35
  16.5 2.2 collective-permute-done.5.refs_6_.refs_12_
  18.8 2.0 collective-permute-start.51
  20.9 2.5 collective-permute-start.53
  23.9 1.2 relay.3.place
  25.0 0.7 convert_element_type.178
  25.8 0.8 copy-done
  26.8 3.1 %attend.2 = (f32[2,512,128]{2,1,0:T(8,128)S(1)}, f32[2,512,128]{2,1,0:T(8,128)S(1)}, f32[2,512,128]{2,1,0:T(8,128)S(1)}) custom-call(s32[4]{0:T(128)S(1)} %pad_add_fusion.refs_0_, bf16[128,1024]{1,0:T(8,128)(2,1)} %refs_1_.3, bf16[2,384,256]{2,1,0:T(8,128)(2,1)S(1)} %pack.1.refs_2_.refs_4_, bf16[2,384,256]{2,1,0:T(8,128)(2,1)S(1)} %collective-permute-done.1.refs_3_.refs_5_, ...), custom_call_target="tpu_custom_call" | custom-call | flops 402653184 | bytes 1572864 | tf_op jit(solution)/shard_map/attend/pallas_call | solution.py:458
  30.1 5.9 %attend.3.attn_ref = bf16[128,1024]{1,0:T(8,128)(2,1)S(1)} custom-call(s32[12]{0:T(128)S(1)} %stack.63.refs_0_, bf16[128,1024]{1,0:T(8,128)(2,1)} %refs_1_.3, bf16[2,384,256]{2,1,0:T(8,128)(2,1)S(1)} %collective-permute-done.refs_2_.refs_8_, bf16[2,384,256]{2,1,0:T(8,128)(2,1)S(1)} %collective-permute-done.2.refs_3_.refs_9_, ...), custom_call_target="tpu_custom_call" | custom-call | flops 1207959552 | bytes 4718592 | tf_op jit(solution)/shard_map/attend/pallas_call | solution.py:458
  36.1 5.1 %project.1 = (f32[32,4096]{1,0:T(8,128)S(1)}, bf16[32,4096]{1,0:T(8,128)(2,1)S(1)}, f32[32,4096]{1,0:T(8,128)S(1)}, bf16[32,4096]{1,0:T(8,128)(2,1)S(1)}) custom-call(s32[1]{0:T(128)} %bitcast.place.in_ref, bf16[128,1024]{1,0:T(8,128)(2,1)S(1)} %attend.3.attn_ref, bf16[1024,4096]{1,0:T(8,128)(2,1)} %proj_ref.1, bf16[32,4096]{1,0:T(8,128)(2,1)} %residual_ref.1), custom_call_target="tpu_custom_call" | custom-call | flops 1073741824 | bytes 8388608 | tf_op jit(solution)/shard_map/project/pallas_call | solution.py:259
  41.2 1.9 collective-permute-start.7
  43.3 14.8 %collective-permute-done.8 = bf16[32,4096]{1,0:T(8,128)(2,1)S(1)} collective-permute-done((bf16[32,4096]{1,0:T(8,128)(2,1)S(1)}, bf16[32,4096]{1,0:T(8,128)(2,1)S(1)}, u32[]{:S(2)}, u32[]{:S(2)}) %collective-permute-start.8) | collective-permute-done | bytes 262176 | tf_op jit(solution)/shard_map/ppermute | solution.py:23
  58.2 0.8 collective-permute-start.9
  58.9 1.0 constant_dynamic-update-slice_fusion.4
  59.9 13.0 %collective-permute-done.9 = bf16[32,4096]{1,0:T(8,128)(2,1)S(1)} collective-permute-done((bf16[32,4096]{1,0:T(8,128)(2,1)S(1)}, bf16[32,4096]{1,0:T(8,128)(2,1)S(1)}, u32[]{:S(2)}, u32[]{:S(2)}) %collective-permute-start.9) | collective-permute-done | bytes 262176 | tf_op jit(solution)/shard_map/ppermute | solution.py:23
  73.4 2.2 collective-permute-start.10
  75.6 1.6 collective-permute-start.13
  77.2 10.6 %collective-permute-done.10.refs_1_ = bf16[32,4224]{1,0:T(8,128)(2,1)S(1)} collective-permute-done((bf16[32,4224]{1,0:T(8,128)(2,1)S(1)}, bf16[32,4224]{1,0:T(8,128)(2,1)S(1)}, u32[]{:S(2)}, u32[]{:S(2)}) %collective-permute-start.10) | collective-permute-done | bytes 270368 | tf_op jit(solution)/shard_map/ppermute | solution.py:23
  87.8 1.5 collective-permute-start.14
  89.9 1.5 collective-permute-start.17
  91.4 6.8 %collective-permute-done.34 = bf16[32,4224]{1,0:T(8,128)(2,1)S(1)} collective-permute-done((bf16[32,4224]{1,0:T(8,128)(2,1)S(1)}, bf16[32,4224]{1,0:T(8,128)(2,1)S(1)}, u32[]{:S(2)}, u32[]{:S(2)}) %collective-permute-start.34) | collective-permute-done | bytes 270368 | tf_op jit(solution)/shard_map/ppermute | solution.py:23
  98.7 1.5 collective-permute-start.18
  100.2 1.5 collective-permute-start.16
  102.3 5.0 %collective-permute-done.15.refs_6_ = bf16[32,4224]{1,0:T(8,128)(2,1)S(1)} collective-permute-done((bf16[32,4224]{1,0:T(8,128)(2,1)S(1)}, bf16[32,4224]{1,0:T(8,128)(2,1)S(1)}, u32[]{:S(2)}, u32[]{:S(2)}) %collective-permute-start.15) | collective-permute-done | bytes 270368 | tf_op jit(solution)/shard_map/ppermute | solution.py:35
  107.4 0.7 collective-permute-done.18.refs_9_
  108.1 2.2 collective-permute-done.16.refs_7_
  110.3 0.6 collective-permute-start.55
  111.1 1.4 collective-permute-start.36
  112.5 14.6 %rise.2 = (bf16[512,1024]{1,0:T(8,128)(2,1)S(1)}, bf16[1024,512]{1,0:T(8,128)(2,1)S(1)}) custom-call(s32[1]{0:T(128)} %relay.3.place, bf16[16,4096]{1,0:T(8,128)(2,1)S(1)} %widen.1.router_ref, bf16[32,4224]{1,0:T(8,128)(2,1)S(1)} %fusion.1.refs_0_, bf16[32,4224]{1,0:T(8,128)(2,1)S(1)} %collective-permute-done.10.refs_1_, ...), custom_call_target="tpu_custom_call" | custom-call | flops 8589934592 | bytes 20971520 | tf_op jit(solution)/shard_map/rise/pallas_call | solution.py:175
  127.1 7.3 %fall.2 = (bf16[64,4096]{1,0:T(8,128)(2,1)S(1)}, bf16[64,4096]{1,0:T(8,128)(2,1)S(1)}, bf16[64,4096]{1,0:T(8,128)(2,1)S(1)}, bf16[64,4096]{1,0:T(8,128)(2,1)S(1)...) custom-call(bf16[512,1024]{1,0:T(8,128)(2,1)S(1)} %get-tuple-element, ...), custom_call_target="tpu_custom_call" | custom-call | flops 4294967296 | bytes 12582912 | tf_op jit(solution)/shard_map/fall/pallas_call | solution.py:220
  134.4 0.6 collective-permute-start.25
  135.0 0.7 collective-permute-start.57
  135.7 1.5 collective-permute-start.56
  137.2 0.6 collective-permute-start.38
  137.7 1.4 collective-permute-start.37
  139.3 32.8 %collective-permute-done.38.refs_4_ = bf16[64,4224]{1,0:T(8,128)(2,1)S(1)} collective-permute-done((bf16[64,4224]{1,0:T(8,128)(2,1)S(1)}, bf16[64,4224]{1,0:T(8,128)(2,1)S(1)}, u32[]{:S(2)}, u32[]{:S(2)}) %collective-permute-start.38) | collective-permute-done | bytes 540704 | tf_op jit(solution)/shard_map/ppermute | solution.py:35
  173.4 0.6 collective-permute-done.41.refs_7_
  174.2 0.6 collective-permute-done.40.refs_6_
  174.8 0.8 collective-permute-start.30
  175.6 14.8 %rise.3 = (bf16[512,1024]{1,0:T(8,128)(2,1)S(1)}, bf16[1024,512]{1,0:T(8,128)(2,1)S(1)}) custom-call(s32[1]{0:T(128)} %relay.3.place, bf16[16,4096]{1,0:T(8,128)(2,1)S(1)} %widen.1.router_ref, bf16[64,4224]{1,0:T(8,128)(2,1)S(1)} %constant_dynamic-update-slice_fusion.refs_0_, bf16[64,4224]{1,0:T(8,128)(2,1)S(1)} %collective-permute-done.35.refs_1_, ...), custom_call_target="tpu_custom_call" | custom-call | flops 8589934592 | bytes 20971520 | tf_op jit(solution)/shard_map/rise/pallas_call | solution.py:175
  190.4 7.3 %fall.3 = (bf16[64,4096]{1,0:T(8,128)(2,1)S(1)}, bf16[64,4096]{1,0:T(8,128)(2,1)S(1)}, bf16[64,4096]{1,0:T(8,128)(2,1)S(1)}, bf16[64,4096]{1,0:T(8,128)(2,1)S(1)...) custom-call(bf16[512,1024]{1,0:T(8,128)(2,1)S(1)} %get-tuple-element, ...), custom_call_target="tpu_custom_call" | custom-call | flops 4294967296 | bytes 12582912 | tf_op jit(solution)/shard_map/fall/pallas_call | solution.py:220
  198.5 1.1 collective-permute-done.42
  199.9 1.6 collective-permute-done.46
  201.6 1.2 collective-permute-start.43
  202.9 7.9 %collective-permute-done.43 = bf16[64,4096]{1,0:T(8,128)(2,1)S(1)} collective-permute-done((bf16[64,4096]{1,0:T(8,128)(2,1)S(1)}, bf16[64,4096]{1,0:T(8,128)(2,1)S(1)}, u32[]{:S(2)}, u32[]{:S(2)}) %collective-permute-start.43) | collective-permute-done | bytes 524320 | tf_op jit(solution)/shard_map/ppermute | solution.py:35
  210.8 1.2 collective-permute-start.47
  212.1 1.0 collective-permute-start.26
  213.1 11.9 %collective-permute-done.47 = bf16[64,4096]{1,0:T(8,128)(2,1)S(1)} collective-permute-done((bf16[64,4096]{1,0:T(8,128)(2,1)S(1)}, bf16[64,4096]{1,0:T(8,128)(2,1)S(1)}, u32[]{:S(2)}, u32[]{:S(2)}) %collective-permute-start.47) | collective-permute-done | bytes 524320 | tf_op jit(solution)/shard_map/ppermute | solution.py:35
  225.2 0.9 collective-permute-start.48
  226.6 1.1 collective-permute-start.31
  227.7 6.7 %outer.2.refs_10_ = f32[1024,4096]{1,0:T(8,128)} custom-call(bf16[128,4096]{1,0:T(8,128)(2,1)S(1)} %constant_dynamic-update-slice_fusion.2.refs_0_, bf16[128,4096]{1,0:T(8,128)(2,1)S(1)} %collective-permute-done.54.refs_1_, bf16[128,4096]{1,0:T(8,128)(2,1)S(1)} %collective-permute-done.55.refs_2_, bf16[128,4096]{1,0:T(8,128)(2,1)S(1)} %collective-permute-done.56.refs_3_, ...), custom_call_target="tpu_custom_call" | custom-call | flops 4294967296 | bytes 16777216 | tf_op jit(solution)/shard_map/outer/pallas_call | solution.py:316
  235.2 4.9 %collective-permute-done.31 = bf16[64,4096]{1,0:T(8,128)(2,1)S(1)} collective-permute-done((bf16[64,4096]{1,0:T(8,128)(2,1)S(1)}, bf16[64,4096]{1,0:T(8,128)(2,1)S(1)}, u32[]{:S(2)}, u32[]{:S(2)}) %collective-permute-start.31) | collective-permute-done | bytes 524320 | tf_op jit(solution)/shard_map/ppermute | solution.py:35
  240.8 2.6 collective-permute-done.49
  243.4 1.5 collective-permute-start.50
  244.9 6.7 %outer.3 = f32[1024,4096]{1,0:T(8,128)} custom-call(bf16[128,4096]{1,0:T(8,128)(2,1)S(1)} %constant_dynamic-update-slice_fusion.2.refs_0_, bf16[128,4096]{1,0:T(8,128)(2,1)S(1)} %collective-permute-done.54.refs_1_, bf16[128,4096]{1,0:T(8,128)(2,1)S(1)} %collective-permute-done.55.refs_2_, ...), custom_call_target="tpu_custom_call", output_to_operand_aliasing={{}: (10, {})} | custom-call | flops 4294967296 | bytes 16777216 | tf_op jit(solution)/shard_map/outer/pallas_call | solution.py:316
  251.7 0.6 collective-permute-done.32
  252.2 4.8 %collective-permute-done.50 = bf16[32,4096]{1,0:T(8,128)(2,1)S(1)} collective-permute-done((bf16[32,4096]{1,0:T(8,128)(2,1)S(1)}, bf16[32,4096]{1,0:T(8,128)(2,1)S(1)}, u32[]{:S(2)}, u32[]{:S(2)}) %collective-permute-start.50) | collective-permute-done | bytes 262176 | tf_op jit(solution)/shard_map/ppermute | solution.py:23
  257.0 0.9 add_convert_fusion.14
  (106 shorter events, 9.0 us)
Async XLA Ops:
  1.6 3.1 %collective-permute-start.1 = (bf16[2,384,256]{2,1,0:T(8,128)(2,1)S(1)}, bf16[2,384,256]{2,1,0:T(8,128)(2,1)S(1)}, u32[]{:S(2)}, u32[]{:S(2)}) collective-permute-start(bf16[2,384,256]{2,1,0:T(8,128)(2,1)S(1)} %pack.1.refs_2_.refs_4_), channel_id=1, source_target_pairs={{0,4},{4,0},{8,12},{12,8},{16,20},{20,16},{24,28},{28,24},{1,5},{5... | collective-permute-start | bytes 1179656 | tf_op jit(solution)/shard_map/ppermute | solution.py:19
  2.2 8.3 %collective-permute-start = (bf16[2,384,256]{2,1,0:T(8,128)(2,1)S(1)}, bf16[2,384,256]{2,1,0:T(8,128)(2,1)S(1)}, u32[]{:S(2)}, u32[]{:S(2)}) collective-permute-start(bf16[2,384,256]{2,1,0:T(8,128)(2,1)S(1)} %pack.1.refs_2_.refs_4_), channel_id=1, source_target_pairs={{0,8},{4,20},{8,0},{12,28},{16,24},{20,4},{24,16},{28,12},{1,9},{5... | collective-permute-start | bytes 1179656 | tf_op jit(solution)/shard_map/ppermute | solution.py:35
  4.8 11.7 %collective-permute-start.2 = (bf16[2,384,256]{2,1,0:T(8,128)(2,1)S(1)}, bf16[2,384,256]{2,1,0:T(8,128)(2,1)S(1)}, u32[]{:S(2)}, u32[]{:S(2)}) collective-permute-start(bf16[2,384,256]{2,1,0:T(8,128)(2,1)S(1)} %collective-permute-done.1.refs_3_.refs_5_), channel_id=1, source_target_pairs={{0,8},{4,20},{8,0},{12,28},{16,24},{20,4},{24,16},{28,12},{1,9},{5... | collective-permute-start | bytes 1179656 | tf_op jit(solution)/shard_map/ppermute | solution.py:35
  10.5 8.2 %collective-permute-start.5 = (bf16[2,384,256]{2,1,0:T(8,128)(2,1)S(1)}, bf16[2,384,256]{2,1,0:T(8,128)(2,1)S(1)}, u32[]{:S(2)}, u32[]{:S(2)}) collective-permute-start(bf16[2,384,256]{2,1,0:T(8,128)(2,1)S(1)} %collective-permute-done.refs_2_.refs_8_), channel_id=1, source_target_pairs={{0,16},{4,12},{8,24},{12,4},{16,0},{20,28},{24,8},{28,20},{1,17},{... | collective-permute-start | bytes 1179656 | tf_op jit(solution)/shard_map/ppermute | solution.py:35
  12.6 17.4 %collective-permute-start.3 = (bf16[2,384,256]{2,1,0:T(8,128)(2,1)S(1)}, bf16[2,384,256]{2,1,0:T(8,128)(2,1)S(1)}, u32[]{:S(2)}, u32[]{:S(2)}) collective-permute-start(bf16[2,384,256]{2,1,0:T(8,128)(2,1)S(1)} %collective-permute-done.refs_2_.refs_8_), channel_id=1, source_target_pairs={{0,4},{4,0},{8,12},{12,8},{16,20},{20,16},{24,28},{28,24},{1,5},{5... | collective-permute-start | bytes 1179656 | tf_op jit(solution)/shard_map/ppermute | solution.py:19
  16.5 13.7 %collective-permute-start.4 = (bf16[2,384,256]{2,1,0:T(8,128)(2,1)S(1)}, bf16[2,384,256]{2,1,0:T(8,128)(2,1)S(1)}, u32[]{:S(2)}, u32[]{:S(2)}) collective-permute-start(bf16[2,384,256]{2,1,0:T(8,128)(2,1)S(1)} %collective-permute-done.2.refs_3_.refs_9_), channel_id=1, source_target_pairs={{0,4},{4,0},{8,12},{12,8},{16,20},{20,16},{24,28},{28,24},{1,5},{5... | collective-permute-start | bytes 1179656 | tf_op jit(solution)/shard_map/ppermute | solution.py:19
  18.7 11.4 %collective-permute-start.6 = (bf16[2,384,256]{2,1,0:T(8,128)(2,1)S(1)}, bf16[2,384,256]{2,1,0:T(8,128)(2,1)S(1)}, u32[]{:S(2)}, u32[]{:S(2)}) collective-permute-start(bf16[2,384,256]{2,1,0:T(8,128)(2,1)S(1)} %collective-permute-done.5.refs_6_.refs_12_), channel_id=1, source_target_pairs={{0,4},{4,0},{8,12},{12,8},{16,20},{20,16},{24,28},{28,24},{1,5},{5... | collective-permute-start | bytes 1179656 | tf_op jit(solution)/shard_map/ppermute | solution.py:19
  18.8 40.1 %collective-permute-start.51 = (bf16[32,4096]{1,0:T(8,128)(2,1)}, bf16[32,4096]{1,0:T(8,128)(2,1)}, u32[]{:S(2)}, u32[]{:S(2)}) collective-permute-start(bf16[32,4096]{1,0:T(8,128)(2,1)} %param.23), channel_id=1, source_target_pairs={{0,1},{1,0},{2,3},{3,2},{4,5},{5,4},{6,7},{7,6},{8,9},{9,8},{10,11... | collective-permute-start | bytes 786440 | tf_op jit(solution)/shard_map/ppermute | solution.py:23
  20.9 68.4 %collective-permute-start.53 = (bf16[32,4096]{1,0:T(8,128)(2,1)}, bf16[32,4096]{1,0:T(8,128)(2,1)S(1)}, u32[]{:S(2)}, u32[]{:S(2)}) collective-permute-start(bf16[32,4096]{1,0:T(8,128)(2,1)} %param.23), channel_id=1, source_target_pairs={{0,3},{1,2},{2,1},{3,0},{4,7},{5,6},{6,5},{7,4},{8,11},{9,10},{10,... | collective-permute-start | bytes 786440 | tf_op jit(solution)/shard_map/ppermute | solution.py:23
  25.8 0.8 copy-start
  26.8 16.5 %copy-start.1 = (bf16[32,4096]{1,0:T(8,128)(2,1)S(1)}, bf16[32,4096]{1,0:T(8,128)(2,1)}, u32[]{:S(2)}) copy-start(bf16[32,4096]{1,0:T(8,128)(2,1)} %param.23) | copy-start | bytes 786436
  29.9 45.7 %collective-permute-start.52 = (bf16[32,4096]{1,0:T(8,128)(2,1)}, bf16[32,4096]{1,0:T(8,128)(2,1)S(1)}, u32[]{:S(2)}, u32[]{:S(2)}) collective-permute-start(bf16[32,4096]{1,0:T(8,128)(2,1)} %param.23), channel_id=1, source_target_pairs={{0,2},{1,3},{2,0},{3,1},{4,6},{5,7},{6,4},{7,5},{8,10},{9,11},{10,... | collective-permute-start | bytes 786440 | tf_op jit(solution)/shard_map/ppermute | solution.py:23
  30.1 43.0 %copy-start.2 = (f32[4096]{0:T(1024)S(1)}, f32[4096]{0:T(1024)}, u32[]{:S(2)}) copy-start(f32[4096]{0:T(1024)} %param.17) | copy-start | bytes 49156
  41.2 18.7 %collective-permute-start.7 = (bf16[32,4096]{1,0:T(8,128)(2,1)S(1)}, bf16[32,4096]{1,0:T(8,128)(2,1)S(1)}, u32[]{:S(2)}, u32[]{:S(2)}) collective-permute-start(bf16[32,4096]{1,0:T(8,128)(2,1)S(1)} %get-tuple-element.36), channel_id=1, source_target_pairs={{0,1},{1,0},{2,3},{3,2},{4,5},{5,4},{6,7},{7,6},{8,9},{9,8},{10,11... | collective-permute-start | bytes 786440 | tf_op jit(solution)/shard_map/ppermute | solution.py:23
  43.0 15.1 %collective-permute-start.8 = (bf16[32,4096]{1,0:T(8,128)(2,1)S(1)}, bf16[32,4096]{1,0:T(8,128)(2,1)S(1)}, u32[]{:S(2)}, u32[]{:S(2)}) collective-permute-start(bf16[32,4096]{1,0:T(8,128)(2,1)S(1)} %get-tuple-element.38), channel_id=1, source_target_pairs={{0,1},{1,0},{2,3},{3,2},{4,5},{5,4},{6,7},{7,6},{8,9},{9,8},{10,11... | collective-permute-start | bytes 786440 | tf_op jit(solution)/shard_map/ppermute | solution.py:23
  58.2 14.8 %collective-permute-start.9 = (bf16[32,4096]{1,0:T(8,128)(2,1)S(1)}, bf16[32,4096]{1,0:T(8,128)(2,1)S(1)}, u32[]{:S(2)}, u32[]{:S(2)}) collective-permute-start(bf16[32,4096]{1,0:T(8,128)(2,1)S(1)} %add_convert_fusion.17), channel_id=1, source_target_pairs={{0,2},{1,3},{2,0},{3,1},{4,6},{5,7},{6,4},{7,5},{8,10},{9,11},{10,... | collective-permute-start | bytes 786440 | tf_op jit(solution)/shard_map/ppermute | solution.py:23
  73.3 15.9 %collective-permute-start.33 = (bf16[32,4224]{1,0:T(8,128)(2,1)S(1)}, bf16[32,4224]{1,0:T(8,128)(2,1)S(1)}, u32[]{:S(2)}, u32[]{:S(2)}) collective-permute-start(bf16[32,4224]{1,0:T(8,128)(2,1)S(1)} %fusion.1.refs_0_), channel_id=1, source_target_pairs={{0,2},{1,3},{2,0},{3,1},{4,6},{5,7},{6,4},{7,5},{8,10},{9,11},{10,... | collective-permute-start | bytes 811016 | tf_op jit(solution)/shard_map/ppermute | solution.py:23
  73.4 14.4 %collective-permute-start.10 = (bf16[32,4224]{1,0:T(8,128)(2,1)S(1)}, bf16[32,4224]{1,0:T(8,128)(2,1)S(1)}, u32[]{:S(2)}, u32[]{:S(2)}) collective-permute-start(bf16[32,4224]{1,0:T(8,128)(2,1)S(1)} %fusion.1.refs_0_), channel_id=1, source_target_pairs={{0,1},{1,0},{2,3},{3,2},{4,5},{5,4},{6,7},{7,6},{8,9},{9,8},{10,11... | collective-permute-start | bytes 811016 | tf_op jit(solution)/shard_map/ppermute | solution.py:23
  75.6 13.9 %collective-permute-start.13 = (bf16[32,4224]{1,0:T(8,128)(2,1)S(1)}, bf16[32,4224]{1,0:T(8,128)(2,1)S(1)}, u32[]{:S(2)}, u32[]{:S(2)}) collective-permute-start(bf16[32,4224]{1,0:T(8,128)(2,1)S(1)} %fusion.1.refs_0_), channel_id=1, source_target_pairs={{0,8},{4,20},{8,0},{12,28},{16,24},{20,4},{24,16},{28,12},{1,9},{5... | collective-permute-start | bytes 811016 | tf_op jit(solution)/shard_map/ppermute | solution.py:35
  77.2 12.7 %collective-permute-start.11 = (bf16[32,4224]{1,0:T(8,128)(2,1)S(1)}, bf16[32,4224]{1,0:T(8,128)(2,1)S(1)}, u32[]{:S(2)}, u32[]{:S(2)}) collective-permute-start(bf16[32,4224]{1,0:T(8,128)(2,1)S(1)} %fusion.1.refs_0_), channel_id=1, source_target_pairs={{0,4},{4,0},{8,12},{12,8},{16,20},{20,16},{24,28},{28,24},{1,5},{5... | collective-permute-start | bytes 811016 | tf_op jit(solution)/shard_map/ppermute | solution.py:19
  87.8 10.9 %collective-permute-start.14 = (bf16[32,4224]{1,0:T(8,128)(2,1)S(1)}, bf16[32,4224]{1,0:T(8,128)(2,1)S(1)}, u32[]{:S(2)}, u32[]{:S(2)}) collective-permute-start(bf16[32,4224]{1,0:T(8,128)(2,1)S(1)} %collective-permute-done.10.refs_1_), channel_id=1, source_target_pairs={{0,8},{4,20},{8,0},{12,28},{16,24},{20,4},{24,16},{28,12},{1,9},{5... | collective-permute-start | bytes 811016 | tf_op jit(solution)/shard_map/ppermute | solution.py:35
  89.3 11.0 %collective-permute-start.12 = (bf16[32,4224]{1,0:T(8,128)(2,1)S(1)}, bf16[32,4224]{1,0:T(8,128)(2,1)S(1)}, u32[]{:S(2)}, u32[]{:S(2)}) collective-permute-start(bf16[32,4224]{1,0:T(8,128)(2,1)S(1)} %collective-permute-done.10.refs_1_), channel_id=1, source_target_pairs={{0,4},{4,0},{8,12},{12,8},{16,20},{20,16},{24,28},{28,24},{1,5},{5... | collective-permute-start | bytes 811016 | tf_op jit(solution)/shard_map/ppermute | solution.py:19
  89.3 8.9 %collective-permute-start.34 = (bf16[32,4224]{1,0:T(8,128)(2,1)S(1)}, bf16[32,4224]{1,0:T(8,128)(2,1)S(1)}, u32[]{:S(2)}, u32[]{:S(2)}) collective-permute-start(bf16[32,4224]{1,0:T(8,128)(2,1)S(1)} %collective-permute-done.33), channel_id=1, source_target_pairs={{0,1},{1,0},{2,3},{3,2},{4,5},{5,4},{6,7},{7,6},{8,9},{9,8},{10,11... | collective-permute-start | bytes 811016 | tf_op jit(solution)/shard_map/ppermute | solution.py:23
  89.5 12.2 %collective-permute-start.19 = (bf16[32,4224]{1,0:T(8,128)(2,1)S(1)}, bf16[32,4224]{1,0:T(8,128)(2,1)S(1)}, u32[]{:S(2)}, u32[]{:S(2)}) collective-permute-start(bf16[32,4224]{1,0:T(8,128)(2,1)S(1)} %collective-permute-done.13.refs_4_), channel_id=1, source_target_pairs={{0,4},{4,0},{8,12},{12,8},{16,20},{20,16},{24,28},{28,24},{1,5},{5... | collective-permute-start | bytes 811016 | tf_op jit(solution)/shard_map/ppermute | solution.py:19
  89.9 12.0 %collective-permute-start.17 = (bf16[32,4224]{1,0:T(8,128)(2,1)S(1)}, bf16[32,4224]{1,0:T(8,128)(2,1)S(1)}, u32[]{:S(2)}, u32[]{:S(2)}) collective-permute-start(bf16[32,4224]{1,0:T(8,128)(2,1)S(1)} %collective-permute-done.13.refs_4_), channel_id=1, source_target_pairs={{0,16},{4,12},{8,24},{12,4},{16,0},{20,28},{24,8},{28,20},{1,17},{... | collective-permute-start | bytes 811016 | tf_op jit(solution)/shard_map/ppermute | solution.py:35
  98.2 9.2 %collective-permute-start.15 = (bf16[32,4224]{1,0:T(8,128)(2,1)S(1)}, bf16[32,4224]{1,0:T(8,128)(2,1)S(1)}, u32[]{:S(2)}, u32[]{:S(2)}) collective-permute-start(bf16[32,4224]{1,0:T(8,128)(2,1)S(1)} %collective-permute-done.11.refs_2_), channel_id=1, source_target_pairs={{0,8},{4,20},{8,0},{12,28},{16,24},{20,4},{24,16},{28,12},{1,9},{5... | collective-permute-start | bytes 811016 | tf_op jit(solution)/shard_map/ppermute | solution.py:35
  98.7 9.4 %collective-permute-start.18 = (bf16[32,4224]{1,0:T(8,128)(2,1)S(1)}, bf16[32,4224]{1,0:T(8,128)(2,1)S(1)}, u32[]{:S(2)}, u32[]{:S(2)}) collective-permute-start(bf16[32,4224]{1,0:T(8,128)(2,1)S(1)} %collective-permute-done.14.refs_5_), channel_id=1, source_target_pairs={{0,16},{4,12},{8,24},{12,4},{16,0},{20,28},{24,8},{28,20},{1,17},{... | collective-permute-start | bytes 811016 | tf_op jit(solution)/shard_map/ppermute | solution.py:35
  100.2 10.0 %collective-permute-start.16 = (bf16[32,4224]{1,0:T(8,128)(2,1)S(1)}, bf16[32,4224]{1,0:T(8,128)(2,1)S(1)}, u32[]{:S(2)}, u32[]{:S(2)}) collective-permute-start(bf16[32,4224]{1,0:T(8,128)(2,1)S(1)} %collective-permute-done.12.refs_3_), channel_id=1, source_target_pairs={{0,8},{4,20},{8,0},{12,28},{16,24},{20,4},{24,16},{28,12},{1,9},{5... | collective-permute-start | bytes 811016 | tf_op jit(solution)/shard_map/ppermute | solution.py:35
  101.8 9.4 %collective-permute-start.20 = (bf16[32,4224]{1,0:T(8,128)(2,1)S(1)}, bf16[32,4224]{1,0:T(8,128)(2,1)S(1)}, u32[]{:S(2)}, u32[]{:S(2)}) collective-permute-start(bf16[32,4224]{1,0:T(8,128)(2,1)S(1)} %collective-permute-done.14.refs_5_), channel_id=1, source_target_pairs={{0,4},{4,0},{8,12},{12,8},{16,20},{20,16},{24,28},{28,24},{1,5},{5... | collective-permute-start | bytes 811016 | tf_op jit(solution)/shard_map/ppermute | solution.py:19
  101.9 8.5 %collective-permute-start.23 = (bf16[32,4224]{1,0:T(8,128)(2,1)S(1)}, bf16[32,4224]{1,0:T(8,128)(2,1)S(1)}, u32[]{:S(2)}, u32[]{:S(2)}) collective-permute-start(bf16[32,4224]{1,0:T(8,128)(2,1)S(1)} %collective-permute-done.17.refs_8_), channel_id=1, source_target_pairs={{0,4},{4,0},{8,12},{12,8},{16,20},{20,16},{24,28},{28,24},{1,5},{5... | collective-permute-start | bytes 811016 | tf_op jit(solution)/shard_map/ppermute | solution.py:19
  107.4 3.5 %collective-permute-start.21 = (bf16[32,4224]{1,0:T(8,128)(2,1)S(1)}, bf16[32,4224]{1,0:T(8,128)(2,1)S(1)}, u32[]{:S(2)}, u32[]{:S(2)}) collective-permute-start(bf16[32,4224]{1,0:T(8,128)(2,1)S(1)} %collective-permute-done.15.refs_6_), channel_id=1, source_target_pairs={{0,4},{4,0},{8,12},{12,8},{16,20},{20,16},{24,28},{28,24},{1,5},{5... | collective-permute-start | bytes 811016 | tf_op jit(solution)/shard_map/ppermute | solution.py:19
  108.1 4.4 %collective-permute-start.24 = (bf16[32,4224]{1,0:T(8,128)(2,1)S(1)}, bf16[32,4224]{1,0:T(8,128)(2,1)S(1)}, u32[]{:S(2)}, u32[]{:S(2)}) collective-permute-start(bf16[32,4224]{1,0:T(8,128)(2,1)S(1)} %collective-permute-done.18.refs_9_), channel_id=1, source_target_pairs={{0,4},{4,0},{8,12},{12,8},{16,20},{20,16},{24,28},{28,24},{1,5},{5... | collective-permute-start | bytes 811016 | tf_op jit(solution)/shard_map/ppermute | solution.py:19
  110.3 2.2 collective-permute-start.22
  110.3 24.6 %collective-permute-start.55 = (bf16[128,4096]{1,0:T(8,128)(2,1)S(1)}, bf16[128,4096]{1,0:T(8,128)(2,1)S(1)}, u32[]{:S(2)}, u32[]{:S(2)}) collective-permute-start(bf16[128,4096]{1,0:T(8,128)(2,1)S(1)} %constant_dynamic-update-slice_fusion.2.refs_0_), channel_id=1, source_target_pairs={{0,8},{4,20},{8,0},{12,28},{16,24},{20,4},{24,16},{28,12},{1,9},{5... | collective-permute-start | bytes 3145736 | tf_op jit(solution)/shard_map/ppermute | solution.py:35
  110.9 24.7 %collective-permute-start.54 = (bf16[128,4096]{1,0:T(8,128)(2,1)S(1)}, bf16[128,4096]{1,0:T(8,128)(2,1)S(1)}, u32[]{:S(2)}, u32[]{:S(2)}) collective-permute-start(bf16[128,4096]{1,0:T(8,128)(2,1)S(1)} %constant_dynamic-update-slice_fusion.2.refs_0_), channel_id=1, source_target_pairs={{0,4},{4,0},{8,12},{12,8},{16,20},{20,16},{24,28},{28,24},{1,5},{5... | collective-permute-start | bytes 3145736 | tf_op jit(solution)/shard_map/ppermute | solution.py:19
  111.1 26.0 %collective-permute-start.36 = (bf16[64,4224]{1,0:T(8,128)(2,1)S(1)}, bf16[64,4224]{1,0:T(8,128)(2,1)S(1)}, u32[]{:S(2)}, u32[]{:S(2)}) collective-permute-start(bf16[64,4224]{1,0:T(8,128)(2,1)S(1)} %constant_dynamic-update-slice_fusion.refs_0_), channel_id=1, source_target_pairs={{0,8},{4,20},{8,0},{12,28},{16,24},{20,4},{24,16},{28,12},{1,9},{5... | collective-permute-start | bytes 1622024 | tf_op jit(solution)/shard_map/ppermute | solution.py:35
  112.5 24.7 %collective-permute-start.35 = (bf16[64,4224]{1,0:T(8,128)(2,1)S(1)}, bf16[64,4224]{1,0:T(8,128)(2,1)S(1)}, u32[]{:S(2)}, u32[]{:S(2)}) collective-permute-start(bf16[64,4224]{1,0:T(8,128)(2,1)S(1)} %constant_dynamic-update-slice_fusion.refs_0_), channel_id=1, source_target_pairs={{0,4},{4,0},{8,12},{12,8},{16,20},{20,16},{24,28},{28,24},{1,5},{5... | collective-permute-start | bytes 1622024 | tf_op jit(solution)/shard_map/ppermute | solution.py:19
  134.4 3.3 %collective-permute-start.25 = (bf16[64,4096]{1,0:T(8,128)(2,1)S(1)}, bf16[64,4096]{1,0:T(8,128)(2,1)S(1)}, u32[]{:S(2)}, u32[]{:S(2)}) collective-permute-start(bf16[64,4096]{1,0:T(8,128)(2,1)S(1)} %get-tuple-element.43), channel_id=1, source_target_pairs={{0,4},{4,0},{8,12},{12,8},{16,20},{20,16},{24,28},{28,24},{1,5},{5... | collective-permute-start | bytes 1572872 | tf_op jit(solution)/shard_map/ppermute | solution.py:19
  135.0 37.8 %collective-permute-start.57 = (bf16[128,4096]{1,0:T(8,128)(2,1)S(1)}, bf16[128,4096]{1,0:T(8,128)(2,1)S(1)}, u32[]{:S(2)}, u32[]{:S(2)}) collective-permute-start(bf16[128,4096]{1,0:T(8,128)(2,1)S(1)} %collective-permute-done.55.refs_2_), channel_id=1, source_target_pairs={{0,16},{4,12},{8,24},{12,4},{16,0},{20,28},{24,8},{28,20},{1,17},{... | collective-permute-start | bytes 3145736 | tf_op jit(solution)/shard_map/ppermute | solution.py:35
  135.7 37.2 %collective-permute-start.56 = (bf16[128,4096]{1,0:T(8,128)(2,1)S(1)}, bf16[128,4096]{1,0:T(8,128)(2,1)S(1)}, u32[]{:S(2)}, u32[]{:S(2)}) collective-permute-start(bf16[128,4096]{1,0:T(8,128)(2,1)S(1)} %collective-permute-done.54.refs_1_), channel_id=1, source_target_pairs={{0,8},{4,20},{8,0},{12,28},{16,24},{20,4},{24,16},{28,12},{1,9},{5... | collective-permute-start | bytes 3145736 | tf_op jit(solution)/shard_map/ppermute | solution.py:35
  137.2 2.1 collective-permute-start.29
  137.2 34.9 %collective-permute-start.38 = (bf16[64,4224]{1,0:T(8,128)(2,1)S(1)}, bf16[64,4224]{1,0:T(8,128)(2,1)S(1)}, u32[]{:S(2)}, u32[]{:S(2)}) collective-permute-start(bf16[64,4224]{1,0:T(8,128)(2,1)S(1)} %collective-permute-done.36.refs_2_), channel_id=1, source_target_pairs={{0,16},{4,12},{8,24},{12,4},{16,0},{20,28},{24,8},{28,20},{1,17},{... | collective-permute-start | bytes 1622024 | tf_op jit(solution)/shard_map/ppermute | solution.py:35
  137.7 34.4 %collective-permute-start.37 = (bf16[64,4224]{1,0:T(8,128)(2,1)S(1)}, bf16[64,4224]{1,0:T(8,128)(2,1)S(1)}, u32[]{:S(2)}, u32[]{:S(2)}) collective-permute-start(bf16[64,4224]{1,0:T(8,128)(2,1)S(1)} %collective-permute-done.35.refs_1_), channel_id=1, source_target_pairs={{0,8},{4,20},{8,0},{12,28},{16,24},{20,4},{24,16},{28,12},{1,9},{5... | collective-permute-start | bytes 1622024 | tf_op jit(solution)/shard_map/ppermute | solution.py:35
  139.2 34.1 %collective-permute-start.39 = (bf16[64,4224]{1,0:T(8,128)(2,1)S(1)}, bf16[64,4224]{1,0:T(8,128)(2,1)S(1)}, u32[]{:S(2)}, u32[]{:S(2)}) collective-permute-start(bf16[64,4224]{1,0:T(8,128)(2,1)S(1)} %collective-permute-done.36.refs_2_), channel_id=1, source_target_pairs={{0,4},{4,0},{8,12},{12,8},{16,20},{20,16},{24,28},{28,24},{1,5},{5... | collective-permute-start | bytes 1622024 | tf_op jit(solution)/shard_map/ppermute | solution.py:19
  172.1 1.9 collective-permute-start.41
  172.1 2.7 %collective-permute-start.40 = (bf16[64,4224]{1,0:T(8,128)(2,1)S(1)}, bf16[64,4224]{1,0:T(8,128)(2,1)S(1)}, u32[]{:S(2)}, u32[]{:S(2)}) collective-permute-start(bf16[64,4224]{1,0:T(8,128)(2,1)S(1)} %collective-permute-done.37.refs_3_), channel_id=1, source_target_pairs={{0,4},{4,0},{8,12},{12,8},{16,20},{20,16},{24,28},{28,24},{1,5},{5... | collective-permute-start | bytes 1622024 | tf_op jit(solution)/shard_map/ppermute | solution.py:19
  172.7 53.5 %collective-permute-start.58 = (bf16[128,4096]{1,0:T(8,128)(2,1)S(1)}, bf16[128,4096]{1,0:T(8,128)(2,1)S(1)}, u32[]{:S(2)}, u32[]{:S(2)}) collective-permute-start(bf16[128,4096]{1,0:T(8,128)(2,1)S(1)} %collective-permute-done.55.refs_2_), channel_id=1, source_target_pairs={{0,4},{4,0},{8,12},{12,8},{16,20},{20,16},{24,28},{28,24},{1,5},{5... | collective-permute-start | bytes 3145736 | tf_op jit(solution)/shard_map/ppermute | solution.py:19
  172.8 24.9 %collective-permute-start.28 = (bf16[64,4096]{1,0:T(8,128)(2,1)S(1)}, bf16[64,4096]{1,0:T(8,128)(2,1)S(1)}, u32[]{:S(2)}, u32[]{:S(2)}) collective-permute-start(bf16[64,4096]{1,0:T(8,128)(2,1)S(1)} %get-tuple-element.45), channel_id=1, source_target_pairs={{0,4},{4,0},{8,12},{12,8},{16,20},{20,16},{24,28},{28,24},{1,5},{5... | collective-permute-start | bytes 1572872 | tf_op jit(solution)/shard_map/ppermute | solution.py:19
  173.3 53.3 %collective-permute-start.60 = (bf16[128,4096]{1,0:T(8,128)(2,1)S(1)}, bf16[128,4096]{1,0:T(8,128)(2,1)S(1)}, u32[]{:S(2)}, u32[]{:S(2)}) collective-permute-start(bf16[128,4096]{1,0:T(8,128)(2,1)S(1)} %collective-permute-done.57.refs_4_), channel_id=1, source_target_pairs={{0,4},{4,0},{8,12},{12,8},{16,20},{20,16},{24,28},{28,24},{1,5},{5... | collective-permute-start | bytes 3145736 | tf_op jit(solution)/shard_map/ppermute | solution.py:19
  174.0 53.7 %collective-permute-start.59 = (bf16[128,4096]{1,0:T(8,128)(2,1)S(1)}, bf16[128,4096]{1,0:T(8,128)(2,1)S(1)}, u32[]{:S(2)}, u32[]{:S(2)}) collective-permute-start(bf16[128,4096]{1,0:T(8,128)(2,1)S(1)} %collective-permute-done.56.refs_3_), channel_id=1, source_target_pairs={{0,4},{4,0},{8,12},{12,8},{16,20},{20,16},{24,28},{28,24},{1,5},{5... | collective-permute-start | bytes 3145736 | tf_op jit(solution)/shard_map/ppermute | solution.py:19
  174.8 23.0 %collective-permute-start.30 = (bf16[64,4096]{1,0:T(8,128)(2,1)S(1)}, bf16[64,4096]{1,0:T(8,128)(2,1)S(1)}, u32[]{:S(2)}, u32[]{:S(2)}) collective-permute-start(bf16[64,4096]{1,0:T(8,128)(2,1)S(1)} %add_convert_fusion.9), channel_id=1, source_target_pairs={{0,16},{4,12},{8,24},{12,4},{16,0},{20,28},{24,8},{28,20},{1,17},{... | collective-permute-start | bytes 1572872 | tf_op jit(solution)/shard_map/ppermute | solution.py:35
  197.7 2.0 collective-permute-start.42
  198.0 14.1 %collective-permute-start.45 = (bf16[64,4096]{1,0:T(8,128)(2,1)S(1)}, bf16[64,4096]{1,0:T(8,128)(2,1)S(1)}, u32[]{:S(2)}, u32[]{:S(2)}) collective-permute-start(bf16[64,4096]{1,0:T(8,128)(2,1)S(1)} %get-tuple-element.54), channel_id=1, source_target_pairs={{0,4},{4,0},{8,12},{12,8},{16,20},{20,16},{24,28},{28,24},{1,5},{5... | collective-permute-start | bytes 1572872 | tf_op jit(solution)/shard_map/ppermute | solution.py:19
  199.7 1.9 collective-permute-start.46
  201.6 9.2 %collective-permute-start.43 = (bf16[64,4096]{1,0:T(8,128)(2,1)S(1)}, bf16[64,4096]{1,0:T(8,128)(2,1)S(1)}, u32[]{:S(2)}, u32[]{:S(2)}) collective-permute-start(bf16[64,4096]{1,0:T(8,128)(2,1)S(1)} %add_convert_fusion.6), channel_id=1, source_target_pairs={{0,8},{4,20},{8,0},{12,28},{16,24},{20,4},{24,16},{28,12},{1,9},{5... | collective-permute-start | bytes 1572872 | tf_op jit(solution)/shard_map/ppermute | solution.py:35
  210.8 14.2 %collective-permute-start.47 = (bf16[64,4096]{1,0:T(8,128)(2,1)S(1)}, bf16[64,4096]{1,0:T(8,128)(2,1)S(1)}, u32[]{:S(2)}, u32[]{:S(2)}) collective-permute-start(bf16[64,4096]{1,0:T(8,128)(2,1)S(1)} %add_convert_fusion.2), channel_id=1, source_target_pairs={{0,16},{4,12},{8,24},{12,4},{16,0},{20,28},{24,8},{28,20},{1,17},{... | collective-permute-start | bytes 1572872 | tf_op jit(solution)/shard_map/ppermute | solution.py:35
  212.1 13.1 %collective-permute-start.26 = (bf16[64,4096]{1,0:T(8,128)(2,1)S(1)}, bf16[64,4096]{1,0:T(8,128)(2,1)S(1)}, u32[]{:S(2)}, u32[]{:S(2)}) collective-permute-start(bf16[64,4096]{1,0:T(8,128)(2,1)S(1)} %add_convert_fusion.13), channel_id=1, source_target_pairs={{0,8},{4,20},{8,0},{12,28},{16,24},{20,4},{24,16},{28,12},{1,9},{5... | collective-permute-start | bytes 1572872 | tf_op jit(solution)/shard_map/ppermute | solution.py:35
  225.0 9.5 %collective-permute-start.44 = (bf16[64,4096]{1,0:T(8,128)(2,1)S(1)}, bf16[64,4096]{1,0:T(8,128)(2,1)S(1)}, u32[]{:S(2)}, u32[]{:S(2)}) collective-permute-start(bf16[64,4096]{1,0:T(8,128)(2,1)S(1)} %add_convert_fusion.5), channel_id=1, source_target_pairs={{0,4},{4,0},{8,12},{12,8},{16,20},{20,16},{24,28},{28,24},{1,5},{5... | collective-permute-start | bytes 1572872 | tf_op jit(solution)/shard_map/ppermute | solution.py:19
  225.2 9.2 %collective-permute-start.48 = (bf16[64,4096]{1,0:T(8,128)(2,1)S(1)}, bf16[64,4096]{1,0:T(8,128)(2,1)S(1)}, u32[]{:S(2)}, u32[]{:S(2)}) collective-permute-start(bf16[64,4096]{1,0:T(8,128)(2,1)S(1)} %add_convert_fusion.1), channel_id=1, source_target_pairs={{0,8},{4,20},{8,0},{12,28},{16,24},{20,4},{24,16},{28,12},{1,9},{5... | collective-permute-start | bytes 1572872 | tf_op jit(solution)/shard_map/ppermute | solution.py:35
  226.3 8.9 %collective-permute-start.27 = (bf16[64,4096]{1,0:T(8,128)(2,1)S(1)}, bf16[64,4096]{1,0:T(8,128)(2,1)S(1)}, u32[]{:S(2)}, u32[]{:S(2)}) collective-permute-start(bf16[64,4096]{1,0:T(8,128)(2,1)S(1)} %add_convert_fusion.12), channel_id=1, source_target_pairs={{0,4},{4,0},{8,12},{12,8},{16,20},{20,16},{24,28},{28,24},{1,5},{5... | collective-permute-start | bytes 1572872 | tf_op jit(solution)/shard_map/ppermute | solution.py:19
  226.6 13.5 %collective-permute-start.31 = (bf16[64,4096]{1,0:T(8,128)(2,1)S(1)}, bf16[64,4096]{1,0:T(8,128)(2,1)S(1)}, u32[]{:S(2)}, u32[]{:S(2)}) collective-permute-start(bf16[64,4096]{1,0:T(8,128)(2,1)S(1)} %add_convert_fusion.8), channel_id=1, source_target_pairs={{0,8},{4,20},{8,0},{12,28},{16,24},{20,4},{24,16},{28,12},{1,9},{5... | collective-permute-start | bytes 1572872 | tf_op jit(solution)/shard_map/ppermute | solution.py:35
  234.7 8.6 %collective-permute-start.49 = (bf16[32,4096]{1,0:T(8,128)(2,1)S(1)}, bf16[32,4096]{1,0:T(8,128)(2,1)S(1)}, u32[]{:S(2)}, u32[]{:S(2)}) collective-permute-start(bf16[32,4096]{1,0:T(8,128)(2,1)S(1)} %slice.19), channel_id=1, source_target_pairs={{0,1},{1,0},{2,3},{3,2},{4,5},{5,4},{6,7},{7,6},{8,9},{9,8},{10,11... | collective-permute-start | bytes 786440 | tf_op jit(solution)/shard_map/ppermute | solution.py:23
  240.3 11.9 %collective-permute-start.32 = (bf16[32,4096]{1,0:T(8,128)(2,1)S(1)}, bf16[32,4096]{1,0:T(8,128)(2,1)S(1)}, u32[]{:S(2)}, u32[]{:S(2)}) collective-permute-start(bf16[32,4096]{1,0:T(8,128)(2,1)S(1)} %slice.17), channel_id=1, source_target_pairs={{0,1},{1,0},{2,3},{3,2},{4,5},{5,4},{6,7},{7,6},{8,9},{9,8},{10,11... | collective-permute-start | bytes 786440 | tf_op jit(solution)/shard_map/ppermute | solution.py:23
  243.4 13.6 %collective-permute-start.50 = (bf16[32,4096]{1,0:T(8,128)(2,1)S(1)}, bf16[32,4096]{1,0:T(8,128)(2,1)S(1)}, u32[]{:S(2)}, u32[]{:S(2)}) collective-permute-start(bf16[32,4096]{1,0:T(8,128)(2,1)S(1)} %add_convert_fusion.15), channel_id=1, source_target_pairs={{0,2},{1,3},{2,0},{3,1},{4,6},{5,7},{6,4},{7,5},{8,10},{9,11},{10,... | collective-permute-start | bytes 786440 | tf_op jit(solution)/shard_map/ppermute | solution.py:23

commit v5 on v4

--- a/solution.py
+++ b/solution.py
@@ -213,20 +213,21 @@
         at += ref.shape[0]
 
 
-def fall(hidden, down_mat, counts):
+def fall(hidden, down_mat, counts, turn):
     units, width = down_mat.shape
-    broad = min(1024, width)
+    rows = sum(counts)
+    broad = min(2048, width)
     column = lambda i: (0, i)
     return pl.pallas_call(
         fall_kernel,
         out_shape=[jax.ShapeDtypeStruct((c, width), jnp.bfloat16) for c in counts],
         grid=(width // broad,),
         in_specs=[
-            pl.BlockSpec(hidden.shape, lambda i: (0, 0), pipeline_mode=pl.Buffered(1)),
+            pl.BlockSpec((rows, units), lambda i: (turn, 0), pipeline_mode=pl.Buffered(1)),
             pl.BlockSpec((units, broad), column),
         ],
         out_specs=[pl.BlockSpec((c, broad), column) for c in counts],
-        compiler_params=pltpu.CompilerParams(vmem_limit_bytes=20 << 20),
+        compiler_params=pltpu.CompilerParams(vmem_limit_bytes=24 << 20),
         cost_estimate=pl.CostEstimate(
             flops=2 * sum(counts) * width * units,
             transcendentals=0,
@@ -583,7 +584,12 @@
         counts.append([plain.shape[0] // pieces] * pieces)
     layer = hidden_one
     for k in range(0, planes, 2):
-        parts = fall(hidden[k // 2], down_mat, counts[k // 2])
+        sizes = counts[k // 2]
+        if k and len(sizes) == 8:
+            leaving = fall(hidden[k // 2], down_mat, sizes[4:], 1)
+            parts = fall(hidden[k // 2], down_mat, sizes[:4], 0) + leaving
+        else:
+            parts = fall(hidden[k // 2], down_mat, sizes, 0)
         summed = scatter(parts)
         both = plus(summed[:row_count], swap_plane(summed[row_count:], 1))
         if k:

time: 258 us -> 259 us (level)
    pallas_call x2 -> x3, Pallas kernels: 14.6 us -> 17.1 us  [fall(): pl.pallas_call(fall_kernel, out_shape=[jax.ShapeDtypeStruct((c, width), j...]
  transfers between devices with their start and end apart: 61 -> 61, of which waited for: 21 -> 20; matrix products, arithmetic and copies ran while one was open for 2% -> 2% of each run, Pallas kernels for 28% -> 29%
where the time goes in v5:
time: 259 us
  waiting for transfers between devices  132 us (51%)
  Pallas kernels  76.5 us (30%)
  starting transfers between devices  43.9 us (17%)
  other arithmetic  3.65 us (1%)
    ppermute x21, waiting for transfers between devices, cross(): return lax.ppermute(value, 'ctx', pairs)  75.7 us
    ppermute x12, waiting for transfers between devices, swap_plane(): lax.ppermute(value, 'exp', [(i, i ^ bits) for i in range(lax.axis_size('e...  53.1 us
    pallas_call x2, Pallas kernels, rise(): pl.pallas_call(functools.partial(rise_kernel, len(rows)), out_shape=[jax....  29.1 us
    ppermute x21, starting transfers between devices, cross(): return lax.ppermute(value, 'ctx', pairs)  26.6 us
    pallas_call x3, Pallas kernels, fall(): pl.pallas_call(fall_kernel, out_shape=[jax.ShapeDtypeStruct((c, width), j...  17.1 us
    pallas_call x2, Pallas kernels, outer(): pl.pallas_call(functools.partial(outer_kernel, len(grads), pieces, blocks...  13.5 us
    ppermute x12, starting transfers between devices, swap_plane(): lax.ppermute(value, 'exp', [(i, i ^ bits) for i in range(lax.axis_size('e...  12.5 us
    pallas_call x2, Pallas kernels, attend(): pl.pallas_call(functools.partial(attend_kernel, slots, cached, window_fre...  9.09 us
  transfers between devices with their start and end apart: 61, of which 20 were waited for; matrix products, arithmetic and copies ran while one was open for 2% of the time, Pallas kernels for 29%

profile of v5, /device:TPU:0, one launch (start us, length us, event | category | flops | bytes accessed | tf_op | source)
XLA Modules:
  0.0 259.1 jit_solution(18094732243852587670)
XLA Ops:
  0.6 1.0 pack.1.refs_2_.refs_4_
  1.6 0.6 collective-permute-start.1
  2.2 2.6 collective-permute-start
  4.8 1.6 collective-permute-start.2
  6.4 4.1 %collective-permute-done.refs_2_.refs_8_ = bf16[2,384,256]{2,1,0:T(8,128)(2,1)S(1)} collective-permute-done((bf16[2,384,256]{2,1,0:T(8,128)(2,1)S(1)}, bf16[2,384,256]{2,1,0:T(8,128)(2,1)S(1)}, u32[]{:S(2)}, u32[]{:S(2)}) %collective-permute-start) | collective-permute-done | bytes 393248 | tf_op jit(solution)/shard_map/ppermute | solution.py:35
  10.5 2.0 collective-permute-start.5
  12.6 3.9 %collective-permute-done.2.refs_3_.refs_9_ = bf16[2,384,256]{2,1,0:T(8,128)(2,1)S(1)} collective-permute-done((bf16[2,384,256]{2,1,0:T(8,128)(2,1)S(1)}, bf16[2,384,256]{2,1,0:T(8,128)(2,1)S(1)}, u32[]{:S(2)}, u32[]{:S(2)}) %collective-permute-start.2) | collective-permute-done | bytes 393248 | tf_op jit(solution)/shard_map/ppermute | solution.py:35
  16.5 2.2 collective-permute-done.5.refs_6_.refs_12_
  18.8 2.0 collective-permute-start.51
  20.9 2.5 collective-permute-start.53
  23.9 1.2 relay.3.place
  25.0 0.7 convert_element_type.178
  25.8 0.8 copy-done
  26.8 3.1 %attend.2 = (f32[2,512,128]{2,1,0:T(8,128)S(1)}, f32[2,512,128]{2,1,0:T(8,128)S(1)}, f32[2,512,128]{2,1,0:T(8,128)S(1)}) custom-call(s32[4]{0:T(128)S(1)} %pad_add_fusion.refs_0_, bf16[128,1024]{1,0:T(8,128)(2,1)} %refs_1_.3, bf16[2,384,256]{2,1,0:T(8,128)(2,1)S(1)} %pack.1.refs_2_.refs_4_, bf16[2,384,256]{2,1,0:T(8,128)(2,1)S(1)} %collective-permute-done.1.refs_3_.refs_5_, ...), custom_call_target="tpu_custom_call" | custom-call | flops 402653184 | bytes 1572864 | tf_op jit(solution)/shard_map/attend/pallas_call | solution.py:459
  30.1 5.9 %attend.3.attn_ref = bf16[128,1024]{1,0:T(8,128)(2,1)S(1)} custom-call(s32[12]{0:T(128)S(1)} %stack.63.refs_0_, bf16[128,1024]{1,0:T(8,128)(2,1)} %refs_1_.3, bf16[2,384,256]{2,1,0:T(8,128)(2,1)S(1)} %collective-permute-done.refs_2_.refs_8_, bf16[2,384,256]{2,1,0:T(8,128)(2,1)S(1)} %collective-permute-done.2.refs_3_.refs_9_, ...), custom_call_target="tpu_custom_call" | custom-call | flops 1207959552 | bytes 4718592 | tf_op jit(solution)/shard_map/attend/pallas_call | solution.py:459
  36.1 5.1 %project.1 = (f32[32,4096]{1,0:T(8,128)S(1)}, bf16[32,4096]{1,0:T(8,128)(2,1)S(1)}, f32[32,4096]{1,0:T(8,128)S(1)}, bf16[32,4096]{1,0:T(8,128)(2,1)S(1)}) custom-call(s32[1]{0:T(128)} %bitcast.place.in_ref, bf16[128,1024]{1,0:T(8,128)(2,1)S(1)} %attend.3.attn_ref, bf16[1024,4096]{1,0:T(8,128)(2,1)} %proj_ref.1, bf16[32,4096]{1,0:T(8,128)(2,1)} %residual_ref.1), custom_call_target="tpu_custom_call" | custom-call | flops 1073741824 | bytes 8388608 | tf_op jit(solution)/shard_map/project/pallas_call | solution.py:260
  41.2 1.9 collective-permute-start.7
  43.3 14.8 %collective-permute-done.8 = bf16[32,4096]{1,0:T(8,128)(2,1)S(1)} collective-permute-done((bf16[32,4096]{1,0:T(8,128)(2,1)S(1)}, bf16[32,4096]{1,0:T(8,128)(2,1)S(1)}, u32[]{:S(2)}, u32[]{:S(2)}) %collective-permute-start.8) | collective-permute-done | bytes 262176 | tf_op jit(solution)/shard_map/ppermute | solution.py:23
  58.2 0.8 collective-permute-start.9
  58.9 1.0 constant_dynamic-update-slice_fusion.4
  59.9 13.0 %collective-permute-done.9 = bf16[32,4096]{1,0:T(8,128)(2,1)S(1)} collective-permute-done((bf16[32,4096]{1,0:T(8,128)(2,1)S(1)}, bf16[32,4096]{1,0:T(8,128)(2,1)S(1)}, u32[]{:S(2)}, u32[]{:S(2)}) %collective-permute-start.9) | collective-permute-done | bytes 262176 | tf_op jit(solution)/shard_map/ppermute | solution.py:23
  73.4 2.2 collective-permute-start.10
  75.6 1.6 collective-permute-start.13
  77.2 10.6 %collective-permute-done.10.refs_1_ = bf16[32,4224]{1,0:T(8,128)(2,1)S(1)} collective-permute-done((bf16[32,4224]{1,0:T(8,128)(2,1)S(1)}, bf16[32,4224]{1,0:T(8,128)(2,1)S(1)}, u32[]{:S(2)}, u32[]{:S(2)}) %collective-permute-start.10) | collective-permute-done | bytes 270368 | tf_op jit(solution)/shard_map/ppermute | solution.py:23
  87.8 1.5 collective-permute-start.14
  89.9 1.5 collective-permute-start.17
  91.4 6.8 %collective-permute-done.34 = bf16[32,4224]{1,0:T(8,128)(2,1)S(1)} collective-permute-done((bf16[32,4224]{1,0:T(8,128)(2,1)S(1)}, bf16[32,4224]{1,0:T(8,128)(2,1)S(1)}, u32[]{:S(2)}, u32[]{:S(2)}) %collective-permute-start.34) | collective-permute-done | bytes 270368 | tf_op jit(solution)/shard_map/ppermute | solution.py:23
  98.7 1.5 collective-permute-start.18
  100.2 1.5 collective-permute-start.16
  102.3 5.0 %collective-permute-done.15.refs_6_ = bf16[32,4224]{1,0:T(8,128)(2,1)S(1)} collective-permute-done((bf16[32,4224]{1,0:T(8,128)(2,1)S(1)}, bf16[32,4224]{1,0:T(8,128)(2,1)S(1)}, u32[]{:S(2)}, u32[]{:S(2)}) %collective-permute-start.15) | collective-permute-done | bytes 270368 | tf_op jit(solution)/shard_map/ppermute | solution.py:35
  107.4 0.7 collective-permute-done.18.refs_9_
  108.1 2.2 collective-permute-done.16.refs_7_
  110.3 0.6 collective-permute-start.55
  111.1 1.4 collective-permute-start.36
  112.5 14.5 %rise.2 = (bf16[512,1024]{1,0:T(8,128)(2,1)S(1)}, bf16[1024,512]{1,0:T(8,128)(2,1)S(1)}) custom-call(s32[1]{0:T(128)} %relay.3.place, bf16[16,4096]{1,0:T(8,128)(2,1)S(1)} %widen.1.router_ref, bf16[32,4224]{1,0:T(8,128)(2,1)S(1)} %fusion.1.refs_0_, bf16[32,4224]{1,0:T(8,128)(2,1)S(1)} %collective-permute-done.10.refs_1_, ...), custom_call_target="tpu_custom_call" | custom-call | flops 8589934592 | bytes 20971520 | tf_op jit(solution)/shard_map/rise/pallas_call | solution.py:175
  127.1 7.4 %fall.3 = (bf16[64,4096]{1,0:T(8,128)(2,1)S(1)}, bf16[64,4096]{1,0:T(8,128)(2,1)S(1)}, bf16[64,4096]{1,0:T(8,128)(2,1)S(1)}, bf16[64,4096]{1,0:T(8,128)(2,1)S(1)...) custom-call(bf16[512,1024]{1,0:T(8,128)(2,1)S(1)} %get-tuple-element, ...), custom_call_target="tpu_custom_call" | custom-call | flops 4294967296 | bytes 12582912 | tf_op jit(solution)/shard_map/fall/pallas_call | solution.py:221
  134.4 0.6 collective-permute-start.25
  135.0 0.7 collective-permute-start.57
  135.7 1.5 collective-permute-start.56
  137.2 0.6 collective-permute-start.38
  137.8 1.4 collective-permute-start.37
  139.4 32.8 %collective-permute-done.38.refs_4_ = bf16[64,4224]{1,0:T(8,128)(2,1)S(1)} collective-permute-done((bf16[64,4224]{1,0:T(8,128)(2,1)S(1)}, bf16[64,4224]{1,0:T(8,128)(2,1)S(1)}, u32[]{:S(2)}, u32[]{:S(2)}) %collective-permute-start.38) | collective-permute-done | bytes 540704 | tf_op jit(solution)/shard_map/ppermute | solution.py:35
  173.4 0.6 collective-permute-done.41.refs_7_
  174.2 0.6 collective-permute-done.40.refs_6_
  174.8 0.9 collective-permute-start.30
  175.7 14.5 %rise.3 = (bf16[512,1024]{1,0:T(8,128)(2,1)S(1)}, bf16[1024,512]{1,0:T(8,128)(2,1)S(1)}) custom-call(s32[1]{0:T(128)} %relay.3.place, bf16[16,4096]{1,0:T(8,128)(2,1)S(1)} %widen.1.router_ref, bf16[64,4224]{1,0:T(8,128)(2,1)S(1)} %constant_dynamic-update-slice_fusion.refs_0_, bf16[64,4224]{1,0:T(8,128)(2,1)S(1)} %collective-permute-done.35.refs_1_, ...), custom_call_target="tpu_custom_call" | custom-call | flops 8589934592 | bytes 20971520 | tf_op jit(solution)/shard_map/rise/pallas_call | solution.py:175
  190.3 4.8 %fall.5 = (bf16[64,4096]{1,0:T(8,128)(2,1)S(1)}, bf16[64,4096]{1,0:T(8,128)(2,1)S(1)}, bf16[64,4096]{1,0:T(8,128)(2,1)S(1)}, bf16[64,4096]{1,0:T(8,128)(2,1)S(1)}) custom-call(bf16[512,1024]{1,0:T(8,128)(2,1)S(1)} %get-tuple-element.48.hidden_ref, bf16[1024,4096]{1,0:T(8,128)(2,1)} %bitcast.24), custom_call_target="tpu_custom_call" | custom-call | flops 2147483648 | bytes 10485760 | tf_op jit(solution)/shard_map/fall/pallas_call | solution.py:221
  196.0 4.8 %fall.4 = (bf16[64,4096]{1,0:T(8,128)(2,1)S(1)}, bf16[64,4096]{1,0:T(8,128)(2,1)S(1)}, bf16[64,4096]{1,0:T(8,128)(2,1)S(1)}, bf16[64,4096]{1,0:T(8,128)(2,1)S(1)}) custom-call(bf16[512,1024]{1,0:T(8,128)(2,1)S(1)} %get-tuple-element.48.hidden_ref, bf16[1024,4096]{1,0:T(8,128)(2,1)} %bitcast.25), custom_call_target="tpu_custom_call" | custom-call | flops 2147483648 | bytes 10485760 | tf_op jit(solution)/shard_map/fall/pallas_call | solution.py:221
  201.0 1.8 collective-permute-done.46
  202.8 1.2 collective-permute-start.43
  204.1 7.9 %collective-permute-done.43 = bf16[64,4096]{1,0:T(8,128)(2,1)S(1)} collective-permute-done((bf16[64,4096]{1,0:T(8,128)(2,1)S(1)}, bf16[64,4096]{1,0:T(8,128)(2,1)S(1)}, u32[]{:S(2)}, u32[]{:S(2)}) %collective-permute-start.43) | collective-permute-done | bytes 524320 | tf_op jit(solution)/shard_map/ppermute | solution.py:35
  212.0 1.2 collective-permute-start.47
  213.3 1.0 collective-permute-start.26
  214.3 11.9 %collective-permute-done.47 = bf16[64,4096]{1,0:T(8,128)(2,1)S(1)} collective-permute-done((bf16[64,4096]{1,0:T(8,128)(2,1)S(1)}, bf16[64,4096]{1,0:T(8,128)(2,1)S(1)}, u32[]{:S(2)}, u32[]{:S(2)}) %collective-permute-start.47) | collective-permute-done | bytes 524320 | tf_op jit(solution)/shard_map/ppermute | solution.py:35
  226.4 0.9 collective-permute-start.48
  227.8 1.1 collective-permute-start.31
  228.9 6.7 %outer.2.refs_10_ = f32[1024,4096]{1,0:T(8,128)} custom-call(bf16[128,4096]{1,0:T(8,128)(2,1)S(1)} %constant_dynamic-update-slice_fusion.2.refs_0_, bf16[128,4096]{1,0:T(8,128)(2,1)S(1)} %collective-permute-done.54.refs_1_, bf16[128,4096]{1,0:T(8,128)(2,1)S(1)} %collective-permute-done.55.refs_2_, bf16[128,4096]{1,0:T(8,128)(2,1)S(1)} %collective-permute-done.56.refs_3_, ...), custom_call_target="tpu_custom_call" | custom-call | flops 4294967296 | bytes 16777216 | tf_op jit(solution)/shard_map/outer/pallas_call | solution.py:317
  236.3 4.9 %collective-permute-done.31 = bf16[64,4096]{1,0:T(8,128)(2,1)S(1)} collective-permute-done((bf16[64,4096]{1,0:T(8,128)(2,1)S(1)}, bf16[64,4096]{1,0:T(8,128)(2,1)S(1)}, u32[]{:S(2)}, u32[]{:S(2)}) %collective-permute-start.31) | collective-permute-done | bytes 524320 | tf_op jit(solution)/shard_map/ppermute | solution.py:35
  242.0 2.5 collective-permute-done.49
  244.6 1.5 collective-permute-start.50
  246.1 6.7 %outer.3 = f32[1024,4096]{1,0:T(8,128)} custom-call(bf16[128,4096]{1,0:T(8,128)(2,1)S(1)} %constant_dynamic-update-slice_fusion.2.refs_0_, bf16[128,4096]{1,0:T(8,128)(2,1)S(1)} %collective-permute-done.54.refs_1_, bf16[128,4096]{1,0:T(8,128)(2,1)S(1)} %collective-permute-done.55.refs_2_, ...), custom_call_target="tpu_custom_call", output_to_operand_aliasing={{}: (10, {})} | custom-call | flops 4294967296 | bytes 16777216 | tf_op jit(solution)/shard_map/outer/pallas_call | solution.py:317
  252.8 0.6 collective-permute-done.32
  253.4 4.8 %collective-permute-done.50 = bf16[32,4096]{1,0:T(8,128)(2,1)S(1)} collective-permute-done((bf16[32,4096]{1,0:T(8,128)(2,1)S(1)}, bf16[32,4096]{1,0:T(8,128)(2,1)S(1)}, u32[]{:S(2)}, u32[]{:S(2)}) %collective-permute-start.50) | collective-permute-done | bytes 262176 | tf_op jit(solution)/shard_map/ppermute | solution.py:23
  258.2 0.9 add_convert_fusion.14
  (107 shorter events, 8.9 us)
Async XLA Ops:
  1.6 3.1 %collective-permute-start.1 = (bf16[2,384,256]{2,1,0:T(8,128)(2,1)S(1)}, bf16[2,384,256]{2,1,0:T(8,128)(2,1)S(1)}, u32[]{:S(2)}, u32[]{:S(2)}) collective-permute-start(bf16[2,384,256]{2,1,0:T(8,128)(2,1)S(1)} %pack.1.refs_2_.refs_4_), channel_id=1, source_target_pairs={{0,4},{4,0},{8,12},{12,8},{16,20},{20,16},{24,28},{28,24},{1,5},{5... | collective-permute-start | bytes 1179656 | tf_op jit(solution)/shard_map/ppermute | solution.py:19
  2.2 8.3 %collective-permute-start = (bf16[2,384,256]{2,1,0:T(8,128)(2,1)S(1)}, bf16[2,384,256]{2,1,0:T(8,128)(2,1)S(1)}, u32[]{:S(2)}, u32[]{:S(2)}) collective-permute-start(bf16[2,384,256]{2,1,0:T(8,128)(2,1)S(1)} %pack.1.refs_2_.refs_4_), channel_id=1, source_target_pairs={{0,8},{4,20},{8,0},{12,28},{16,24},{20,4},{24,16},{28,12},{1,9},{5... | collective-permute-start | bytes 1179656 | tf_op jit(solution)/shard_map/ppermute | solution.py:35
  4.8 11.7 %collective-permute-start.2 = (bf16[2,384,256]{2,1,0:T(8,128)(2,1)S(1)}, bf16[2,384,256]{2,1,0:T(8,128)(2,1)S(1)}, u32[]{:S(2)}, u32[]{:S(2)}) collective-permute-start(bf16[2,384,256]{2,1,0:T(8,128)(2,1)S(1)} %collective-permute-done.1.refs_3_.refs_5_), channel_id=1, source_target_pairs={{0,8},{4,20},{8,0},{12,28},{16,24},{20,4},{24,16},{28,12},{1,9},{5... | collective-permute-start | bytes 1179656 | tf_op jit(solution)/shard_map/ppermute | solution.py:35
  10.5 8.2 %collective-permute-start.5 = (bf16[2,384,256]{2,1,0:T(8,128)(2,1)S(1)}, bf16[2,384,256]{2,1,0:T(8,128)(2,1)S(1)}, u32[]{:S(2)}, u32[]{:S(2)}) collective-permute-start(bf16[2,384,256]{2,1,0:T(8,128)(2,1)S(1)} %collective-permute-done.refs_2_.refs_8_), channel_id=1, source_target_pairs={{0,16},{4,12},{8,24},{12,4},{16,0},{20,28},{24,8},{28,20},{1,17},{... | collective-permute-start | bytes 1179656 | tf_op jit(solution)/shard_map/ppermute | solution.py:35
  12.6 17.4 %collective-permute-start.3 = (bf16[2,384,256]{2,1,0:T(8,128)(2,1)S(1)}, bf16[2,384,256]{2,1,0:T(8,128)(2,1)S(1)}, u32[]{:S(2)}, u32[]{:S(2)}) collective-permute-start(bf16[2,384,256]{2,1,0:T(8,128)(2,1)S(1)} %collective-permute-done.refs_2_.refs_8_), channel_id=1, source_target_pairs={{0,4},{4,0},{8,12},{12,8},{16,20},{20,16},{24,28},{28,24},{1,5},{5... | collective-permute-start | bytes 1179656 | tf_op jit(solution)/shard_map/ppermute | solution.py:19
  16.5 13.7 %collective-permute-start.4 = (bf16[2,384,256]{2,1,0:T(8,128)(2,1)S(1)}, bf16[2,384,256]{2,1,0:T(8,128)(2,1)S(1)}, u32[]{:S(2)}, u32[]{:S(2)}) collective-permute-start(bf16[2,384,256]{2,1,0:T(8,128)(2,1)S(1)} %collective-permute-done.2.refs_3_.refs_9_), channel_id=1, source_target_pairs={{0,4},{4,0},{8,12},{12,8},{16,20},{20,16},{24,28},{28,24},{1,5},{5... | collective-permute-start | bytes 1179656 | tf_op jit(solution)/shard_map/ppermute | solution.py:19
  18.7 11.4 %collective-permute-start.6 = (bf16[2,384,256]{2,1,0:T(8,128)(2,1)S(1)}, bf16[2,384,256]{2,1,0:T(8,128)(2,1)S(1)}, u32[]{:S(2)}, u32[]{:S(2)}) collective-permute-start(bf16[2,384,256]{2,1,0:T(8,128)(2,1)S(1)} %collective-permute-done.5.refs_6_.refs_12_), channel_id=1, source_target_pairs={{0,4},{4,0},{8,12},{12,8},{16,20},{20,16},{24,28},{28,24},{1,5},{5... | collective-permute-start | bytes 1179656 | tf_op jit(solution)/shard_map/ppermute | solution.py:19
  18.8 40.1 %collective-permute-start.51 = (bf16[32,4096]{1,0:T(8,128)(2,1)}, bf16[32,4096]{1,0:T(8,128)(2,1)}, u32[]{:S(2)}, u32[]{:S(2)}) collective-permute-start(bf16[32,4096]{1,0:T(8,128)(2,1)} %param.23), channel_id=1, source_target_pairs={{0,1},{1,0},{2,3},{3,2},{4,5},{5,4},{6,7},{7,6},{8,9},{9,8},{10,11... | collective-permute-start | bytes 786440 | tf_op jit(solution)/shard_map/ppermute | solution.py:23
  20.9 68.4 %collective-permute-start.53 = (bf16[32,4096]{1,0:T(8,128)(2,1)}, bf16[32,4096]{1,0:T(8,128)(2,1)S(1)}, u32[]{:S(2)}, u32[]{:S(2)}) collective-permute-start(bf16[32,4096]{1,0:T(8,128)(2,1)} %param.23), channel_id=1, source_target_pairs={{0,3},{1,2},{2,1},{3,0},{4,7},{5,6},{6,5},{7,4},{8,11},{9,10},{10,... | collective-permute-start | bytes 786440 | tf_op jit(solution)/shard_map/ppermute | solution.py:23
  25.8 0.8 copy-start
  26.8 16.5 %copy-start.1 = (bf16[32,4096]{1,0:T(8,128)(2,1)S(1)}, bf16[32,4096]{1,0:T(8,128)(2,1)}, u32[]{:S(2)}) copy-start(bf16[32,4096]{1,0:T(8,128)(2,1)} %param.23) | copy-start | bytes 786436
  29.9 45.7 %collective-permute-start.52 = (bf16[32,4096]{1,0:T(8,128)(2,1)}, bf16[32,4096]{1,0:T(8,128)(2,1)S(1)}, u32[]{:S(2)}, u32[]{:S(2)}) collective-permute-start(bf16[32,4096]{1,0:T(8,128)(2,1)} %param.23), channel_id=1, source_target_pairs={{0,2},{1,3},{2,0},{3,1},{4,6},{5,7},{6,4},{7,5},{8,10},{9,11},{10,... | collective-permute-start | bytes 786440 | tf_op jit(solution)/shard_map/ppermute | solution.py:23
  30.1 43.0 %copy-start.2 = (f32[4096]{0:T(1024)S(1)}, f32[4096]{0:T(1024)}, u32[]{:S(2)}) copy-start(f32[4096]{0:T(1024)} %param.17) | copy-start | bytes 49156
  41.2 18.7 %collective-permute-start.7 = (bf16[32,4096]{1,0:T(8,128)(2,1)S(1)}, bf16[32,4096]{1,0:T(8,128)(2,1)S(1)}, u32[]{:S(2)}, u32[]{:S(2)}) collective-permute-start(bf16[32,4096]{1,0:T(8,128)(2,1)S(1)} %get-tuple-element.36), channel_id=1, source_target_pairs={{0,1},{1,0},{2,3},{3,2},{4,5},{5,4},{6,7},{7,6},{8,9},{9,8},{10,11... | collective-permute-start | bytes 786440 | tf_op jit(solution)/shard_map/ppermute | solution.py:23
  43.0 15.1 %collective-permute-start.8 = (bf16[32,4096]{1,0:T(8,128)(2,1)S(1)}, bf16[32,4096]{1,0:T(8,128)(2,1)S(1)}, u32[]{:S(2)}, u32[]{:S(2)}) collective-permute-start(bf16[32,4096]{1,0:T(8,128)(2,1)S(1)} %get-tuple-element.38), channel_id=1, source_target_pairs={{0,1},{1,0},{2,3},{3,2},{4,5},{5,4},{6,7},{7,6},{8,9},{9,8},{10,11... | collective-permute-start | bytes 786440 | tf_op jit(solution)/shard_map/ppermute | solution.py:23
  58.2 14.8 %collective-permute-start.9 = (bf16[32,4096]{1,0:T(8,128)(2,1)S(1)}, bf16[32,4096]{1,0:T(8,128)(2,1)S(1)}, u32[]{:S(2)}, u32[]{:S(2)}) collective-permute-start(bf16[32,4096]{1,0:T(8,128)(2,1)S(1)} %add_convert_fusion.17), channel_id=1, source_target_pairs={{0,2},{1,3},{2,0},{3,1},{4,6},{5,7},{6,4},{7,5},{8,10},{9,11},{10,... | collective-permute-start | bytes 786440 | tf_op jit(solution)/shard_map/ppermute | solution.py:23
  73.3 15.9 %collective-permute-start.33 = (bf16[32,4224]{1,0:T(8,128)(2,1)S(1)}, bf16[32,4224]{1,0:T(8,128)(2,1)S(1)}, u32[]{:S(2)}, u32[]{:S(2)}) collective-permute-start(bf16[32,4224]{1,0:T(8,128)(2,1)S(1)} %fusion.1.refs_0_), channel_id=1, source_target_pairs={{0,2},{1,3},{2,0},{3,1},{4,6},{5,7},{6,4},{7,5},{8,10},{9,11},{10,... | collective-permute-start | bytes 811016 | tf_op jit(solution)/shard_map/ppermute | solution.py:23
  73.4 14.4 %collective-permute-start.10 = (bf16[32,4224]{1,0:T(8,128)(2,1)S(1)}, bf16[32,4224]{1,0:T(8,128)(2,1)S(1)}, u32[]{:S(2)}, u32[]{:S(2)}) collective-permute-start(bf16[32,4224]{1,0:T(8,128)(2,1)S(1)} %fusion.1.refs_0_), channel_id=1, source_target_pairs={{0,1},{1,0},{2,3},{3,2},{4,5},{5,4},{6,7},{7,6},{8,9},{9,8},{10,11... | collective-permute-start | bytes 811016 | tf_op jit(solution)/shard_map/ppermute | solution.py:23
  75.6 13.9 %collective-permute-start.13 = (bf16[32,4224]{1,0:T(8,128)(2,1)S(1)}, bf16[32,4224]{1,0:T(8,128)(2,1)S(1)}, u32[]{:S(2)}, u32[]{:S(2)}) collective-permute-start(bf16[32,4224]{1,0:T(8,128)(2,1)S(1)} %fusion.1.refs_0_), channel_id=1, source_target_pairs={{0,8},{4,20},{8,0},{12,28},{16,24},{20,4},{24,16},{28,12},{1,9},{5... | collective-permute-start | bytes 811016 | tf_op jit(solution)/shard_map/ppermute | solution.py:35
  77.2 12.7 %collective-permute-start.11 = (bf16[32,4224]{1,0:T(8,128)(2,1)S(1)}, bf16[32,4224]{1,0:T(8,128)(2,1)S(1)}, u32[]{:S(2)}, u32[]{:S(2)}) collective-permute-start(bf16[32,4224]{1,0:T(8,128)(2,1)S(1)} %fusion.1.refs_0_), channel_id=1, source_target_pairs={{0,4},{4,0},{8,12},{12,8},{16,20},{20,16},{24,28},{28,24},{1,5},{5... | collective-permute-start | bytes 811016 | tf_op jit(solution)/shard_map/ppermute | solution.py:19
  87.8 10.9 %collective-permute-start.14 = (bf16[32,4224]{1,0:T(8,128)(2,1)S(1)}, bf16[32,4224]{1,0:T(8,128)(2,1)S(1)}, u32[]{:S(2)}, u32[]{:S(2)}) collective-permute-start(bf16[32,4224]{1,0:T(8,128)(2,1)S(1)} %collective-permute-done.10.refs_1_), channel_id=1, source_target_pairs={{0,8},{4,20},{8,0},{12,28},{16,24},{20,4},{24,16},{28,12},{1,9},{5... | collective-permute-start | bytes 811016 | tf_op jit(solution)/shard_map/ppermute | solution.py:35
  89.3 11.0 %collective-permute-start.12 = (bf16[32,4224]{1,0:T(8,128)(2,1)S(1)}, bf16[32,4224]{1,0:T(8,128)(2,1)S(1)}, u32[]{:S(2)}, u32[]{:S(2)}) collective-permute-start(bf16[32,4224]{1,0:T(8,128)(2,1)S(1)} %collective-permute-done.10.refs_1_), channel_id=1, source_target_pairs={{0,4},{4,0},{8,12},{12,8},{16,20},{20,16},{24,28},{28,24},{1,5},{5... | collective-permute-start | bytes 811016 | tf_op jit(solution)/shard_map/ppermute | solution.py:19
  89.3 8.9 %collective-permute-start.34 = (bf16[32,4224]{1,0:T(8,128)(2,1)S(1)}, bf16[32,4224]{1,0:T(8,128)(2,1)S(1)}, u32[]{:S(2)}, u32[]{:S(2)}) collective-permute-start(bf16[32,4224]{1,0:T(8,128)(2,1)S(1)} %collective-permute-done.33), channel_id=1, source_target_pairs={{0,1},{1,0},{2,3},{3,2},{4,5},{5,4},{6,7},{7,6},{8,9},{9,8},{10,11... | collective-permute-start | bytes 811016 | tf_op jit(solution)/shard_map/ppermute | solution.py:23
  89.5 12.2 %collective-permute-start.19 = (bf16[32,4224]{1,0:T(8,128)(2,1)S(1)}, bf16[32,4224]{1,0:T(8,128)(2,1)S(1)}, u32[]{:S(2)}, u32[]{:S(2)}) collective-permute-start(bf16[32,4224]{1,0:T(8,128)(2,1)S(1)} %collective-permute-done.13.refs_4_), channel_id=1, source_target_pairs={{0,4},{4,0},{8,12},{12,8},{16,20},{20,16},{24,28},{28,24},{1,5},{5... | collective-permute-start | bytes 811016 | tf_op jit(solution)/shard_map/ppermute | solution.py:19
  89.9 12.0 %collective-permute-start.17 = (bf16[32,4224]{1,0:T(8,128)(2,1)S(1)}, bf16[32,4224]{1,0:T(8,128)(2,1)S(1)}, u32[]{:S(2)}, u32[]{:S(2)}) collective-permute-start(bf16[32,4224]{1,0:T(8,128)(2,1)S(1)} %collective-permute-done.13.refs_4_), channel_id=1, source_target_pairs={{0,16},{4,12},{8,24},{12,4},{16,0},{20,28},{24,8},{28,20},{1,17},{... | collective-permute-start | bytes 811016 | tf_op jit(solution)/shard_map/ppermute | solution.py:35
  98.2 9.2 %collective-permute-start.15 = (bf16[32,4224]{1,0:T(8,128)(2,1)S(1)}, bf16[32,4224]{1,0:T(8,128)(2,1)S(1)}, u32[]{:S(2)}, u32[]{:S(2)}) collective-permute-start(bf16[32,4224]{1,0:T(8,128)(2,1)S(1)} %collective-permute-done.11.refs_2_), channel_id=1, source_target_pairs={{0,8},{4,20},{8,0},{12,28},{16,24},{20,4},{24,16},{28,12},{1,9},{5... | collective-permute-start | bytes 811016 | tf_op jit(solution)/shard_map/ppermute | solution.py:35
  98.7 9.4 %collective-permute-start.18 = (bf16[32,4224]{1,0:T(8,128)(2,1)S(1)}, bf16[32,4224]{1,0:T(8,128)(2,1)S(1)}, u32[]{:S(2)}, u32[]{:S(2)}) collective-permute-start(bf16[32,4224]{1,0:T(8,128)(2,1)S(1)} %collective-permute-done.14.refs_5_), channel_id=1, source_target_pairs={{0,16},{4,12},{8,24},{12,4},{16,0},{20,28},{24,8},{28,20},{1,17},{... | collective-permute-start | bytes 811016 | tf_op jit(solution)/shard_map/ppermute | solution.py:35
  100.2 10.0 %collective-permute-start.16 = (bf16[32,4224]{1,0:T(8,128)(2,1)S(1)}, bf16[32,4224]{1,0:T(8,128)(2,1)S(1)}, u32[]{:S(2)}, u32[]{:S(2)}) collective-permute-start(bf16[32,4224]{1,0:T(8,128)(2,1)S(1)} %collective-permute-done.12.refs_3_), channel_id=1, source_target_pairs={{0,8},{4,20},{8,0},{12,28},{16,24},{20,4},{24,16},{28,12},{1,9},{5... | collective-permute-start | bytes 811016 | tf_op jit(solution)/shard_map/ppermute | solution.py:35
  101.8 9.4 %collective-permute-start.20 = (bf16[32,4224]{1,0:T(8,128)(2,1)S(1)}, bf16[32,4224]{1,0:T(8,128)(2,1)S(1)}, u32[]{:S(2)}, u32[]{:S(2)}) collective-permute-start(bf16[32,4224]{1,0:T(8,128)(2,1)S(1)} %collective-permute-done.14.refs_5_), channel_id=1, source_target_pairs={{0,4},{4,0},{8,12},{12,8},{16,20},{20,16},{24,28},{28,24},{1,5},{5... | collective-permute-start | bytes 811016 | tf_op jit(solution)/shard_map/ppermute | solution.py:19
  101.9 8.5 %collective-permute-start.23 = (bf16[32,4224]{1,0:T(8,128)(2,1)S(1)}, bf16[32,4224]{1,0:T(8,128)(2,1)S(1)}, u32[]{:S(2)}, u32[]{:S(2)}) collective-permute-start(bf16[32,4224]{1,0:T(8,128)(2,1)S(1)} %collective-permute-done.17.refs_8_), channel_id=1, source_target_pairs={{0,4},{4,0},{8,12},{12,8},{16,20},{20,16},{24,28},{28,24},{1,5},{5... | collective-permute-start | bytes 811016 | tf_op jit(solution)/shard_map/ppermute | solution.py:19
  107.4 3.5 %collective-permute-start.21 = (bf16[32,4224]{1,0:T(8,128)(2,1)S(1)}, bf16[32,4224]{1,0:T(8,128)(2,1)S(1)}, u32[]{:S(2)}, u32[]{:S(2)}) collective-permute-start(bf16[32,4224]{1,0:T(8,128)(2,1)S(1)} %collective-permute-done.15.refs_6_), channel_id=1, source_target_pairs={{0,4},{4,0},{8,12},{12,8},{16,20},{20,16},{24,28},{28,24},{1,5},{5... | collective-permute-start | bytes 811016 | tf_op jit(solution)/shard_map/ppermute | solution.py:19
  108.1 4.4 %collective-permute-start.24 = (bf16[32,4224]{1,0:T(8,128)(2,1)S(1)}, bf16[32,4224]{1,0:T(8,128)(2,1)S(1)}, u32[]{:S(2)}, u32[]{:S(2)}) collective-permute-start(bf16[32,4224]{1,0:T(8,128)(2,1)S(1)} %collective-permute-done.18.refs_9_), channel_id=1, source_target_pairs={{0,4},{4,0},{8,12},{12,8},{16,20},{20,16},{24,28},{28,24},{1,5},{5... | collective-permute-start | bytes 811016 | tf_op jit(solution)/shard_map/ppermute | solution.py:19
  110.3 2.2 collective-permute-start.22
  110.3 24.7 %collective-permute-start.55 = (bf16[128,4096]{1,0:T(8,128)(2,1)S(1)}, bf16[128,4096]{1,0:T(8,128)(2,1)S(1)}, u32[]{:S(2)}, u32[]{:S(2)}) collective-permute-start(bf16[128,4096]{1,0:T(8,128)(2,1)S(1)} %constant_dynamic-update-slice_fusion.2.refs_0_), channel_id=1, source_target_pairs={{0,8},{4,20},{8,0},{12,28},{16,24},{20,4},{24,16},{28,12},{1,9},{5... | collective-permute-start | bytes 3145736 | tf_op jit(solution)/shard_map/ppermute | solution.py:35
  110.9 24.8 %collective-permute-start.54 = (bf16[128,4096]{1,0:T(8,128)(2,1)S(1)}, bf16[128,4096]{1,0:T(8,128)(2,1)S(1)}, u32[]{:S(2)}, u32[]{:S(2)}) collective-permute-start(bf16[128,4096]{1,0:T(8,128)(2,1)S(1)} %constant_dynamic-update-slice_fusion.2.refs_0_), channel_id=1, source_target_pairs={{0,4},{4,0},{8,12},{12,8},{16,20},{20,16},{24,28},{28,24},{1,5},{5... | collective-permute-start | bytes 3145736 | tf_op jit(solution)/shard_map/ppermute | solution.py:19
  111.1 26.1 %collective-permute-start.36 = (bf16[64,4224]{1,0:T(8,128)(2,1)S(1)}, bf16[64,4224]{1,0:T(8,128)(2,1)S(1)}, u32[]{:S(2)}, u32[]{:S(2)}) collective-permute-start(bf16[64,4224]{1,0:T(8,128)(2,1)S(1)} %constant_dynamic-update-slice_fusion.refs_0_), channel_id=1, source_target_pairs={{0,8},{4,20},{8,0},{12,28},{16,24},{20,4},{24,16},{28,12},{1,9},{5... | collective-permute-start | bytes 1622024 | tf_op jit(solution)/shard_map/ppermute | solution.py:35
  112.5 24.7 %collective-permute-start.35 = (bf16[64,4224]{1,0:T(8,128)(2,1)S(1)}, bf16[64,4224]{1,0:T(8,128)(2,1)S(1)}, u32[]{:S(2)}, u32[]{:S(2)}) collective-permute-start(bf16[64,4224]{1,0:T(8,128)(2,1)S(1)} %constant_dynamic-update-slice_fusion.refs_0_), channel_id=1, source_target_pairs={{0,4},{4,0},{8,12},{12,8},{16,20},{20,16},{24,28},{28,24},{1,5},{5... | collective-permute-start | bytes 1622024 | tf_op jit(solution)/shard_map/ppermute | solution.py:19
  134.4 3.4 %collective-permute-start.25 = (bf16[64,4096]{1,0:T(8,128)(2,1)S(1)}, bf16[64,4096]{1,0:T(8,128)(2,1)S(1)}, u32[]{:S(2)}, u32[]{:S(2)}) collective-permute-start(bf16[64,4096]{1,0:T(8,128)(2,1)S(1)} %get-tuple-element.43), channel_id=1, source_target_pairs={{0,4},{4,0},{8,12},{12,8},{16,20},{20,16},{24,28},{28,24},{1,5},{5... | collective-permute-start | bytes 1572872 | tf_op jit(solution)/shard_map/ppermute | solution.py:19
  135.0 37.8 %collective-permute-start.57 = (bf16[128,4096]{1,0:T(8,128)(2,1)S(1)}, bf16[128,4096]{1,0:T(8,128)(2,1)S(1)}, u32[]{:S(2)}, u32[]{:S(2)}) collective-permute-start(bf16[128,4096]{1,0:T(8,128)(2,1)S(1)} %collective-permute-done.55.refs_2_), channel_id=1, source_target_pairs={{0,16},{4,12},{8,24},{12,4},{16,0},{20,28},{24,8},{28,20},{1,17},{... | collective-permute-start | bytes 3145736 | tf_op jit(solution)/shard_map/ppermute | solution.py:35
  135.7 37.2 %collective-permute-start.56 = (bf16[128,4096]{1,0:T(8,128)(2,1)S(1)}, bf16[128,4096]{1,0:T(8,128)(2,1)S(1)}, u32[]{:S(2)}, u32[]{:S(2)}) collective-permute-start(bf16[128,4096]{1,0:T(8,128)(2,1)S(1)} %collective-permute-done.54.refs_1_), channel_id=1, source_target_pairs={{0,8},{4,20},{8,0},{12,28},{16,24},{20,4},{24,16},{28,12},{1,9},{5... | collective-permute-start | bytes 3145736 | tf_op jit(solution)/shard_map/ppermute | solution.py:35
  137.2 2.1 collective-permute-start.29
  137.2 34.9 %collective-permute-start.38 = (bf16[64,4224]{1,0:T(8,128)(2,1)S(1)}, bf16[64,4224]{1,0:T(8,128)(2,1)S(1)}, u32[]{:S(2)}, u32[]{:S(2)}) collective-permute-start(bf16[64,4224]{1,0:T(8,128)(2,1)S(1)} %collective-permute-done.36.refs_2_), channel_id=1, source_target_pairs={{0,16},{4,12},{8,24},{12,4},{16,0},{20,28},{24,8},{28,20},{1,17},{... | collective-permute-start | bytes 1622024 | tf_op jit(solution)/shard_map/ppermute | solution.py:35
  137.8 34.4 %collective-permute-start.37 = (bf16[64,4224]{1,0:T(8,128)(2,1)S(1)}, bf16[64,4224]{1,0:T(8,128)(2,1)S(1)}, u32[]{:S(2)}, u32[]{:S(2)}) collective-permute-start(bf16[64,4224]{1,0:T(8,128)(2,1)S(1)} %collective-permute-done.35.refs_1_), channel_id=1, source_target_pairs={{0,8},{4,20},{8,0},{12,28},{16,24},{20,4},{24,16},{28,12},{1,9},{5... | collective-permute-start | bytes 1622024 | tf_op jit(solution)/shard_map/ppermute | solution.py:35
  139.3 34.1 %collective-permute-start.39 = (bf16[64,4224]{1,0:T(8,128)(2,1)S(1)}, bf16[64,4224]{1,0:T(8,128)(2,1)S(1)}, u32[]{:S(2)}, u32[]{:S(2)}) collective-permute-start(bf16[64,4224]{1,0:T(8,128)(2,1)S(1)} %collective-permute-done.36.refs_2_), channel_id=1, source_target_pairs={{0,4},{4,0},{8,12},{12,8},{16,20},{20,16},{24,28},{28,24},{1,5},{5... | collective-permute-start | bytes 1622024 | tf_op jit(solution)/shard_map/ppermute | solution.py:19
  172.1 1.9 collective-permute-start.41
  172.1 2.7 %collective-permute-start.40 = (bf16[64,4224]{1,0:T(8,128)(2,1)S(1)}, bf16[64,4224]{1,0:T(8,128)(2,1)S(1)}, u32[]{:S(2)}, u32[]{:S(2)}) collective-permute-start(bf16[64,4224]{1,0:T(8,128)(2,1)S(1)} %collective-permute-done.37.refs_3_), channel_id=1, source_target_pairs={{0,4},{4,0},{8,12},{12,8},{16,20},{20,16},{24,28},{28,24},{1,5},{5... | collective-permute-start | bytes 1622024 | tf_op jit(solution)/shard_map/ppermute | solution.py:19
  172.8 54.7 %collective-permute-start.58 = (bf16[128,4096]{1,0:T(8,128)(2,1)S(1)}, bf16[128,4096]{1,0:T(8,128)(2,1)S(1)}, u32[]{:S(2)}, u32[]{:S(2)}) collective-permute-start(bf16[128,4096]{1,0:T(8,128)(2,1)S(1)} %collective-permute-done.55.refs_2_), channel_id=1, source_target_pairs={{0,4},{4,0},{8,12},{12,8},{16,20},{20,16},{24,28},{28,24},{1,5},{5... | collective-permute-start | bytes 3145736 | tf_op jit(solution)/shard_map/ppermute | solution.py:19
  172.9 22.2 %collective-permute-start.28 = (bf16[64,4096]{1,0:T(8,128)(2,1)S(1)}, bf16[64,4096]{1,0:T(8,128)(2,1)S(1)}, u32[]{:S(2)}, u32[]{:S(2)}) collective-permute-start(bf16[64,4096]{1,0:T(8,128)(2,1)S(1)} %get-tuple-element.45), channel_id=1, source_target_pairs={{0,4},{4,0},{8,12},{12,8},{16,20},{20,16},{24,28},{28,24},{1,5},{5... | collective-permute-start | bytes 1572872 | tf_op jit(solution)/shard_map/ppermute | solution.py:19
  173.4 54.5 %collective-permute-start.60 = (bf16[128,4096]{1,0:T(8,128)(2,1)S(1)}, bf16[128,4096]{1,0:T(8,128)(2,1)S(1)}, u32[]{:S(2)}, u32[]{:S(2)}) collective-permute-start(bf16[128,4096]{1,0:T(8,128)(2,1)S(1)} %collective-permute-done.57.refs_4_), channel_id=1, source_target_pairs={{0,4},{4,0},{8,12},{12,8},{16,20},{20,16},{24,28},{28,24},{1,5},{5... | collective-permute-start | bytes 3145736 | tf_op jit(solution)/shard_map/ppermute | solution.py:19
  174.1 54.8 %collective-permute-start.59 = (bf16[128,4096]{1,0:T(8,128)(2,1)S(1)}, bf16[128,4096]{1,0:T(8,128)(2,1)S(1)}, u32[]{:S(2)}, u32[]{:S(2)}) collective-permute-start(bf16[128,4096]{1,0:T(8,128)(2,1)S(1)} %collective-permute-done.56.refs_3_), channel_id=1, source_target_pairs={{0,4},{4,0},{8,12},{12,8},{16,20},{20,16},{24,28},{28,24},{1,5},{5... | collective-permute-start | bytes 3145736 | tf_op jit(solution)/shard_map/ppermute | solution.py:19
  174.8 20.4 %collective-permute-start.30 = (bf16[64,4096]{1,0:T(8,128)(2,1)S(1)}, bf16[64,4096]{1,0:T(8,128)(2,1)S(1)}, u32[]{:S(2)}, u32[]{:S(2)}) collective-permute-start(bf16[64,4096]{1,0:T(8,128)(2,1)S(1)} %add_convert_fusion.9), channel_id=1, source_target_pairs={{0,16},{4,12},{8,24},{12,4},{16,0},{20,28},{24,8},{28,20},{1,17},{... | collective-permute-start | bytes 1572872 | tf_op jit(solution)/shard_map/ppermute | solution.py:35
  195.1 5.7 %collective-permute-start.42 = (bf16[64,4096]{1,0:T(8,128)(2,1)S(1)}, bf16[64,4096]{1,0:T(8,128)(2,1)S(1)}, u32[]{:S(2)}, u32[]{:S(2)}) collective-permute-start(bf16[64,4096]{1,0:T(8,128)(2,1)S(1)} %get-tuple-element.52), channel_id=1, source_target_pairs={{0,4},{4,0},{8,12},{12,8},{16,20},{20,16},{24,28},{28,24},{1,5},{5... | collective-permute-start | bytes 1572872 | tf_op jit(solution)/shard_map/ppermute | solution.py:19
  195.4 17.9 %collective-permute-start.45 = (bf16[64,4096]{1,0:T(8,128)(2,1)S(1)}, bf16[64,4096]{1,0:T(8,128)(2,1)S(1)}, u32[]{:S(2)}, u32[]{:S(2)}) collective-permute-start(bf16[64,4096]{1,0:T(8,128)(2,1)S(1)} %get-tuple-element.54), channel_id=1, source_target_pairs={{0,4},{4,0},{8,12},{12,8},{16,20},{20,16},{24,28},{28,24},{1,5},{5... | collective-permute-start | bytes 1572872 | tf_op jit(solution)/shard_map/ppermute | solution.py:19
  200.8 2.0 collective-permute-start.46
  202.8 9.2 %collective-permute-start.43 = (bf16[64,4096]{1,0:T(8,128)(2,1)S(1)}, bf16[64,4096]{1,0:T(8,128)(2,1)S(1)}, u32[]{:S(2)}, u32[]{:S(2)}) collective-permute-start(bf16[64,4096]{1,0:T(8,128)(2,1)S(1)} %add_convert_fusion.6), channel_id=1, source_target_pairs={{0,8},{4,20},{8,0},{12,28},{16,24},{20,4},{24,16},{28,12},{1,9},{5... | collective-permute-start | bytes 1572872 | tf_op jit(solution)/shard_map/ppermute | solution.py:35
  212.0 14.2 %collective-permute-start.47 = (bf16[64,4096]{1,0:T(8,128)(2,1)S(1)}, bf16[64,4096]{1,0:T(8,128)(2,1)S(1)}, u32[]{:S(2)}, u32[]{:S(2)}) collective-permute-start(bf16[64,4096]{1,0:T(8,128)(2,1)S(1)} %add_convert_fusion.2), channel_id=1, source_target_pairs={{0,16},{4,12},{8,24},{12,4},{16,0},{20,28},{24,8},{28,20},{1,17},{... | collective-permute-start | bytes 1572872 | tf_op jit(solution)/shard_map/ppermute | solution.py:35
  213.3 13.1 %collective-permute-start.26 = (bf16[64,4096]{1,0:T(8,128)(2,1)S(1)}, bf16[64,4096]{1,0:T(8,128)(2,1)S(1)}, u32[]{:S(2)}, u32[]{:S(2)}) collective-permute-start(bf16[64,4096]{1,0:T(8,128)(2,1)S(1)} %add_convert_fusion.13), channel_id=1, source_target_pairs={{0,8},{4,20},{8,0},{12,28},{16,24},{20,4},{24,16},{28,12},{1,9},{5... | collective-permute-start | bytes 1572872 | tf_op jit(solution)/shard_map/ppermute | solution.py:35
  226.2 9.5 %collective-permute-start.44 = (bf16[64,4096]{1,0:T(8,128)(2,1)S(1)}, bf16[64,4096]{1,0:T(8,128)(2,1)S(1)}, u32[]{:S(2)}, u32[]{:S(2)}) collective-permute-start(bf16[64,4096]{1,0:T(8,128)(2,1)S(1)} %add_convert_fusion.5), channel_id=1, source_target_pairs={{0,4},{4,0},{8,12},{12,8},{16,20},{20,16},{24,28},{28,24},{1,5},{5... | collective-permute-start | bytes 1572872 | tf_op jit(solution)/shard_map/ppermute | solution.py:19
  226.4 9.2 %collective-permute-start.48 = (bf16[64,4096]{1,0:T(8,128)(2,1)S(1)}, bf16[64,4096]{1,0:T(8,128)(2,1)S(1)}, u32[]{:S(2)}, u32[]{:S(2)}) collective-permute-start(bf16[64,4096]{1,0:T(8,128)(2,1)S(1)} %add_convert_fusion.1), channel_id=1, source_target_pairs={{0,8},{4,20},{8,0},{12,28},{16,24},{20,4},{24,16},{28,12},{1,9},{5... | collective-permute-start | bytes 1572872 | tf_op jit(solution)/shard_map/ppermute | solution.py:35
  227.4 8.9 %collective-permute-start.27 = (bf16[64,4096]{1,0:T(8,128)(2,1)S(1)}, bf16[64,4096]{1,0:T(8,128)(2,1)S(1)}, u32[]{:S(2)}, u32[]{:S(2)}) collective-permute-start(bf16[64,4096]{1,0:T(8,128)(2,1)S(1)} %add_convert_fusion.12), channel_id=1, source_target_pairs={{0,4},{4,0},{8,12},{12,8},{16,20},{20,16},{24,28},{28,24},{1,5},{5... | collective-permute-start | bytes 1572872 | tf_op jit(solution)/shard_map/ppermute | solution.py:19
  227.8 13.4 %collective-permute-start.31 = (bf16[64,4096]{1,0:T(8,128)(2,1)S(1)}, bf16[64,4096]{1,0:T(8,128)(2,1)S(1)}, u32[]{:S(2)}, u32[]{:S(2)}) collective-permute-start(bf16[64,4096]{1,0:T(8,128)(2,1)S(1)} %add_convert_fusion.8), channel_id=1, source_target_pairs={{0,8},{4,20},{8,0},{12,28},{16,24},{20,4},{24,16},{28,12},{1,9},{5... | collective-permute-start | bytes 1572872 | tf_op jit(solution)/shard_map/ppermute | solution.py:35
  235.9 8.6 %collective-permute-start.49 = (bf16[32,4096]{1,0:T(8,128)(2,1)S(1)}, bf16[32,4096]{1,0:T(8,128)(2,1)S(1)}, u32[]{:S(2)}, u32[]{:S(2)}) collective-permute-start(bf16[32,4096]{1,0:T(8,128)(2,1)S(1)} %slice.19), channel_id=1, source_target_pairs={{0,1},{1,0},{2,3},{3,2},{4,5},{5,4},{6,7},{7,6},{8,9},{9,8},{10,11... | collective-permute-start | bytes 786440 | tf_op jit(solution)/shard_map/ppermute | solution.py:23
  241.5 11.9 %collective-permute-start.32 = (bf16[32,4096]{1,0:T(8,128)(2,1)S(1)}, bf16[32,4096]{1,0:T(8,128)(2,1)S(1)}, u32[]{:S(2)}, u32[]{:S(2)}) collective-permute-start(bf16[32,4096]{1,0:T(8,128)(2,1)S(1)} %slice.17), channel_id=1, source_target_pairs={{0,1},{1,0},{2,3},{3,2},{4,5},{5,4},{6,7},{7,6},{8,9},{9,8},{10,11... | collective-permute-start | bytes 786440 | tf_op jit(solution)/shard_map/ppermute | solution.py:23
  244.6 13.6 %collective-permute-start.50 = (bf16[32,4096]{1,0:T(8,128)(2,1)S(1)}, bf16[32,4096]{1,0:T(8,128)(2,1)S(1)}, u32[]{:S(2)}, u32[]{:S(2)}) collective-permute-start(bf16[32,4096]{1,0:T(8,128)(2,1)S(1)} %add_convert_fusion.15), channel_id=1, source_target_pairs={{0,2},{1,3},{2,0},{3,1},{4,6},{5,7},{6,4},{7,5},{8,10},{9,11},{10,... | collective-permute-start | bytes 786440 | tf_op jit(solution)/shard_map/ppermute | solution.py:23
